TPU v7x, 512 devices: a whole 4x8x8 slice. The times are simulated.
512 devices in a mesh: row: 32 (over x, y), rhs: 16 (over z, core).
Axes of the slice: x: 4, y: 8, z: 8, core: 2. Of those that a mesh axis runs over, the one named last changes fastest.
Arguments:
- factor: float32 [32, 704, 4, 1024], P('row', None, None, 'rhs'), may hold values from -0.09375 to 0.09375
- inverses: float32 [32, 4, 1024, 32], P('row', None, 'rhs'), may hold values from -0.1875 to 0.1875
- right_side: float32 [32, 704, 4096], P('row', None, 'rhs'), may hold values from -6 to 6
Outputs:
- solution: float32 [32, 128, 4096], P('row', None, 'rhs')
- trailing: float32 [32, 576, 4096], P('row', None, 'rhs')
All inputs are finite; a program needn't handle non-finite values.
Results may differ from a plain program's by a relative error of at most 0.0001.
Values sent between devices are 32-bit elements; how exact they have to be, the bound alone decides.
No kernel may reach another device: no remote copies, remote signals or barrier semaphores. Data moves between devices by JAX's collectives and lax.ppermute only.
A program may use at most 64 MiB of HBM per device.

v0:
```python
import jax
import jax.numpy as jnp
from jax import lax
from jax.sharding import PartitionSpec as P


def from_everyone(array, axis):
    length = lax.axis_size(axis)
    return lax.all_to_all(
        jnp.broadcast_to(array[None], (length, *array.shape)), axis, 0, 0, tiled=True
    )


def in_order(blocks, dim):
    blocks = jnp.moveaxis(blocks, 0, dim)
    lengths = blocks.shape
    return blocks.reshape(*lengths[:dim], lengths[dim] * lengths[dim + 1], *lengths[dim + 2 :])


def gather_directly(array, axis, dim):
    blocks = from_everyone(array, axis)
    return in_order(blocks, dim)


def rows_for(lines, length):
    spare = -lines.shape[0] % length
    if not spare:
        return lines
    return jnp.concatenate([lines, jnp.zeros((spare, *lines.shape[1:]), lines.dtype)])


def cut_along(array, dim, length):
    lengths = array.shape
    blocks = array.reshape(*lengths[:dim], length, lengths[dim] // length, *lengths[dim + 1 :])
    return jnp.moveaxis(blocks, dim, 0)


def summed_on_arrival(array, axis, dim):
    blocks = cut_along(array, dim, lax.axis_size(axis))
    arrived = lax.all_to_all(blocks, axis, split_axis=0, concat_axis=0, tiled=True)
    return arrived.sum(axis=0)


def nested_sum(array, axes):
    lines = array.reshape(-1, array.shape[-1])
    padded = rows_for(lines, lax.axis_size(axes))
    whole = gather_directly(summed_on_arrival(padded, axes, 0), axes, 0)
    return lax.slice_in_dim(whole, 0, len(lines)).reshape(array.shape)


def contract(lower_rows, stacked):
    return jnp.einsum("rpc,pcd->rd", lower_rows, stacked, precision=lax.Precision.HIGHEST)


def body(factor, inverses, right_side):
    lower = factor[0]
    current = right_side[0]
    panels = lower.shape[1]
    width = inverses.shape[3]
    block_inv = gather_directly(inverses[0], "rhs", 1)
    solved = []
    rows_all = current.shape[0]
    for k in range(panels):
        low = k * width
        high = (k + 1) * width
        block = current[low:high]
        partial_value = jnp.dot(
            block_inv[k], block, precision=lax.Precision.HIGHEST, preferred_element_type=jnp.float32
        )
        full = nested_sum(partial_value, "row")
        solved.append(full)
        stacked = full[None]
        current = current.at[high:].add(
            -contract(
                lax.all_gather(lower[high:rows_all, k : k + 1], "rhs", axis=2, tiled=True), stacked
            )
        )
    tail_start = panels * width
    trailing = current[tail_start:]
    place = lax.axis_index("row") * width
    mine = jnp.concatenate(
        [lax.dynamic_slice_in_dim(full, place, width, 0) for full in solved], axis=0
    )
    return (mine[None], trailing[None])


def solution(mesh):
    in_specs = (P("row", None, None, "rhs"), P("row", None, "rhs", None), P("row", None, "rhs"))
    out_specs = (P("row", None, "rhs"), P("row", None, "rhs"))
    return jax.shard_map(body, mesh=mesh, in_specs=in_specs, out_specs=out_specs, check_vma=False)
```

profile of v0, /device:TPU:8, one launch (start us, length us, event | category | flops | bytes accessed | tf_op | source)
XLA Modules:
  0.0 358.8 jit_solution(7640284521515474278)
XLA Ops:
  7.2 0.8 copy-done
  8.0 0.1 broadcast_bitcast_fusion
  8.1 1.5 reshape.173
  9.6 10.4 %all-to-all-start = ((f32[16,1,8192]{2,1,0:T(1,128)}), f32[16,1,8192]{2,1,0:T(1,128)S(1)}, u32[]{:S(2)}, u32[]{:S(2)}) async-start(f32[16,1,8192]{2,1,0:T(1,128)} %reshape.173), calls=%async_computation | async-start | bytes 1048576 | tf_op jit(solution)/shard_map/all_to_all | solution.py:9
  20.0 0.0 all-gather.5.cloned.1.call-start
  20.1 1.7 slice.144
  21.8 0.0 all-gather.5.cloned.1.call-update
  21.8 14.1 %all-to-all-done = f32[16,1,8192]{2,1,0:T(1,128)S(1)} async-done(((f32[16,1,8192]{2,1,0:T(1,128)}), f32[16,1,8192]{2,1,0:T(1,128)S(1)}, u32[]{:S(2)}, u32[]{:S(2)}) %all-to-all-start) | async-done | bytes 524320 | tf_op jit(solution)/shard_map/all_to_all | solution.py:9
  35.9 0.5 broadcast.52
  36.5 1.9 reduce.8
  38.4 0.4 reshape.174
  38.8 0.1 bitcast_bitcast_fusion
  38.9 0.1 fusion.53
  39.0 0.2 copy.17
  39.2 1.7 fusion.50
  40.9 39.2 %all_to_all.45 = f32[32,32,256]{2,1,0:T(8,128)S(1)} all-to-all(f32[32,32,256]{2,1,0:T(8,128)S(1)} %fusion.50), channel_id=1, replica_groups=mesh['row'=32,'rhs'=16] {'row'}, dimensions={0} | all-to-all | bytes 2097152 | tf_op jit(solution)/shard_map/all_to_all | solution.py:40
  80.2 0.1 reduce_sum.36
  80.2 1.1 broadcast_in_dim.18
  81.3 5.7 %all-to-all-start.2 = ((f32[32,32,256]{2,1,0:T(8,128)}), f32[32,32,256]{2,1,0:T(8,128)S(1)}, u32[]{:S(2)}, u32[]{:S(2)}) async-start(f32[32,32,256]{2,1,0:T(8,128)} %broadcast_in_dim.18), calls=%async_computation.2 | async-start | bytes 2097152 | tf_op jit(solution)/shard_map/all_to_all | solution.py:9
  87.1 0.0 all-gather.7.cloned.1.call-start
  87.1 1.7 slice.148
  88.8 0.0 all-gather.7.cloned.1.call-update
  88.9 0.2 copy.18
  89.0 0.8 squeeze.15
  89.8 26.1 %all-to-all-done.2 = f32[32,32,256]{2,1,0:T(8,128)S(1)} async-done(((f32[32,32,256]{2,1,0:T(8,128)}), f32[32,32,256]{2,1,0:T(8,128)S(1)}, u32[]{:S(2)}, u32[]{:S(2)}) %all-to-all-start.2) | async-done | bytes 1048608 | tf_op jit(solution)/shard_map/all_to_all | solution.py:9
  115.9 7.5 %fusion.14 = f32[672,256]{1,0:T(8,128)S(1)} fusion(f32[1024,256]{1,0:T(8,128)S(1)} %bitcast.115, f32[672,1,1024]{0,2,1:T(8,128)} %all-gather.5.cloned.1.call-done, f32[1,704,256]{2,1,0:T(8,128)} %param.13), kind=kOutput, calls=%fused_computation.13 | convolution fusion | flops 2114273280 | bytes 5177344 | tf_op jit(solution)/shard_map/rpc,pcd->rd/dot_general | solution.py:52
  123.4 1.0 convolution_bitcast_fusion.2
  124.4 0.3 copy.19
  124.8 33.0 %all_to_all.46 = f32[32,32,256]{2,1,0:T(8,128)S(1)} all-to-all(f32[32,32,256]{2,1,0:T(8,128)S(1)} %bitcast.117), channel_id=1, replica_groups=mesh['row'=32,'rhs'=16] {'row'}, dimensions={0} | all-to-all | bytes 2097152 | tf_op jit(solution)/shard_map/all_to_all | solution.py:40
  157.8 0.1 reduce_sum.37
  157.8 1.1 broadcast_in_dim.19
  158.9 5.2 %all-to-all-start.4 = ((f32[32,32,256]{2,1,0:T(8,128)}), f32[32,32,256]{2,1,0:T(8,128)S(1)}, u32[]{:S(2)}, u32[]{:S(2)}) async-start(f32[32,32,256]{2,1,0:T(8,128)} %broadcast_in_dim.19), calls=%async_computation.4 | async-start | bytes 2097152 | tf_op jit(solution)/shard_map/all_to_all | solution.py:9
  164.1 0.0 all-gather.9.cloned.1.call-start
  164.2 1.7 slice.152
  165.9 0.2 copy.21
  166.1 0.1 squeeze.16
  166.2 0.0 all-gather.7.cloned.1.call-done
  166.2 25.9 %all-to-all-done.4 = f32[32,32,256]{2,1,0:T(8,128)S(1)} async-done(((f32[32,32,256]{2,1,0:T(8,128)}), f32[32,32,256]{2,1,0:T(8,128)S(1)}, u32[]{:S(2)}, u32[]{:S(2)}) %all-to-all-start.4) | async-done | bytes 1048608 | tf_op jit(solution)/shard_map/all_to_all | solution.py:9
  192.2 6.0 %fusion.23 = f32[640,256]{1,0:T(8,128)S(1)} fusion(f32[1024,256]{1,0:T(8,128)S(1)} %bitcast.109, f32[640,1,1024]{0,2,1:T(8,128)} %all-gather.7.cloned.1.call-done, f32[672,256]{1,0:T(8,128)S(1)} %fusion.14), kind=kOutput, calls=%fused_computation.16 | convolution fusion | flops 2013593600 | bytes 4980736 | tf_op jit(solution)/shard_map/rpc,pcd->rd/dot_general | solution.py:52
  198.2 0.8 copy-done.2
  199.0 1.0 convolution_bitcast_fusion.1
  200.0 0.3 copy.22
  200.4 33.1 %all_to_all.47 = f32[32,32,256]{2,1,0:T(8,128)S(1)} all-to-all(f32[32,32,256]{2,1,0:T(8,128)S(1)} %bitcast.118), channel_id=1, replica_groups=mesh['row'=32,'rhs'=16] {'row'}, dimensions={0} | all-to-all | bytes 2097152 | tf_op jit(solution)/shard_map/all_to_all | solution.py:40
  233.4 0.1 reduce_sum.38
  233.5 1.1 broadcast_in_dim.20
  234.6 5.2 %all-to-all-start.6 = ((f32[32,32,256]{2,1,0:T(8,128)}), f32[32,32,256]{2,1,0:T(8,128)S(1)}, u32[]{:S(2)}, u32[]{:S(2)}) async-start(f32[32,32,256]{2,1,0:T(8,128)} %broadcast_in_dim.20), calls=%async_computation.6 | async-start | bytes 2097152 | tf_op jit(solution)/shard_map/all_to_all | solution.py:9
  239.8 0.3 all-gather.11.cloned.1.call-start
  240.1 1.6 slice.156
  241.7 0.2 copy.23
  241.9 0.1 squeeze.17
  242.0 0.0 all-gather.9.cloned.1.call-done
  242.0 25.8 %all-to-all-done.6 = f32[32,32,256]{2,1,0:T(8,128)S(1)} async-done(((f32[32,32,256]{2,1,0:T(8,128)}), f32[32,32,256]{2,1,0:T(8,128)S(1)}, u32[]{:S(2)}, u32[]{:S(2)}) %all-to-all-start.6) | async-done | bytes 1048608 | tf_op jit(solution)/shard_map/all_to_all | solution.py:9
  267.9 6.0 %fusion.32 = f32[608,256]{1,0:T(8,128)S(1)} fusion(f32[1024,256]{1,0:T(8,128)S(1)} %bitcast.111, f32[608,1,1024]{0,2,1:T(8,128)} %all-gather.9.cloned.1.call-done, f32[640,256]{1,0:T(8,128)S(1)} %copy-done.3), kind=kOutput, calls=%fused_computation.19 | convolution fusion | flops 1912913920 | bytes 4784128 | tf_op jit(solution)/shard_map/rpc,pcd->rd/dot_general | solution.py:52
  273.9 0.8 copy-done.4
  274.7 1.0 convolution_bitcast_fusion
  275.7 1.3 copy.24
  277.0 33.3 %all_to_all.48 = f32[32,32,256]{2,1,0:T(8,128)S(1)} all-to-all(f32[32,32,256]{2,1,0:T(8,128)} %bitcast.119), channel_id=1, replica_groups=mesh['row'=32,'rhs'=16] {'row'}, dimensions={0} | all-to-all | bytes 2097152 | tf_op jit(solution)/shard_map/all_to_all | solution.py:40
  310.3 0.1 reduce_sum.39
  310.4 1.1 broadcast_in_dim.42
  311.5 5.2 %all-to-all-start.8 = ((f32[32,32,256]{2,1,0:T(8,128)}), f32[32,32,256]{2,1,0:T(8,128)S(1)}, u32[]{:S(2)}, u32[]{:S(2)}) async-start(f32[32,32,256]{2,1,0:T(8,128)} %broadcast_in_dim.42), calls=%async_computation.8 | async-start | bytes 2097152 | tf_op jit(solution)/shard_map/all_to_all | solution.py:9
  316.7 0.8 constant_dynamic-slice_fusion.3
  317.4 27.2 %all-to-all-done.8 = f32[32,32,256]{2,1,0:T(8,128)S(1)} async-done(((f32[32,32,256]{2,1,0:T(8,128)}), f32[32,32,256]{2,1,0:T(8,128)S(1)}, u32[]{:S(2)}, u32[]{:S(2)}) %all-to-all-start.8) | async-done | bytes 1048608 | tf_op jit(solution)/shard_map/all_to_all | solution.py:9
  344.7 0.7 maximum_bitcast_fusion
  345.3 6.9 %fusion.44 = f32[1,576,256]{2,1,0:T(8,128)} fusion(f32[1024,256]{1,0:T(8,128)S(1)} %bitcast.114, f32[576,1,1024]{0,2,1:T(8,128)} %all-gather.11.cloned.1.call-done, f32[608,256]{1,0:T(8,128)} %copy-done.4), kind=kOutput, calls=%fused_computation.23 | convolution fusion | flops 1812234240 | bytes 4587520 | tf_op jit(solution)/shard_map/rpc,pcd->rd/dot_general | solution.py:52
  (16 shorter events, 0.1 us)
Async XLA Ops:
  7.2 0.8 copy-start
  9.6 26.4 %all-to-all-start = ((f32[16,1,8192]{2,1,0:T(1,128)}), f32[16,1,8192]{2,1,0:T(1,128)S(1)}, u32[]{:S(2)}, u32[]{:S(2)}) async-start(f32[16,1,8192]{2,1,0:T(1,128)} %reshape.173), calls=%async_computation | async-start | bytes 1048576 | tf_op jit(solution)/shard_map/all_to_all | solution.py:9
  20.0 95.9 %all-gather.5.cloned.1.call-start = ((), (), s32[]{:S(2)}) async-start(), calls=%async_computation.9 | async-start | bytes 3342336 | tf_op jit(solution)/shard_map/all_gather | solution.py:75
  81.3 34.5 %all-to-all-start.2 = ((f32[32,32,256]{2,1,0:T(8,128)}), f32[32,32,256]{2,1,0:T(8,128)S(1)}, u32[]{:S(2)}, u32[]{:S(2)}) async-start(f32[32,32,256]{2,1,0:T(8,128)} %broadcast_in_dim.18), calls=%async_computation.2 | async-start | bytes 2097152 | tf_op jit(solution)/shard_map/all_to_all | solution.py:9
  87.1 79.2 %all-gather.7.cloned.1.call-start = ((), (), s32[]{:S(2)}) async-start(), calls=%async_computation.10 | async-start | bytes 2785280 | tf_op jit(solution)/shard_map/all_gather | solution.py:75
  115.9 7.5 %copy-start.1 = (f32[32,32,256]{2,1,0:T(8,128)}, f32[32,32,256]{2,1,0:T(8,128)S(1)}, u32[]{:S(2)}) copy-start(f32[32,32,256]{2,1,0:T(8,128)S(1)} %all-to-all-done.2) | copy-start | bytes 3145732
  115.9 7.5 %copy-start.5 = (f32[1024,32]{0,1:T(8,128)S(1)}, f32[1024,32]{0,1:T(8,128)}, u32[]{:S(2)}) copy-start(f32[1024,32]{0,1:T(8,128)} %squeeze.15) | copy-start | bytes 393220
  158.9 33.2 %all-to-all-start.4 = ((f32[32,32,256]{2,1,0:T(8,128)}), f32[32,32,256]{2,1,0:T(8,128)S(1)}, u32[]{:S(2)}, u32[]{:S(2)}) async-start(f32[32,32,256]{2,1,0:T(8,128)} %broadcast_in_dim.19), calls=%async_computation.4 | async-start | bytes 2097152 | tf_op jit(solution)/shard_map/all_to_all | solution.py:9
  164.1 77.9 %all-gather.9.cloned.1.call-start = ((), (), s32[]{:S(2)}) async-start(), calls=%async_computation.11 | async-start | bytes 2785280 | tf_op jit(solution)/shard_map/all_gather | solution.py:75
  198.1 0.9 copy-start.2
  233.5 34.3 %copy-start.3 = (f32[640,256]{1,0:T(8,128)S(1)}, f32[640,256]{1,0:T(8,128)}, u32[]{:S(2)}) copy-start(f32[640,256]{1,0:T(8,128)} %copy-done.2) | copy-start | bytes 1966084
  234.6 33.2 %all-to-all-start.6 = ((f32[32,32,256]{2,1,0:T(8,128)}), f32[32,32,256]{2,1,0:T(8,128)S(1)}, u32[]{:S(2)}, u32[]{:S(2)}) async-start(f32[32,32,256]{2,1,0:T(8,128)} %broadcast_in_dim.20), calls=%async_computation.6 | async-start | bytes 2097152 | tf_op jit(solution)/shard_map/all_to_all | solution.py:9
  239.8 105.5 %all-gather.11.cloned.1.call-start = ((), (), s32[]{:S(2)}) async-start(), calls=%async_computation.12 | async-start | bytes 2785280 | tf_op jit(solution)/shard_map/all_gather | solution.py:75
  273.8 0.8 copy-start.4
  311.5 33.2 %all-to-all-start.8 = ((f32[32,32,256]{2,1,0:T(8,128)}), f32[32,32,256]{2,1,0:T(8,128)S(1)}, u32[]{:S(2)}, u32[]{:S(2)}) async-start(f32[32,32,256]{2,1,0:T(8,128)} %broadcast_in_dim.42), calls=%async_computation.8 | async-start | bytes 2097152 | tf_op jit(solution)/shard_map/all_to_all | solution.py:9
Sparse Core Ops, SparseCore 0:
  22.9 45.2 all-gather.4
  90.6 40.5 all-gather.6
  167.1 39.7 all-gather.8
  243.0 39.7 all-gather.10
where the time goes:
time: 360 us; the launch traced here: 359 us
  blocking collectives  139 us (39%)
  waiting for transfers between devices  119 us (33%)
  starting transfers between devices  32.1 us (9%)
  matrix products  31.2 us (9%)
  local copies, waits for them, and re-layouts  20.8 us (6%)
  between operations  14 us (4%)
    all_to_all x4, blocking collectives, summed_on_arrival(): lax.all_to_all(blocks, axis, split_axis=0, concat_axis=0, tiled=True)  139 us
    all_to_all x5, waiting for transfers between devices, from_everyone(): lax.all_to_all(jnp.broadcast_to(array[None], (length, *array.shape)), axi...  119 us
    all_to_all x5, starting transfers between devices, from_everyone(): lax.all_to_all(jnp.broadcast_to(array[None], (length, *array.shape)), axi...  31.7 us
    dot_general x4, matrix products, contract(): jnp.einsum('rpc,pcd->rd', lower_rows, stacked, precision=lax.Precision.HI...  26.4 us
  transfers between devices with their start and end apart: 9, of which 5 were waited for; matrix products, arithmetic and copies ran while one was open for 12% of the time, Pallas kernels for 0%

commit v1 on v0

v1 whole, which is shorter than its diff:
```python
import jax
import jax.numpy as jnp
from jax import lax
from jax.sharding import Mesh, PartitionSpec as P

PREC = lax.Precision.HIGH
QUADS = 4
RHS = ("z", "core")
GROUP = ("x", "yp")


def spread(array, axes):
    length = lax.axis_size(axes)
    return lax.all_to_all(
        jnp.broadcast_to(array[None], (length, *array.shape)), axes, 0, 0, tiled=True
    )


def body(factor, inverses, right_side):
    lower = jnp.transpose(factor[0], (1, 2, 0))
    inv = inverses[0]
    current = right_side[0]
    panels, cols, _ = lower.shape
    width = inv.shape[2]
    count = current.shape[1]
    tail = panels * width
    quads = lax.axis_size("yq")
    nx, npair = lax.axis_size("x"), lax.axis_size("yp")
    group = nx * npair
    per = count // quads
    rows = quads * width
    half = cols // npair

    small = jnp.concatenate(
        [lower[k, :, (k + 1) * width : tail] for k in range(panels - 1)], axis=1
    )
    steps = small.shape[1] // width
    diag = jnp.transpose(inv, (1, 0, 2)).reshape(cols, panels * width)
    shared = jnp.concatenate([small, diag], axis=1)
    first = jnp.transpose(current[:tail]).reshape(quads, per, tail)
    sent = jnp.concatenate(
        [first, jnp.broadcast_to(shared[None], (quads, *shared.shape))], axis=2
    )
    got = lax.all_to_all(sent, "yq", 0, 0, tiled=True)
    heads = jnp.transpose(
        got[:, :, :tail].reshape(quads, per, panels, width), (2, 1, 0, 3)
    ).reshape(panels, per, rows)
    small = jnp.transpose(
        got[:, :, tail : tail + steps * width].reshape(quads, cols, steps, width), (1, 2, 0, 3)
    ).reshape(cols, steps * rows)
    diag = jnp.transpose(
        got[:, :, tail + steps * width :].reshape(quads, cols, panels, width), (1, 2, 0, 3)
    ).reshape(cols, panels * rows)

    diag0 = spread(diag[:, :rows], RHS)
    rest = jnp.concatenate([diag[:, rows:], small], axis=1)
    rest = lax.all_gather(rest.reshape(npair, half, -1), RHS, axis=1)
    trail = jnp.transpose(lower[:, :, tail:], (1, 0, 2)).reshape(npair, half, -1)
    trail, _ = lax.optimization_barrier((trail, rest[0, 0, 0, 0]))
    trail = lax.all_gather(trail, RHS, axis=1)

    def by_group(block):
        return block.reshape(npair, nx, rows, block.shape[-1])

    def diagonal(k):
        if k == 0:
            return jnp.transpose(
                diag0.reshape(nx, quads, npair, half, rows), (2, 0, 1, 3, 4)
            ).reshape(npair, nx, rows, rows)
        return by_group(rest[..., (k - 1) * rows : k * rows])

    offset = (panels - 1) * rows
    whole = []
    for k in range(panels):
        partial = jnp.einsum(
            "mj,pxij->xpmi", heads[k], diagonal(k), precision=PREC,
            preferred_element_type=jnp.float32,
        ).reshape(group, per, rows)
        mine = lax.all_to_all(partial, GROUP, 0, 0, tiled=True).sum(axis=0)
        if k < panels - 1:
            solved = spread(mine, GROUP)
            n = (panels - 1 - k) * rows
            lines = by_group(rest[..., offset : offset + n])
            offset += n
            change = jnp.einsum(
                "xpmc,pxcn->mn", solved.reshape(nx, npair, per, rows), lines,
                precision=PREC, preferred_element_type=jnp.float32,
            )
            update = jnp.transpose(change.reshape(per, panels - 1 - k, rows), (1, 0, 2))
            heads = heads.at[k + 1 :].add(-update)
            every = spread(solved, "yq")
            every = jnp.transpose(every, (1, 0, 2, 3))
        else:
            every = spread(spread(mine, "yq"), GROUP)
        whole.append(every.reshape(nx, npair, count, rows))

    place = lax.axis_index("x") * npair + lax.axis_index("yp")
    lane = lax.axis_index("yq") * width
    mine = []
    total = 0
    for k in range(panels):
        got = whole[k].reshape(group, count, rows)
        piece = lax.dynamic_slice(got, (place, 0, lane), (1, count, width))[0]
        mine.append(jnp.transpose(piece))
        width_tail = lower.shape[2] - tail
        lines = by_group(trail[..., k * width_tail : (k + 1) * width_tail])
        total = total + jnp.einsum(
            "xpmc,pxcn->nm", whole[k], lines, precision=PREC,
            preferred_element_type=jnp.float32,
        )
    return (jnp.concatenate(mine, axis=0)[None], (current[tail:] - total)[None])


def solution(mesh):
    nx, ny, nz, nc = SIZES(mesh)
    fine = Mesh(
        mesh.devices.reshape(nx, QUADS, ny // QUADS, nz, nc), ("x", "yq", "yp", "z", "core")
    )
    row = ("x", "yq", "yp")
    in_specs = (P(row, None, None, RHS), P(row, None, RHS, None), P(row, None, RHS))
    out_specs = (P(row, None, RHS), P(row, None, RHS))
    return jax.shard_map(body, mesh=fine, in_specs=in_specs, out_specs=out_specs, check_vma=False)


def SIZES(mesh):
    nrow, nrhs = mesh.shape["row"], mesh.shape["rhs"]
    nx = 4 if nrow % 32 == 0 else 2
    return nx, nrow // nx, nrhs // 2, 2
```

time: 360 us -> 293 us (0.81)
  waiting for transfers between devices: 119 us -> 73.1 us
  blocking collectives: 139 us -> 121 us
  matrix products: 31.2 us -> 15.1 us
  local copies, waits for them, and re-layouts: 20.8 us -> 33.7 us
    all_to_all x5 -> x6, waiting for transfers between devices: 119 us -> 70.8 us  [spread(): lax.all_to_all(jnp.broadcast_to(array[None], (length, *array.shape)), axe...]
    all_to_all x4 -> x8, blocking collectives: 139 us -> 121 us  [the longest x4 50.2 us: body(): mine = lax.all_to_all(partial, GROUP, 0, 0, tiled=True).sum(axis=0)]
    dot_general x8 -> x11, matrix products: 31.2 us -> 15.1 us  [the longest x4 10.9 us: body(): jnp.einsum('xpmc,pxcn->nm', whole[k], lines, precision=PREC, preferred_el...]
    slice x9 -> x18, local copies, waits for them, and re-layouts: 7.5 us -> 13 us  [the longest x1 6.29 us: body(): lines = by_group(trail[..., k * width_tail:(k + 1) * width_tail])]
    all_to_all x5 -> x6, starting transfers between devices: 31.7 us -> 32.6 us  [spread(): lax.all_to_all(jnp.broadcast_to(array[None], (length, *array.shape)), axe...]
  transfers between devices with their start and end apart: 9 -> 8, of which waited for: 5 -> 6; matrix products, arithmetic and copies ran while one was open for 12% -> 8% of each run, Pallas kernels for 0% -> 0%
where the time goes in v1:
time: 293 us; the launch traced here: 292 us
  blocking collectives  121 us (41%)
  waiting for transfers between devices  73.1 us (25%)
  local copies, waits for them, and re-layouts  33.7 us (12%)
  starting transfers between devices  32.7 us (11%)
  matrix products  15.1 us (5%)
  between operations  14.6 us (5%)
    all_to_all x6, waiting for transfers between devices, spread(): lax.all_to_all(jnp.broadcast_to(array[None], (length, *array.shape)), axe...  70.8 us
    all_to_all x4, blocking collectives, body(): mine = lax.all_to_all(partial, GROUP, 0, 0, tiled=True).sum(axis=0)  50.2 us
    all_to_all x3, blocking collectives, spread(): lax.all_to_all(jnp.broadcast_to(array[None], (length, *array.shape)), axe...  49.5 us
    all_to_all x6, starting transfers between devices, spread(): lax.all_to_all(jnp.broadcast_to(array[None], (length, *array.shape)), axe...  32.6 us
    all_to_all x1, blocking collectives, body(): got = lax.all_to_all(sent, 'yq', 0, 0, tiled=True)  21.1 us
    dot_general x4, matrix products, body(): jnp.einsum('xpmc,pxcn->nm', whole[k], lines, precision=PREC, preferred_el...  10.9 us
    slice x1, local copies, waits for them, and re-layouts, body(): lines = by_group(trail[..., k * width_tail:(k + 1) * width_tail])  6.29 us
  transfers between devices with their start and end apart: 8, of which 6 were waited for; matrix products, arithmetic and copies ran while one was open for 8% of the time, Pallas kernels for 0%

profile of v1, /device:TPU:8, one launch (start us, length us, event | category | flops | bytes accessed | tf_op | source)
XLA Modules:
  0.0 291.6 jit_solution(15379413939195896838)
XLA Ops:
  7.2 0.8 slice_bitcast_fusion.5
  8.0 0.8 slice_bitcast_fusion.6
  8.9 0.8 slice_bitcast_fusion.7
  9.7 0.9 copy.87
  10.6 0.9 slice.158
  11.7 0.1 pad_maximum_fusion.2
  11.9 21.1 %all_to_all.70 = f32[4,64,448]{2,1,0:T(8,128)S(1)} all-to-all(f32[4,64,448]{2,1,0:T(8,128)S(1)} %pad_maximum_fusion), channel_id=1, replica_groups=mesh['x'=4,'yq'=4,'yp'=2,'z'=8,'core'=2] {'yq'}, dimensions={0} | all-to-all | bytes 917504 | tf_op jit(solution)/shard_map/all_to_all | solution.py:44
  33.0 0.1 copy.149
  33.4 0.2 copy.151
  33.6 0.3 copy.99
  33.9 0.5 concatenate.26
  34.4 0.7 pad_maximum_fusion.1
  35.3 0.4 copy.121
  35.7 1.2 reshape.235
  37.0 0.9 broadcast_in_dim.25
  37.9 10.4 %all-to-all-start.1 = ((f32[16,64,128]{2,1,0:T(8,128)}), f32[16,64,128]{2,1,0:T(8,128)S(1)}, u32[]{:S(2)}, u32[]{:S(2)}) async-start(f32[16,64,128]{2,1,0:T(8,128)} %broadcast_in_dim.25), calls=%async_computation.1 | async-start | bytes 1048576 | tf_op jit(solution)/shard_map/all_to_all | solution.py:14
  48.3 0.1 copy.150
  48.5 18.9 %all-to-all-done.1 = f32[16,64,128]{2,1,0:T(8,128)S(1)} async-done(((f32[16,64,128]{2,1,0:T(8,128)}), f32[16,64,128]{2,1,0:T(8,128)S(1)}, u32[]{:S(2)}, u32[]{:S(2)}) %all-to-all-start.1) | async-done | bytes 524320 | tf_op jit(solution)/shard_map/all_to_all | solution.py:14
  67.5 0.4 convolution_bitcast_fusion.7
  67.9 14.4 %all_to_all.71 = f32[8,64,128]{2,1,0:T(8,128)S(1)} all-to-all(f32[8,64,128]{2,1,0:T(8,128)S(1)} %bitcast.261), channel_id=1, replica_groups=mesh['x'=4,'yq'=4,'yp'=2,'z'=8,'core'=2] {'x','yp'}, dimensions={0} | all-to-all | bytes 524288 | tf_op jit(solution)/shard_map/all_to_all | solution.py:79
  82.4 0.7 broadcast_in_dim.26
  83.1 4.6 %all-to-all-start.3 = ((f32[8,64,128]{2,1,0:T(8,128)}), f32[8,64,128]{2,1,0:T(8,128)S(1)}, u32[]{:S(2)}, u32[]{:S(2)}) async-start(f32[8,64,128]{2,1,0:T(8,128)} %broadcast_in_dim.26), calls=%async_computation.3 | async-start | bytes 524288 | tf_op jit(solution)/shard_map/all_to_all | solution.py:14
  87.7 0.8 copy.105
  88.5 2.3 all-gather.4.cloned.1.call-done
  90.8 1.4 slice-done
  92.3 0.5 copy.103
  92.8 2.8 fusion.34
  95.7 0.8 fusion.17
  96.5 0.4 convolution_bitcast_fusion.6
  97.0 13.2 %all_to_all.72 = f32[8,64,128]{2,1,0:T(8,128)S(1)} all-to-all(f32[8,64,128]{2,1,0:T(8,128)S(1)} %bitcast.262), channel_id=1, replica_groups=mesh['x'=4,'yq'=4,'yp'=2,'z'=8,'core'=2] {'x','yp'}, dimensions={0} | all-to-all | bytes 524288 | tf_op jit(solution)/shard_map/all_to_all | solution.py:79
  110.2 0.7 broadcast_in_dim.28
  110.9 4.5 %all-to-all-start.6 = ((f32[8,64,128]{2,1,0:T(8,128)}), f32[8,64,128]{2,1,0:T(8,128)S(1)}, u32[]{:S(2)}, u32[]{:S(2)}) async-start(f32[8,64,128]{2,1,0:T(8,128)} %broadcast_in_dim.28), calls=%async_computation.6 | async-start | bytes 524288 | tf_op jit(solution)/shard_map/all_to_all | solution.py:14
  115.5 0.3 copy.111
  115.9 1.1 copy.109
  117.0 4.6 %all-to-all-done.6 = f32[8,64,128]{2,1,0:T(8,128)S(1)} async-done(((f32[8,64,128]{2,1,0:T(8,128)}), f32[8,64,128]{2,1,0:T(8,128)S(1)}, u32[]{:S(2)}, u32[]{:S(2)}) %all-to-all-start.6) | async-done | bytes 262176 | tf_op jit(solution)/shard_map/all_to_all | solution.py:14
  121.6 0.6 fusion.22
  122.2 0.4 convolution_bitcast_fusion.5
  122.6 9.9 %all_to_all.73 = f32[8,64,128]{2,1,0:T(8,128)S(1)} all-to-all(f32[8,64,128]{2,1,0:T(8,128)S(1)} %bitcast.263), channel_id=1, replica_groups=mesh['x'=4,'yq'=4,'yp'=2,'z'=8,'core'=2] {'x','yp'}, dimensions={0} | all-to-all | bytes 524288 | tf_op jit(solution)/shard_map/all_to_all | solution.py:79
  132.6 9.9 %all_to_all.74 = f32[8,64,128]{2,1,0:T(8,128)S(1)} all-to-all(f32[8,64,128]{2,1,0:T(8,128)S(1)} %broadcast_in_dim.30), channel_id=1, replica_groups=mesh['x'=4,'yq'=4,'yp'=2,'z'=8,'core'=2] {'x','yp'}, dimensions={0} | all-to-all | bytes 524288 | tf_op jit(solution)/shard_map/all_to_all | solution.py:14
  142.6 1.1 broadcast_in_dim.27
  143.7 3.5 %all-to-all-start.4 = ((f32[4,8,64,128]{3,2,1,0:T(8,128)}), f32[4,8,64,128]{3,2,1,0:T(8,128)S(1)}, u32[]{:S(2)}, u32[]{:S(2)}) async-start(f32[4,8,64,128]{3,2,1,0:T(8,128)} %broadcast_in_dim.27), calls=%async_computation.4 | async-start | bytes 2097152 | tf_op jit(solution)/shard_map/all_to_all | solution.py:14
  147.3 1.0 fusion.26
  148.4 0.4 convolution_bitcast_fusion.4
  148.8 19.6 %all-to-all-done.4 = f32[4,8,64,128]{3,2,1,0:T(8,128)S(1)} async-done(((f32[4,8,64,128]{3,2,1,0:T(8,128)}), f32[4,8,64,128]{3,2,1,0:T(8,128)S(1)}, u32[]{:S(2)}, u32[]{:S(2)}) %all-to-all-start.4) | async-done | bytes 1048608 | tf_op jit(solution)/shard_map/all_to_all | solution.py:14
  168.4 12.6 %all_to_all.75 = f32[8,64,128]{2,1,0:T(8,128)S(1)} all-to-all(f32[8,64,128]{2,1,0:T(8,128)S(1)} %bitcast.259), channel_id=1, replica_groups=mesh['x'=4,'yq'=4,'yp'=2,'z'=8,'core'=2] {'x','yp'}, dimensions={0} | all-to-all | bytes 524288 | tf_op jit(solution)/shard_map/all_to_all | solution.py:79
  181.0 1.1 broadcast_in_dim.29
  182.1 3.5 %all-to-all-start.7 = ((f32[4,8,64,128]{3,2,1,0:T(8,128)}), f32[4,8,64,128]{3,2,1,0:T(8,128)S(1)}, u32[]{:S(2)}, u32[]{:S(2)}) async-start(f32[4,8,64,128]{3,2,1,0:T(8,128)} %broadcast_in_dim.29), calls=%async_computation.7 | async-start | bytes 2097152 | tf_op jit(solution)/shard_map/all_to_all | solution.py:14
  185.7 22.6 %all-to-all-done.7 = f32[4,8,64,128]{3,2,1,0:T(8,128)S(1)} async-done(((f32[4,8,64,128]{3,2,1,0:T(8,128)}), f32[4,8,64,128]{3,2,1,0:T(8,128)S(1)}, u32[]{:S(2)}, u32[]{:S(2)}) %all-to-all-start.7) | async-done | bytes 1048608 | tf_op jit(solution)/shard_map/all_to_all | solution.py:14
  208.3 13.7 %all_to_all.76 = f32[4,64,128]{2,1,0:T(8,128)S(1)} all-to-all(f32[4,64,128]{2,1,0:T(8,128)S(1)} %broadcast_in_dim.32), channel_id=1, replica_groups=mesh['x'=4,'yq'=4,'yp'=2,'z'=8,'core'=2] {'yq'}, dimensions={0} | all-to-all | bytes 262144 | tf_op jit(solution)/shard_map/all_to_all | solution.py:14
  222.1 25.9 %all_to_all.77 = f32[4,8,64,128]{3,2,1,0:T(8,128)} all-to-all(f32[4,8,64,128]{3,2,1,0:T(8,128)S(1)} %broadcast_in_dim.31), channel_id=1, replica_groups=mesh['x'=4,'yq'=4,'yp'=2,'z'=8,'core'=2] {'yq'}, dimensions={0} | all-to-all | bytes 2097152 | tf_op jit(solution)/shard_map/all_to_all | solution.py:14
  248.0 1.1 broadcast_in_dim.33
  249.1 6.1 %all-to-all-start.13 = ((f32[8,4,64,128]{3,2,1,0:T(8,128)}), f32[8,4,64,128]{3,2,1,0:T(8,128)S(1)}, u32[]{:S(2)}, u32[]{:S(2)}) async-start(f32[8,4,64,128]{3,2,1,0:T(8,128)} %broadcast_in_dim.33), calls=%async_computation.13 | async-start | bytes 2097152 | tf_op jit(solution)/shard_map/all_to_all | solution.py:14
  255.2 1.4 copy.95
  256.9 1.0 copy-done
  257.9 0.1 constant_dynamic-slice_fusion.2
  258.2 2.4 copy.114
  260.6 5.0 %all-to-all-done.13 = f32[8,4,64,128]{3,2,1,0:T(8,128)S(1)} async-done(((f32[8,4,64,128]{3,2,1,0:T(8,128)}), f32[8,4,64,128]{3,2,1,0:T(8,128)S(1)}, u32[]{:S(2)}, u32[]{:S(2)}) %all-to-all-start.13) | async-done | bytes 1048608 | tf_op jit(solution)/shard_map/all_to_all | solution.py:14
  265.6 1.0 constant_dynamic-slice_fusion
  266.8 0.7 maximum_bitcast_fusion
  267.4 6.3 %fusion.33 = (f32[2,16,32,576]{3,2,1,0:T(8,128)S(1)}, f32[2,16,32,576]{3,2,1,0:T(8,128)S(1)}, f32[2,16,32,576]{3,2,1,0:T(8,128)S(1)}, f32[2,16,32,576]{3,2,1,0:T(8,128)S(1)}) fusion(f32[2,16,32,2304]{3,2,1,0:T(8,128)} %bitcast.228), kind=kLoop, calls=%fused_computation.49 | loop fusion | bytes 18874368 | tf_op jit(solution)/shard_map/slice | solution.py:106
  273.7 3.4 %convolution_bitcast_fusion.1 = f32[256,576]{0,1:T(8,128)S(1)} fusion(f32[2,4,128,576]{3,2,1,0:T(8,128)S(1)} %bitcast.232, f32[4,2,256,128]{3,2,1,0:T(8,128)} %bitcast.242), kind=kOutput, calls=%fused_computation.3 | convolution fusion | flops 905969664 | bytes 3997696 | tf_op jit(solution)/shard_map/xpmc,pxcn->nm/dot_general | solution.py:107
  277.2 2.2 convolution_bitcast_fusion
  279.4 2.2 convolution_bitcast_fusion.2
  281.7 3.1 %fusion.7 = f32[1,576,256]{2,1,0:T(8,128)} fusion(f32[256,576]{0,1:T(8,128)S(1)} %convolution_bitcast_fusion, f32[256,576]{0,1:T(8,128)S(1)} %convolution_bitcast_fusion.1, f32[256,576]{0,1:T(8,128)S(1)} %convolution_bitcast_fusion.2, f32[2,4,128,576]{3,2,1,0:T(8,128)S(1)} %bitcast.229, f32[4,2,256,128]{3,2,1,0:T(8,128)S(1)} %bitcast.236, ...), kind=kOutput, calls=%fused_computation.11 | convolution fusion | flops 906559488 | bytes 6356992 | tf_op jit(solution)/shard_map/xpmc,pxcn->nm/dot_general | solution.py:107
  (66 shorter events, 1.9 us)
Async XLA Ops:
  7.2 83.6 %all-gather.4.cloned.1.call-start = ((), (), s32[]{:S(2)}) async-start(), calls=%async_computation.14 | async-start | bytes 5013504 | tf_op jit(solution)/shard_map/all_gather | solution.py:57
  33.2 2.0 copy-start.7
  35.2 232.3 %all-gather.6.cloned.1.call-start = ((), (), s32[]{:S(2)}) async-start(), calls=%async_computation.15 | async-start | bytes 10027008 | tf_op jit(solution)/shard_map/all_gather | solution.py:60
  37.9 29.5 %all-to-all-start.1 = ((f32[16,64,128]{2,1,0:T(8,128)}), f32[16,64,128]{2,1,0:T(8,128)S(1)}, u32[]{:S(2)}, u32[]{:S(2)}) async-start(f32[16,64,128]{2,1,0:T(8,128)} %broadcast_in_dim.25), calls=%async_computation.1 | async-start | bytes 1048576 | tf_op jit(solution)/shard_map/all_to_all | solution.py:14
  83.1 12.6 %all-to-all-start.3 = ((f32[8,64,128]{2,1,0:T(8,128)}), f32[8,64,128]{2,1,0:T(8,128)S(1)}, u32[]{:S(2)}, u32[]{:S(2)}) async-start(f32[8,64,128]{2,1,0:T(8,128)} %broadcast_in_dim.26), calls=%async_computation.3 | async-start | bytes 524288 | tf_op jit(solution)/shard_map/all_to_all | solution.py:14
  90.8 1.4 slice-start
  92.8 2.9 copy-start.9
  96.5 18.9 %slice-start.1 = ((f32[2,16,32,1152]{3,2,0,1:T(8,128)}), f32[2,16,32,256]{3,2,0,1:T(8,128)S(1)}, s32[]{:S(2)}) async-start(f32[2,16,32,1152]{3,2,0,1:T(8,128)} %all-gather.4.cloned.1.call-done), calls=%async_computation.17 | async-start | bytes 2097152 | tf_op jit(solution)/shard_map/slice | solution.py:83
  110.9 10.6 %all-to-all-start.6 = ((f32[8,64,128]{2,1,0:T(8,128)}), f32[8,64,128]{2,1,0:T(8,128)S(1)}, u32[]{:S(2)}, u32[]{:S(2)}) async-start(f32[8,64,128]{2,1,0:T(8,128)} %broadcast_in_dim.28), calls=%async_computation.6 | async-start | bytes 524288 | tf_op jit(solution)/shard_map/all_to_all | solution.py:14
  122.2 21.5 %copy-start.10 = (f32[2,64,128]{2,1,0:T(8,128)}, f32[2,64,128]{2,1,0:T(8,128)S(1)}, u32[]{:S(2)}) copy-start(f32[2,64,128]{2,1,0:T(8,128)S(1)} %fusion.22) | copy-start | bytes 196612
  122.6 24.6 %copy-start.6 = (f32[2,16,32,128]{3,2,0,1:T(8,128)S(1)}, f32[2,16,32,128]{3,2,0,1:T(8,128)}, u32[]{:S(2)}) copy-start(f32[2,16,32,128]{3,2,0,1:T(8,128)} %get-tuple-element.44) | copy-start | bytes 1572868
  132.6 14.7 %copy-start.5 = (f32[2,16,32,128]{3,2,0,1:T(8,128)S(1)}, f32[2,16,32,128]{3,2,0,1:T(8,128)}, u32[]{:S(2)}) copy-start(f32[2,16,32,128]{3,2,0,1:T(8,128)} %get-tuple-element.43) | copy-start | bytes 1572868
  143.7 24.7 %all-to-all-start.4 = ((f32[4,8,64,128]{3,2,1,0:T(8,128)}), f32[4,8,64,128]{3,2,1,0:T(8,128)S(1)}, u32[]{:S(2)}, u32[]{:S(2)}) async-start(f32[4,8,64,128]{3,2,1,0:T(8,128)} %broadcast_in_dim.27), calls=%async_computation.4 | async-start | bytes 2097152 | tf_op jit(solution)/shard_map/all_to_all | solution.py:14
  168.4 53.7 %copy-start.2 = (f32[4,8,64,128]{3,2,1,0:T(8,128)}, f32[4,8,64,128]{3,2,1,0:T(8,128)S(1)}, u32[]{:S(2)}) copy-start(f32[4,8,64,128]{3,2,1,0:T(8,128)S(1)} %all-to-all-done.4) | copy-start | bytes 3145732
  182.1 26.2 %all-to-all-start.7 = ((f32[4,8,64,128]{3,2,1,0:T(8,128)}), f32[4,8,64,128]{3,2,1,0:T(8,128)S(1)}, u32[]{:S(2)}, u32[]{:S(2)}) async-start(f32[4,8,64,128]{3,2,1,0:T(8,128)} %broadcast_in_dim.29), calls=%async_computation.7 | async-start | bytes 2097152 | tf_op jit(solution)/shard_map/all_to_all | solution.py:14
  208.3 40.8 %copy-start.3 = (f32[4,8,64,128]{3,2,1,0:T(8,128)}, f32[4,8,64,128]{3,2,1,0:T(8,128)S(1)}, u32[]{:S(2)}) copy-start(f32[4,8,64,128]{3,2,1,0:T(8,128)S(1)} %all-to-all-done.7) | copy-start | bytes 3145732
  249.1 16.4 %all-to-all-start.13 = ((f32[8,4,64,128]{3,2,1,0:T(8,128)}), f32[8,4,64,128]{3,2,1,0:T(8,128)S(1)}, u32[]{:S(2)}, u32[]{:S(2)}) async-start(f32[8,4,64,128]{3,2,1,0:T(8,128)} %broadcast_in_dim.33), calls=%async_computation.13 | async-start | bytes 2097152 | tf_op jit(solution)/shard_map/all_to_all | solution.py:14
  255.2 1.5 copy-start.4
  256.9 1.0 copy-start
  277.2 2.2 copy-start.1
  279.4 2.2 copy-start.8
Sparse Core Ops, SparseCore 0:
  35.3 55.4 all-gather.3
  93.5 61.0 all-gather.5

commit v2 on v1

v2 whole, which is shorter than its diff:
```python
import jax
import jax.numpy as jnp
from jax import lax
from jax.experimental import pallas as pl
from jax.experimental.pallas import tpu as pltpu
from jax.sharding import Mesh, PartitionSpec as P

QUADS = 4
RHS = ("z", "core")
GROUP = ("yp", "x")
F32 = jnp.float32


def halves(value):
    high = value.astype(jnp.bfloat16)
    return high, (value - high.astype(F32)).astype(jnp.bfloat16)


def dot(a, b, dims):
    def one(u, v):
        return lax.dot_general(u, v, (dims, ((), ())), preferred_element_type=F32)

    ah, al = halves(a)
    bh, bl = halves(b)
    return one(ah, bh) + (one(ah, bl) + one(al, bh))


NN = ((1,), (0,))
NT = ((1,), (1,))


def call(kernel, shapes, in_specs=None, **more):
    shapes = [jax.ShapeDtypeStruct(s, F32) for s in shapes]
    out = pl.pallas_call(
        kernel,
        out_shape=shapes,
        grid=(1,),
        in_specs=in_specs,
        **more,
    )
    return out


def whole(shape):
    return pl.BlockSpec(shape, lambda i: (0,) * len(shape))


def pack(f_ref, inv_ref, r_ref, out_ref):
    quads, _, _ = out_ref.shape
    cols = f_ref.shape[1]
    per = r_ref.shape[1] // quads
    w = inv_ref.shape[1]
    turned = r_ref[...].T
    wide = jnp.concatenate([f_ref[0][:, w:], f_ref[2][:, 3 * w :]], axis=1)
    mid = f_ref[1][:, 2 * w :]
    mid = jnp.concatenate([mid[: cols // 2], mid[cols // 2 :]], axis=1)
    diag = jnp.concatenate([inv_ref[k].T for k in range(4)], axis=1)
    for q in range(quads):
        out_ref[q, :per] = turned[q * per : (q + 1) * per]
        out_ref[q, per : per + cols] = wide
        out_ref[q, per + cols : per + cols + cols // 2] = mid
        out_ref[q, per + cols + cols // 2 :] = diag


def sort(w, per, got_ref, heads_ref, pay_ref, first_ref):
    quads = got_ref.shape[0]
    half = pay_ref.shape[2]
    cols = 2 * half
    a, b, d = per, per + cols, per + cols + half

    def lanes(start, n, at):
        return jnp.concatenate(
            [got_ref[q, start : start + n][:, at : at + w] for q in range(quads)], axis=1
        )

    for k in range(4):
        heads_ref[k] = lanes(0, per, k * w)
    for h in range(2):
        for k in range(1, 4):
            pay_ref[k - 1, h] = lanes(d + h * half, half, k * w)
        for j in range(3):
            pay_ref[3 + j, h] = lanes(a + h * half, half, j * w)
        for j in range(2):
            pay_ref[6 + j, h] = lanes(b, half, h * 2 * w + j * w)
        pay_ref[8, h] = lanes(a + h * half, half, 3 * w)
        piece = lanes(d + h * half, half, 0)
        for c in range(first_ref.shape[0]):
            first_ref[c, h] = piece


def begin(head_ref, first_ref, out_ref):
    blocks, pair, half, rows = first_ref.shape
    head = head_ref[0]
    for p in range(pair):
        block = first_ref[:, p].reshape(blocks * half, rows)
        y = dot(head, block, NT)
        n = blocks * half // rows
        for x in range(n):
            out_ref[p * n + x] = y[:, x * rows : (x + 1) * rows]


def add_up(got_ref, out_ref):
    total = jnp.sum(got_ref[...], axis=0)
    for c in range(out_ref.shape[0]):
        out_ref[c] = total


def advance(pick, quad_ref, solved_ref, heads_ref, lines_ref, diag_ref, heads_out, y_out):
    group = solved_ref.shape[0]
    left = lines_ref.shape[0]
    rows = diag_ref.shape[2]
    if pick:
        quad = quad_ref[0]
        x = jnp.concatenate([solved_ref[s, quad] for s in range(group)], axis=1)
    else:
        x = jnp.concatenate([solved_ref[s] for s in range(group)], axis=1)
    base = heads_ref.shape[0] - left
    head = None
    for b in range(left):
        new = heads_ref[base + b] - dot(x, lines_ref[b], NN)
        heads_out[b] = new
        if b == 0:
            head = new
    y = dot(head, diag_ref[0], NT)
    for s in range(group):
        y_out[s] = y[:, s * rows : (s + 1) * rows]


def gathered_first(x_ref, pair):
    parts = [x_ref[:, 0, s] if len(x_ref.shape) == 5 else x_ref[s] for s in range(pair)]
    parts = [p.reshape(-1, p.shape[-1]) for p in parts]
    return jnp.concatenate(parts, axis=1)


def trail_sum(x_ref, f_ref, out_ref):
    @pl.when(pl.program_id(0) == 0)
    def _():
        out_ref[...] = jnp.zeros_like(out_ref)

    out_ref[...] += dot(gathered_first(x_ref, 2), f_ref[0, 0], NN)


def trail_more(x_ref, f_ref, init_ref, out_ref):
    @pl.when(pl.program_id(0) == 0)
    def _():
        out_ref[...] = init_ref[...]

    out_ref[...] += dot(gathered_first(x_ref, 2), f_ref[0, 0], NN)


def trail_end(x_ref, f_ref, init_ref, r_ref, out_ref, acc_ref):
    @pl.when(pl.program_id(0) == 0)
    def _():
        acc_ref[...] = init_ref[...]

    acc_ref[...] += dot(gathered_first(x_ref, 2), f_ref[0, 0], NN)

    @pl.when(pl.program_id(0) == pl.num_programs(0) - 1)
    def _():
        n = out_ref.shape[0]
        out_ref[...] = r_ref[r_ref.shape[0] - n :] - acc_ref[...].T


def trail_call(kernel, x, f, k, steps, out_shape, extra=(), scratch=()):
    per_pair = f.shape[2] // 256
    per_panel = f.shape[1] * per_pair
    if x.ndim == 5:
        x_spec = pl.BlockSpec(
            (x.shape[0], 1, 2, *x.shape[3:]), lambda i: (0, i // per_panel, i % per_panel, 0, 0)
        )
    else:
        x_spec = pl.BlockSpec((2, *x.shape[1:]), lambda i: (i % per_panel, 0, 0, 0))
    f_spec = pl.BlockSpec(
        (1, 1, 256, f.shape[3]),
        lambda i: (k + i // per_panel, (i % per_panel) // per_pair, i % per_pair, 0),
    )
    return pl.pallas_call(
        kernel,
        out_shape=jax.ShapeDtypeStruct(out_shape, F32),
        grid=(steps * per_panel,),
        in_specs=[x_spec, f_spec] + [whole(e.shape) for e in extra],
        out_specs=whole(out_shape),
        scratch_shapes=scratch,
    )(x, f, *extra)


def spread(array, axes):
    return lax.all_to_all(
        jnp.broadcast_to(array[None], (lax.axis_size(axes), *array.shape)), axes, 0, 0, tiled=True
    )


def body(factor, inverses, right_side):
    lower = jnp.transpose(factor[0], (1, 2, 0))
    inv = jnp.transpose(inverses[0], (0, 2, 1))
    current = right_side[0]
    panels, cols, _ = lower.shape
    width = inv.shape[1]
    count = current.shape[1]
    tail = panels * width
    quads = lax.axis_size("yq")
    nx, npair = lax.axis_size("x"), lax.axis_size("yp")
    blocks = lax.axis_size(RHS)
    group = nx * npair
    per = count // quads
    rows = quads * width
    half = cols // npair
    quad = lax.axis_index("yq")

    (sent,) = call(
        pack,
        [(quads, per + 2 * cols + half, tail)],
        [whole((panels, cols, tail)), whole(inv.shape), whole((tail, count))],
    )(lower, inv, current)
    got = lax.all_to_all(sent, "yq", 0, 0, tiled=True)
    heads, pay, first = call(
        lambda *refs: sort(width, per, *refs),
        [(panels, per, rows), (9, npair, half, rows), (blocks, npair, half, rows)],
        [whole(sent.shape)],
    )(got)
    first = lax.all_to_all(first, RHS, 0, 0, tiled=True)
    rest = lax.all_gather(pay, RHS, axis=2, tiled=True)
    trail = lower[:, :, tail:].reshape(panels, npair, half, -1)
    trail = lax.all_gather(trail, RHS, axis=2, tiled=True)
    rest = rest.reshape(9, group * rows, rows)

    (y,) = call(
        begin,
        [(group, per, rows)],
        [pl.BlockSpec((1, per, rows), lambda i: (0, 0, 0)), whole(first.shape)],
    )(heads, first)
    block = (group, per, rows)
    early, own, late = [], [], []
    for k in range(panels):
        got = lax.all_to_all(y, GROUP, 0, 0, tiled=True)
        direct = k < 2
        copies = group if direct else quads
        (mine,) = call(add_up, [(copies, per, rows)], [whole(block)])(got)
        if direct:
            solved = lax.all_to_all(mine, GROUP, 0, 0, tiled=True)
            early.append(solved)
        else:
            mine = lax.all_to_all(mine, "yq", 0, 0, tiled=True)
            own.append(mine)
            solved = spread(mine, GROUP)
            late.append(solved)
        if k == panels - 1:
            break
        left = panels - 1 - k
        at = {3: 1, 2: 3, 1: 8}[left]
        heads, y = call(
            lambda *refs, p=not direct: advance(p, *refs),
            [(left, per, rows), block],
            [
                pl.BlockSpec(memory_space=pltpu.SMEM),
                whole(solved.shape),
                whole(heads.shape),
                pl.BlockSpec((left, group * rows, rows), lambda i, at=at: (at, 0, 0)),
                pl.BlockSpec((1, group * rows, rows), lambda i, k=k: (k, 0, 0)),
            ],
        )(quad.reshape(1).astype(jnp.int32), solved, heads, rest, rest)

    early = jnp.stack(early)
    early = lax.all_gather(early, "yq", axis=0)

    place = lax.axis_index("yp") * nx + lax.axis_index("x")
    acc_shape = (count, trail.shape[3])
    acc = trail_call(trail_sum, early, trail, 0, 2, acc_shape)
    acc = trail_call(trail_more, late[0], trail, 2, 1, acc_shape, (acc,))
    out = trail_call(
        trail_end, late[1], trail, 3, 1, (trail.shape[3], count), (acc, current),
        [pltpu.VMEM(acc_shape, F32)],
    )
    pieces = lax.dynamic_index_in_dim(early, place, 2, keepdims=False)
    pieces = jnp.concatenate([jnp.swapaxes(pieces, 0, 1), jnp.stack(own)], axis=0)
    pieces = lax.dynamic_slice_in_dim(pieces, quad * width, width, 3)
    mine = jnp.transpose(pieces, (0, 3, 1, 2)).reshape(tail, count)
    return (mine[None], out[None])


def solution(mesh):
    nx, ny, nz, nc = SIZES(mesh)
    fine = Mesh(
        mesh.devices.reshape(nx, QUADS, ny // QUADS, nz, nc), ("x", "yq", "yp", "z", "core")
    )
    row = ("x", "yq", "yp")
    in_specs = (P(row, None, None, RHS), P(row, None, RHS, None), P(row, None, RHS))
    out_specs = (P(row, None, RHS), P(row, None, RHS))
    return jax.shard_map(body, mesh=fine, in_specs=in_specs, out_specs=out_specs, check_vma=False)


def SIZES(mesh):
    nrow, nrhs = mesh.shape["row"], mesh.shape["rhs"]
    return nrow // 8, 8, nrhs // 2, 2
```

time: 293 us -> 279 us (0.952)
  the two profiles are of different devices: /device:TPU:8 before, /device:TPU:1 now
where the time goes in v2:
time: 279 us; the launch traced here: 277 us
  blocking collectives  164 us (59%)
  waiting for transfers between devices  43.3 us (16%)
  Pallas kernels  41 us (15%)
  between operations  13.8 us (5%)
  starting transfers between devices  7.15 us (3%)
  local copies, waits for them, and re-layouts  5.87 us (2%)
    all_to_all x4, blocking collectives, body(): got = lax.all_to_all(y, GROUP, 0, 0, tiled=True)  41.6 us
    all_gather x1, waiting for transfers between devices, body(): trail = lax.all_gather(trail, RHS, axis=2, tiled=True)  36.4 us
    all_to_all x1, blocking collectives, body(): first = lax.all_to_all(first, RHS, 0, 0, tiled=True)  34.5 us
    all_to_all x1, blocking collectives, spread(): lax.all_to_all(jnp.broadcast_to(array[None], (lax.axis_size(axes), *array...  29.7 us
    all_to_all x2, blocking collectives, body(): mine = lax.all_to_all(mine, 'yq', 0, 0, tiled=True)  28.4 us
    all_to_all x1, blocking collectives, body(): got = lax.all_to_all(sent, 'yq', 0, 0, tiled=True)  20.3 us
    pallas_call x3, Pallas kernels, trail_call(): pl.pallas_call(kernel, out_shape=jax.ShapeDtypeStruct(out_shape, F32), gr...  18.9 us
    all_to_all x1, blocking collectives, body(): solved = lax.all_to_all(mine, GROUP, 0, 0, tiled=True)  9.39 us
  transfers between devices with their start and end apart: 5, of which 2 were waited for; matrix products, arithmetic and copies ran while one was open for 2% of the time, Pallas kernels for 9%

profile of v2, /device:TPU:1, one launch (start us, length us, event | category | flops | bytes accessed | tf_op | source)
XLA Modules:
  0.0 277.3 jit_solution(1676699435238202402)
XLA Ops:
  7.2 0.0 all-gather.5.cloned.1.call-start
  7.2 2.0 shard_map.50
  9.2 20.3 %all_to_all.60.refs_0_ = f32[4,224,128]{2,1,0:T(8,128)} all-to-all(f32[4,224,128]{2,1,0:T(8,128)} %shard_map.50), channel_id=1, replica_groups=mesh['x'=4,'yq'=4,'yp'=2,'z'=8,'core'=2] {'yq'}, dimensions={0} | all-to-all | bytes 917504 | tf_op jit(solution)/shard_map/all_to_all | solution.py:215
  29.5 2.3 shard_map.51
  31.8 0.0 all-gather.5.cloned.1.call-update
  31.9 34.5 %all_to_all.61.first_ref = f32[16,2,32,128]{3,2,1,0:T(8,128)} all-to-all(f32[16,2,32,128]{3,2,1,0:T(8,128)} %get-tuple-element.11), channel_id=1, replica_groups=mesh['x'=4,'yq'=4,'yp'=2,'z'=8,'core'=2] {'z','core'}, dimensions={0} | all-to-all | bytes 1048576 | tf_op jit(solution)/shard_map/all_to_all | solution.py:221
  66.4 2.2 shard_map.52
  68.5 11.2 %all_to_all.62.got_ref = f32[8,64,128]{2,1,0:T(8,128)} all-to-all(f32[8,64,128]{2,1,0:T(8,128)} %shard_map.52), channel_id=1, replica_groups=mesh['x'=4,'yq'=4,'yp'=2,'z'=8,'core'=2] {'yp','x'}, dimensions={0} | all-to-all | bytes 524288 | tf_op jit(solution)/shard_map/all_to_all | solution.py:235
  79.8 1.7 shard_map.53
  81.5 3.4 %all-to-all-start.3 = ((f32[8,64,128]{2,1,0:T(8,128)}), f32[8,64,128]{2,1,0:T(8,128)S(1)}, u32[]{:S(2)}, u32[]{:S(2)}) async-start(f32[8,64,128]{2,1,0:T(8,128)} %shard_map.53), calls=%async_computation.3 | async-start | bytes 524288 | tf_op jit(solution)/shard_map/all_to_all | solution.py:240
  84.9 0.0 all-gather.9.cloned.1.call-start
  85.0 6.8 %all-to-all-done.3.refs_1_ = f32[8,64,128]{2,1,0:T(8,128)S(1)} async-done(((f32[8,64,128]{2,1,0:T(8,128)}), f32[8,64,128]{2,1,0:T(8,128)S(1)}, u32[]{:S(2)}, u32[]{:S(2)}) %all-to-all-start.3) | async-done | bytes 262176 | tf_op jit(solution)/shard_map/all_to_all | solution.py:240
  91.8 0.0 copy-start.2
  91.8 0.0 all-gather.5.cloned.1.call-done
  91.8 0.7 copy-done.2
  92.5 0.0 copy-start.1
  92.5 3.3 %shard_map.54 = (f32[3,64,128]{2,1,0:T(8,128)}, f32[8,64,128]{2,1,0:T(8,128)}) custom-call(s32[1]{0:T(128)} %bitcast.6.refs_0_, f32[8,64,128]{2,1,0:T(8,128)} %copy-done.2, f32[4,64,128]{2,1,0:T(8,128)} %get-tuple-element.10.head_ref.refs_2_, f32[9,1024,128]{2,1,0:T(8,128)} %bitcast.26, f32[9,1024,128]{2,1,0:T(8,128)} %bitcast.27), custom_call_target="tpu_custom_call" | custom-call | tf_op jit(solution)/shard_map/pallas_call | solution.py:251
  95.8 10.2 %all_to_all.63.got_ref = f32[8,64,128]{2,1,0:T(8,128)} all-to-all(f32[8,64,128]{2,1,0:T(8,128)} %get-tuple-element.13), channel_id=1, replica_groups=mesh['x'=4,'yq'=4,'yp'=2,'z'=8,'core'=2] {'yp','x'}, dimensions={0} | all-to-all | bytes 524288 | tf_op jit(solution)/shard_map/all_to_all | solution.py:235
  105.9 1.7 shard_map.55
  107.6 9.4 %all_to_all.64.refs_1_ = f32[8,64,128]{2,1,0:T(8,128)S(1)} all-to-all(f32[8,64,128]{2,1,0:T(8,128)} %shard_map.55), channel_id=1, replica_groups=mesh['x'=4,'yq'=4,'yp'=2,'z'=8,'core'=2] {'yp','x'}, dimensions={0} | all-to-all | bytes 524288 | tf_op jit(solution)/shard_map/all_to_all | solution.py:240
  117.0 0.0 copy-start.3
  117.0 1.9 pad_maximum_fusion
  118.9 0.0 all-gather.9.cloned.1.call-update
  118.9 0.0 all-gather.7.cloned.1.call-start
  119.0 0.0 copy-done.1
  119.0 0.9 slice.4
  119.8 0.0 all-gather.7.cloned.1.call-update
  119.9 0.0 copy-done.3
  119.9 2.9 %shard_map.56 = (f32[2,64,128]{2,1,0:T(8,128)}, f32[8,64,128]{2,1,0:T(8,128)}) custom-call(s32[1]{0:T(128)} %bitcast.6.refs_0_, f32[8,64,128]{2,1,0:T(8,128)} %copy-done.3, f32[3,64,128]{2,1,0:T(8,128)} %get-tuple-element.14.refs_2_, f32[9,1024,128]{2,1,0:T(8,128)} %bitcast.28, f32[9,1024,128]{2,1,0:T(8,128)} %bitcast.29), custom_call_target="tpu_custom_call" | custom-call | tf_op jit(solution)/shard_map/pallas_call | solution.py:251
  122.8 10.1 %all_to_all.65.got_ref = f32[8,64,128]{2,1,0:T(8,128)} all-to-all(f32[8,64,128]{2,1,0:T(8,128)} %get-tuple-element.15), channel_id=1, replica_groups=mesh['x'=4,'yq'=4,'yp'=2,'z'=8,'core'=2] {'yp','x'}, dimensions={0} | all-to-all | bytes 524288 | tf_op jit(solution)/shard_map/all_to_all | solution.py:235
  132.9 1.6 shard_map.57
  134.5 17.1 %all_to_all.66 = f32[4,64,128]{2,1,0:T(8,128)S(1)} all-to-all(f32[4,64,128]{2,1,0:T(8,128)} %shard_map.57), channel_id=1, replica_groups=mesh['x'=4,'yq'=4,'yp'=2,'z'=8,'core'=2] {'yq'}, dimensions={0} | all-to-all | bytes 262144 | tf_op jit(solution)/shard_map/all_to_all | solution.py:243
  151.7 0.1 broadcast_in_dim.6
  151.8 29.7 %all_to_all.67.refs_1_.x_ref = f32[8,4,64,128]{3,2,1,0:T(8,128)} all-to-all(f32[8,4,64,128]{3,2,1,0:T(8,128)S(1)} %broadcast_in_dim.6), channel_id=1, replica_groups=mesh['x'=4,'yq'=4,'yp'=2,'z'=8,'core'=2] {'yp','x'}, dimensions={0} | all-to-all | bytes 2097152 | tf_op jit(solution)/shard_map/all_to_all | solution.py:188
  181.5 2.9 %shard_map.58 = (f32[1,64,128]{2,1,0:T(8,128)}, f32[8,64,128]{2,1,0:T(8,128)}) custom-call(s32[1]{0:T(128)} %bitcast.6.refs_0_, f32[8,4,64,128]{3,2,1,0:T(8,128)} %all_to_all.67.refs_1_.x_ref, f32[2,64,128]{2,1,0:T(8,128)} %get-tuple-element.16.refs_2_, f32[9,1024,128]{2,1,0:T(8,128)} %bitcast.30, f32[9,1024,128]{2,1,0:T(8,128)} %bitcast.31), custom_call_target="tpu_custom_call" | custom-call | tf_op jit(solution)/shard_map/pallas_call | solution.py:251
  184.4 10.1 %all_to_all.68.got_ref = f32[8,64,128]{2,1,0:T(8,128)} all-to-all(f32[8,64,128]{2,1,0:T(8,128)} %get-tuple-element.17), channel_id=1, replica_groups=mesh['x'=4,'yq'=4,'yp'=2,'z'=8,'core'=2] {'yp','x'}, dimensions={0} | all-to-all | bytes 524288 | tf_op jit(solution)/shard_map/all_to_all | solution.py:235
  194.5 1.6 shard_map.59
  196.1 11.3 %all_to_all.69 = f32[4,64,128]{2,1,0:T(8,128)S(1)} all-to-all(f32[4,64,128]{2,1,0:T(8,128)} %shard_map.59), channel_id=1, replica_groups=mesh['x'=4,'yq'=4,'yp'=2,'z'=8,'core'=2] {'yq'}, dimensions={0} | all-to-all | bytes 262144 | tf_op jit(solution)/shard_map/all_to_all | solution.py:243
  207.4 1.1 broadcast_in_dim.7
  208.5 3.6 %all-to-all-start.11 = ((f32[8,4,64,128]{3,2,1,0:T(8,128)}), f32[8,4,64,128]{3,2,1,0:T(8,128)S(1)}, u32[]{:S(2)}, u32[]{:S(2)}) async-start(f32[8,4,64,128]{3,2,1,0:T(8,128)} %broadcast_in_dim.7), calls=%async_computation.11 | async-start | bytes 2097152 | tf_op jit(solution)/shard_map/all_to_all | solution.py:188
  212.1 0.0 all-gather.9.cloned.1.call-done
  212.2 1.0 dynamic-slice_bitcast_fusion
  213.2 0.2 fusion
  213.4 0.2 copy.14
  213.6 0.9 broadcast_in_dim_reshape.3
  214.5 36.4 %all-gather.7.cloned.1.call-done.f_ref = f32[4,2,512,576]{3,2,1,0:T(8,128)} async-done(((f32[4,2,32,576]{3,2,1,0:T(8,128)}), f32[4,2,512,576]{3,2,1,0:T(8,128)}) %all-gather.7.cloned.1.call-update) | async-done | bytes 9437200 | tf_op jit(solution)/shard_map/all_gather | solution.py:224
  250.9 8.4 %shard_map.60.init_ref = f32[256,576]{1,0:T(8,128)} custom-call(f32[4,2,8,64,128]{4,3,2,1,0:T(8,128)} %bitcast.35, f32[4,2,512,576]{3,2,1,0:T(8,128)} %all-gather.7.cloned.1.call-done.f_ref), custom_call_target="tpu_custom_call" | custom-call | tf_op jit(solution)/shard_map/pallas_call | solution.py:177
  259.3 5.0 %shard_map.61.init_ref = f32[256,576]{1,0:T(8,128)} custom-call(f32[8,4,64,128]{3,2,1,0:T(8,128)} %all_to_all.67.refs_1_.x_ref, f32[4,2,512,576]{3,2,1,0:T(8,128)} %all-gather.7.cloned.1.call-done.f_ref, f32[256,576]{1,0:T(8,128)} %shard_map.60.init_ref), custom_call_target="tpu_custom_call" | custom-call | tf_op jit(solution)/shard_map/pallas_call | solution.py:177
  264.3 0.0 all-to-all-done.11.x_ref
  264.3 0.0 copy-start
  264.3 1.0 copy-done
  265.3 5.5 %shard_map.62 = f32[576,256]{1,0:T(8,128)} custom-call(f32[8,4,64,128]{3,2,1,0:T(8,128)} %copy-done, f32[4,2,512,576]{3,2,1,0:T(8,128)} %all-gather.7.cloned.1.call-done.f_ref, f32[256,576]{1,0:T(8,128)} %shard_map.61.init_ref, f32[704,256]{1,0:T(8,128)} %bitcast.33), custom_call_target="tpu_custom_call" | custom-call | tf_op jit(solution)/shard_map/pallas_call | solution.py:177
Async XLA Ops:
  7.2 84.6 %all-gather.5.cloned.1.call-start = ((), (), s32[]{:S(2)}) async-start(), calls=%async_computation.12 | async-start | bytes 5013504 | tf_op jit(solution)/shard_map/all_gather | solution.py:222
  81.5 10.3 %all-to-all-start.3 = ((f32[8,64,128]{2,1,0:T(8,128)}), f32[8,64,128]{2,1,0:T(8,128)S(1)}, u32[]{:S(2)}, u32[]{:S(2)}) async-start(f32[8,64,128]{2,1,0:T(8,128)} %shard_map.53), calls=%async_computation.3 | async-start | bytes 524288 | tf_op jit(solution)/shard_map/all_to_all | solution.py:240
  84.9 127.3 %all-gather.9.cloned.1.call-start = ((), (), s32[]{:S(2)}) async-start(), calls=%async_computation.14 | async-start | bytes 2621440 | tf_op jit(solution)/shard_map/all_gather | solution.py:264
  91.8 0.7 copy-start.2
  92.5 26.5 %copy-start.1 = (f32[1,704,4,64]{1,3,2,0:T(8,128)S(1)}, f32[1,704,4,64]{1,3,2,0:T(8,128)}, u32[]{:S(2)}) copy-start(f32[1,704,4,64]{1,3,2,0:T(8,128)} %param.3) | copy-start | bytes 2162692
  117.0 2.9 %copy-start.3 = (f32[8,64,128]{2,1,0:T(8,128)}, f32[8,64,128]{2,1,0:T(8,128)S(1)}, u32[]{:S(2)}) copy-start(f32[8,64,128]{2,1,0:T(8,128)S(1)} %all_to_all.64.refs_1_) | copy-start | bytes 786436
  118.9 132.0 %all-gather.7.cloned.1.call-start = ((), (), s32[]{:S(2)}) async-start(), calls=%async_computation.13 | async-start | bytes 11141120 | tf_op jit(solution)/shard_map/all_gather | solution.py:224
  208.5 55.8 %all-to-all-start.11 = ((f32[8,4,64,128]{3,2,1,0:T(8,128)}), f32[8,4,64,128]{3,2,1,0:T(8,128)S(1)}, u32[]{:S(2)}, u32[]{:S(2)}) async-start(f32[8,4,64,128]{3,2,1,0:T(8,128)} %broadcast_in_dim.7), calls=%async_computation.11 | async-start | bytes 2097152 | tf_op jit(solution)/shard_map/all_to_all | solution.py:188
  264.3 1.0 copy-start
Sparse Core Ops, SparseCore 0:
  32.0 55.9 all-gather.4
  119.0 57.1 all-gather.8
  178.3 72.5 all-gather.6

commit v3 on v2

v3 whole, which is shorter than its diff:
```python
import jax
import jax.numpy as jnp
from jax import lax
from jax.experimental import pallas as pl
from jax.experimental.pallas import tpu as pltpu
from jax.sharding import Mesh, PartitionSpec as P

QUADS = 4
DIRECT = ()
RHS = ("z", "core")
GROUP = ("yp", "x")
F32 = jnp.float32


def halves(value):
    high = value.astype(jnp.bfloat16)
    return high, (value - high.astype(F32)).astype(jnp.bfloat16)


def dot(a, b, dims):
    def one(u, v):
        return lax.dot_general(u, v, (dims, ((), ())), preferred_element_type=F32)

    ah, al = halves(a)
    bh, bl = halves(b)
    return one(ah, bh) + (one(ah, bl) + one(al, bh))


NN = ((1,), (0,))
NT = ((1,), (1,))


VMEM = pl.BlockSpec(memory_space=pltpu.VMEM)
SMEM = pl.BlockSpec(memory_space=pltpu.SMEM)
HBM = pl.BlockSpec(memory_space=pltpu.HBM)


def call(kernel, shapes, in_specs, scratch=(), limit=20 << 20):
    return pl.pallas_call(
        kernel,
        out_shape=[jax.ShapeDtypeStruct(s, F32) for s in shapes],
        in_specs=in_specs,
        out_specs=[VMEM] * len(shapes),
        scratch_shapes=scratch,
        compiler_params=pltpu.CompilerParams(vmem_limit_bytes=limit),
    )


def whole(shape):
    return pl.BlockSpec(shape, lambda i: (0,) * len(shape))


def pack(f_ref, inv_ref, r_ref, out_ref):
    quads, _, _ = out_ref.shape
    cols = f_ref.shape[1]
    per = r_ref.shape[1] // quads
    w = inv_ref.shape[1]
    turned = r_ref[...].T
    wide = jnp.concatenate([f_ref[0][:, w:], f_ref[2][:, 3 * w :]], axis=1)
    mid = f_ref[1][:, 2 * w :]
    mid = jnp.concatenate([mid[: cols // 2], mid[cols // 2 :]], axis=1)
    diag = jnp.concatenate([inv_ref[k].T for k in range(4)], axis=1)
    for q in range(quads):
        out_ref[q, :per] = turned[q * per : (q + 1) * per]
        out_ref[q, per : per + cols] = wide
        out_ref[q, per + cols : per + cols + cols // 2] = mid
        out_ref[q, per + cols + cols // 2 :] = diag


def sort(w, per, got_ref, heads_ref, pay_ref, first_ref):
    quads = got_ref.shape[0]
    half = pay_ref.shape[2]
    cols = 2 * half
    a, b, d = per, per + cols, per + cols + half

    def lanes(start, n, at):
        return jnp.concatenate(
            [got_ref[q, start : start + n][:, at : at + w] for q in range(quads)], axis=1
        )

    for k in range(4):
        heads_ref[k] = lanes(0, per, k * w)
    for h in range(2):
        for k in range(1, 4):
            pay_ref[k - 1, h] = lanes(d + h * half, half, k * w)
        for j in range(3):
            pay_ref[3 + j, h] = lanes(a + h * half, half, j * w)
        for j in range(2):
            pay_ref[6 + j, h] = lanes(b, half, h * 2 * w + j * w)
        pay_ref[8, h] = lanes(a + h * half, half, 3 * w)
        piece = lanes(d + h * half, half, 0)
        for c in range(first_ref.shape[0]):
            first_ref[c, h] = piece


def begin(head_ref, first_ref, out_ref):
    blocks, pair, half, rows = first_ref.shape
    head = head_ref[0]
    for p in range(pair):
        block = first_ref[:, p].reshape(blocks * half, rows)
        y = dot(head, block, NT)
        n = blocks * half // rows
        for x in range(n):
            out_ref[p * n + x] = y[:, x * rows : (x + 1) * rows]


def add_up(got_ref, out_ref):
    total = jnp.sum(got_ref[...], axis=0)
    for c in range(out_ref.shape[0]):
        out_ref[c] = total


def advance(at, diag_at, quad_ref, solved_ref, heads_ref, rest_ref, heads_out, y_out,
            lines_ref, diag_ref, sems):
    group, rows = y_out.shape[0], y_out.shape[2]
    left = lines_ref.shape[0]
    first = pltpu.make_async_copy(rest_ref.at[pl.ds(at, left)], lines_ref, sems.at[0])
    second = pltpu.make_async_copy(rest_ref.at[diag_at], diag_ref, sems.at[1])
    first.start()
    second.start()
    if len(solved_ref.shape) == 4:
        quad = quad_ref[0]
        x = jnp.concatenate([solved_ref[s, quad] for s in range(group)], axis=1)
    else:
        x = jnp.concatenate([solved_ref[s] for s in range(group)], axis=1)
    base = heads_ref.shape[0] - left
    first.wait()
    for b in range(left):
        heads_out[b] = heads_ref[base + b] - dot(x, lines_ref[b], NN)
    second.wait()
    y = dot(heads_out[0], diag_ref[...], NT)
    for s in range(group):
        y_out[s] = y[:, s * rows : (s + 1) * rows]


def stacked(x_refs):
    if len(x_refs) == 1:
        parts = [x_refs[0][s].reshape(-1, x_refs[0].shape[-1]) for s in range(2)]
    else:
        parts = [jnp.concatenate([x[0, s] for x in x_refs], axis=0) for s in range(2)]
    return jnp.concatenate(parts, axis=1)


def trail_sum(n, *refs):
    x_refs, f_ref, out_ref = refs[:n], refs[n], refs[-1]

    @pl.when(pl.program_id(0) == 0)
    def _():
        out_ref[...] = jnp.zeros_like(out_ref) if len(refs) == n + 2 else refs[n + 1][...]

    out_ref[...] += dot(stacked(x_refs), f_ref[0, 0], NN)


def trail_end(x_ref, f_ref, acc_ref, turn_ref, quad_ref, r_ref, out_ref, sum_ref):
    quads, per, _ = turn_ref.shape

    @pl.when(pl.program_id(0) == 0)
    def _():
        for q in range(quads):
            at = lax.rem(q + quads - quad_ref[0], quads)
            sum_ref[q * per : (q + 1) * per] = (
                acc_ref[q * per : (q + 1) * per] + turn_ref[at]
            )

    sum_ref[...] += dot(stacked([x_ref]), f_ref[0, 0], NN)

    @pl.when(pl.program_id(0) == pl.num_programs(0) - 1)
    def _():
        n = out_ref.shape[0]
        out_ref[...] = r_ref[r_ref.shape[0] - n :] - sum_ref[...].T


def trail_call(kernel, x, f, k, out_shape, extra=(), specs=(), steps=1, scratch=()):
    per_pair = f.shape[2] // 256
    per_panel = f.shape[1] * per_pair
    if len(x) == 1:
        x_specs = [pl.BlockSpec((2, *x[0].shape[1:]), lambda i: (i % per_panel, 0, 0, 0))]
    else:
        x_specs = [
            pl.BlockSpec((1, 2, *p.shape[2:]), lambda i: (i // per_panel, i % per_panel, 0, 0))
            for p in x
        ]
    f_spec = pl.BlockSpec(
        (1, 1, 256, f.shape[3]),
        lambda i: (k + i // per_panel, (i % per_panel) // per_pair, i % per_pair, 0),
    )
    return pl.pallas_call(
        kernel,
        out_shape=jax.ShapeDtypeStruct(out_shape, F32),
        grid=(steps * per_panel,),
        in_specs=[*x_specs, f_spec, *specs],
        out_specs=whole(out_shape),
        scratch_shapes=scratch,
        compiler_params=pltpu.CompilerParams(vmem_limit_bytes=56 << 20),
    )(*x, f, *extra)


def spread(array, axes):
    return lax.all_to_all(
        jnp.broadcast_to(array[None], (lax.axis_size(axes), *array.shape)), axes, 0, 0, tiled=True
    )


def body(factor, inverses, right_side):
    lower = jnp.transpose(factor[0], (1, 2, 0))
    inv = jnp.transpose(inverses[0], (0, 2, 1))
    current = right_side[0]
    panels, cols, _ = lower.shape
    width = inv.shape[1]
    count = current.shape[1]
    tail = panels * width
    quads = lax.axis_size("yq")
    nx, npair = lax.axis_size("x"), lax.axis_size("yp")
    blocks = lax.axis_size(RHS)
    group = nx * npair
    per = count // quads
    rows = quads * width
    half = cols // npair
    quad = lax.axis_index("yq")

    index = quad.reshape(1).astype(jnp.int32)
    corner = lower[:, :, :tail]
    (sent,) = call(
        pack, [(quads, per + 2 * cols + half, tail)], [VMEM, VMEM, VMEM]
    )(corner, inv, current[:tail])
    got = lax.all_to_all(sent, "yq", 0, 0, tiled=True)
    heads, pay, first = call(
        lambda *refs: sort(width, per, *refs),
        [(panels, per, rows), (9, npair, half, rows), (blocks, npair, half, rows)],
        [VMEM],
    )(got)
    first = lax.all_to_all(first, RHS, 0, 0, tiled=True)
    pay, first = lax.optimization_barrier((pay, first))
    rest = lax.all_gather(pay, RHS, axis=2, tiled=True)
    trail = lower[:, :, tail:].reshape(panels, npair, half, -1)
    trail = lax.all_gather(trail, RHS, axis=2, tiled=True)
    rest = rest.reshape(9, group * rows, rows)

    (y,) = call(begin, [(group, per, rows)], [VMEM, VMEM])(heads, first)
    block = (group, per, rows)
    acc_shape = (count, trail.shape[3])
    direct, own, late = [], {}, {}

    def add_trail(acc, k):
        more = () if acc is None else (acc,)
        return trail_call(
            lambda *refs: trail_sum(1, *refs), [late[k]], trail, k, acc_shape,
            more, (whole(acc_shape),) * len(more),
        )

    acc = None
    for k in range(panels):
        got = lax.all_to_all(y, GROUP, 0, 0, tiled=True)
        copies = group if k in DIRECT else quads
        (mine,) = call(add_up, [(copies, per, rows)], [VMEM])(got)
        if k in DIRECT:
            solved = lax.all_to_all(mine, GROUP, 0, 0, tiled=True)
            direct.append(solved)
        else:
            mine = lax.all_to_all(mine, "yq", 0, 0, tiled=True)
            if k == 3 and not DIRECT:
                acc = add_trail(acc, 1)
                mine, acc = lax.optimization_barrier((mine, acc))
            own[k] = mine
            solved = spread(mine, GROUP)
            if k == 2 and not DIRECT:
                acc = add_trail(acc, 0)
                solved, acc = lax.optimization_barrier((solved, acc))
            late[k] = solved
        if k == panels - 1:
            break
        left = panels - 1 - k
        at = {3: 3, 2: 6, 1: 8}[left]
        heads, y = call(
            lambda *refs, at=at, k=k: advance(at, k, *refs),
            [(left, per, rows), block],
            [SMEM, VMEM, VMEM, HBM],
            [
                pltpu.VMEM((left, group * rows, rows), F32),
                pltpu.VMEM((group * rows, rows), F32),
                pltpu.SemaphoreType.DMA((2,)),
            ],
            limit=63_000_000,
        )(index, solved, heads, rest)

    place = lax.axis_index("yp") * nx + lax.axis_index("x")
    turn = jnp.zeros((quads, per, trail.shape[3]), F32)
    if DIRECT:
        direct = jnp.stack(direct)
        parts = [direct] + [
            lax.ppermute(direct, "yq", [(i, (i - t) % quads) for i in range(quads)])
            for t in range(1, quads)
        ]
        turn = trail_call(
            lambda *refs: trail_sum(quads, *refs), parts, trail, DIRECT[0], acc_shape,
            steps=len(DIRECT),
        ).reshape(turn.shape)
        pieces = jnp.stack(
            [lax.dynamic_index_in_dim(p, place, 1, keepdims=False) for p in parts]
        )
        pieces = jnp.concatenate([pieces, pieces], axis=0)
        pieces = lax.dynamic_slice_in_dim(pieces, (quads - quad) % quads, quads, 0)
        for n, k in enumerate(DIRECT):
            own[k] = pieces[:, n]
    for k in (0,) if DIRECT else (2,):
        acc = add_trail(acc, k)
    out = trail_call(
        trail_end, [late[panels - 1]], trail, panels - 1, (trail.shape[3], count),
        (acc, turn, index, current),
        (whole(acc_shape), whole(turn.shape), SMEM, whole(current.shape)),
        scratch=[pltpu.VMEM(acc_shape, F32)],
    )
    pieces = jnp.stack([own[k] for k in range(panels)])
    pieces = lax.dynamic_slice_in_dim(pieces, quad * width, width, 3)
    mine = jnp.transpose(pieces, (0, 3, 1, 2)).reshape(tail, count)
    return (mine[None], out[None])


def solution(mesh):
    nx, ny, nz, nc = SIZES(mesh)
    fine = Mesh(
        mesh.devices.reshape(nx, QUADS, ny // QUADS, nz, nc), ("x", "yq", "yp", "z", "core")
    )
    row = ("x", "yq", "yp")
    in_specs = (P(row, None, None, RHS), P(row, None, RHS, None), P(row, None, RHS))
    out_specs = (P(row, None, RHS), P(row, None, RHS))
    return jax.shard_map(body, mesh=fine, in_specs=in_specs, out_specs=out_specs, check_vma=False)


def SIZES(mesh):
    nrow, nrhs = mesh.shape["row"], mesh.shape["rhs"]
    return nrow // 8, 8, nrhs // 2, 2
```

time: 279 us -> 250 us (0.90)
  the two profiles are of different devices: /device:TPU:1 before, /device:TPU:8 now
where the time goes in v3:
time: 250 us; the launch traced here: 248 us
  blocking collectives  141 us (56%)
  Pallas kernels  35 us (14%)
  waiting for transfers between devices  27.7 us (11%)
  starting transfers between devices  18.5 us (7%)
  between operations  14.1 us (6%)
  local copies, waits for them, and re-layouts  12.3 us (5%)
    all_to_all x4, blocking collectives, body(): got = lax.all_to_all(y, GROUP, 0, 0, tiled=True)  42.4 us
    all_to_all x3, blocking collectives, body(): mine = lax.all_to_all(mine, 'yq', 0, 0, tiled=True)  33.9 us
    all_to_all x1, blocking collectives, body(): first = lax.all_to_all(first, RHS, 0, 0, tiled=True)  26.1 us
    all_to_all x3, waiting for transfers between devices, spread(): lax.all_to_all(jnp.broadcast_to(array[None], (lax.axis_size(axes), *array...  23.4 us
    all_to_all x1, blocking collectives, body(): got = lax.all_to_all(sent, 'yq', 0, 0, tiled=True)  21.8 us
    pallas_call x4, Pallas kernels, trail_call(): pl.pallas_call(kernel, out_shape=jax.ShapeDtypeStruct(out_shape, F32), gr...  20.6 us
    all_to_all x1, blocking collectives, spread(): lax.all_to_all(jnp.broadcast_to(array[None], (lax.axis_size(axes), *array...  16.4 us
    all_to_all x3, starting transfers between devices, spread(): lax.all_to_all(jnp.broadcast_to(array[None], (lax.axis_size(axes), *array...  15.1 us
  transfers between devices with their start and end apart: 6, of which 4 were waited for; matrix products, arithmetic and copies ran while one was open for 2% of the time, Pallas kernels for 10%

profile of v3, /device:TPU:8, one launch (start us, length us, event | category | flops | bytes accessed | tf_op | source)
XLA Modules:
  0.0 248.5 jit_solution(14375947063189477056)
XLA Ops:
  7.2 0.0 all-gather.3.cloned.1.call-start
  7.2 0.9 slice.16.f_ref
  8.1 0.9 slice_bitcast_fusion.r_ref
  9.0 0.0 copy-start.1
  9.1 0.8 copy-done.1
  9.9 0.2 shard_map.50
  10.1 21.8 %all_to_all.70.refs_0_ = f32[4,224,128]{2,1,0:T(8,128)S(1)} all-to-all(f32[4,224,128]{2,1,0:T(8,128)S(1)} %shard_map.50), channel_id=1, replica_groups=mesh['x'=4,'yq'=4,'yp'=2,'z'=8,'core'=2] {'yq'}, dimensions={0} | all-to-all | bytes 917504 | tf_op jit(solution)/shard_map/all_to_all | solution.py:226
  31.9 1.1 shard_map.51
  33.0 0.0 copy-start
  33.0 26.1 %all_to_all.71.first_ref = f32[16,2,32,128]{3,2,1,0:T(8,128)S(1)} all-to-all(f32[16,2,32,128]{3,2,1,0:T(8,128)S(1)} %get-tuple-element.18), channel_id=1, replica_groups=mesh['x'=4,'yq'=4,'yp'=2,'z'=8,'core'=2] {'z','core'}, dimensions={0} | all-to-all | bytes 1048576 | tf_op jit(solution)/shard_map/all_to_all | solution.py:232
  59.2 0.0 all-gather.3.cloned.1.call-update
  59.2 0.0 all-gather.5.cloned.1.call-start
  59.3 2.0 slice.17
  61.2 0.0 all-gather.5.cloned.1.call-update
  61.3 0.4 shard_map.52
  61.7 11.7 %all_to_all.72.got_ref = f32[8,64,128]{2,1,0:T(8,128)S(1)} all-to-all(f32[8,64,128]{2,1,0:T(8,128)S(1)} %shard_map.52), channel_id=1, replica_groups=mesh['x'=4,'yq'=4,'yp'=2,'z'=8,'core'=2] {'yp','x'}, dimensions={0} | all-to-all | bytes 524288 | tf_op jit(solution)/shard_map/all_to_all | solution.py:253
  73.4 11.3 %all_to_all.73 = f32[4,64,128]{2,1,0:T(8,128)S(1)} all-to-all(f32[4,64,128]{2,1,0:T(8,128)S(1)} %shard_map.53), channel_id=1, replica_groups=mesh['x'=4,'yq'=4,'yp'=2,'z'=8,'core'=2] {'yq'}, dimensions={0} | all-to-all | bytes 262144 | tf_op jit(solution)/shard_map/all_to_all | solution.py:260
  84.6 1.1 broadcast_in_dim.12
  85.7 5.2 %all-to-all-start.4 = ((f32[8,4,64,128]{3,2,1,0:T(8,128)}), f32[8,4,64,128]{3,2,1,0:T(8,128)S(1)}, u32[]{:S(2)}, u32[]{:S(2)}) async-start(f32[8,4,64,128]{3,2,1,0:T(8,128)} %broadcast_in_dim.12), calls=%async_computation.4 | async-start | bytes 2097152 | tf_op jit(solution)/shard_map/all_to_all | solution.py:199
  91.0 14.4 %all-to-all-done.4.refs_1_.refs_0_ = f32[8,4,64,128]{3,2,1,0:T(8,128)S(1)} async-done(((f32[8,4,64,128]{3,2,1,0:T(8,128)}), f32[8,4,64,128]{3,2,1,0:T(8,128)S(1)}, u32[]{:S(2)}, u32[]{:S(2)}) %all-to-all-start.4) | async-done | bytes 1048608 | tf_op jit(solution)/shard_map/all_to_all | solution.py:199
  105.4 0.0 copy-start.3
  105.4 0.0 all-gather.3.cloned.1.call-done
  105.4 0.0 copy-done
  105.4 1.0 copy-done.3
  106.4 4.3 %shard_map.54 = (f32[3,64,128]{2,1,0:T(8,128)}, f32[8,64,128]{2,1,0:T(8,128)}) custom-call(s32[1]{0:T(128)} %bitcast.6.refs_0_.quad_ref, f32[8,4,64,128]{3,2,1,0:T(8,128)} %copy-done.3, f32[4,64,128]{2,1,0:T(8,128)} %copy-done, f32[9,1024,128]{2,1,0:T(8,128)} %bitcast.20), custom_call_target="tpu_custom_call" | custom-call | tf_op jit(solution)/shard_map/pallas_call | solution.py:274
  110.7 10.1 %all_to_all.74.got_ref = f32[8,64,128]{2,1,0:T(8,128)S(1)} all-to-all(f32[8,64,128]{2,1,0:T(8,128)} %get-tuple-element.21), channel_id=1, replica_groups=mesh['x'=4,'yq'=4,'yp'=2,'z'=8,'core'=2] {'yp','x'}, dimensions={0} | all-to-all | bytes 524288 | tf_op jit(solution)/shard_map/all_to_all | solution.py:253
  120.8 10.9 %all_to_all.75 = f32[4,64,128]{2,1,0:T(8,128)S(1)} all-to-all(f32[4,64,128]{2,1,0:T(8,128)S(1)} %shard_map.55), channel_id=1, replica_groups=mesh['x'=4,'yq'=4,'yp'=2,'z'=8,'core'=2] {'yq'}, dimensions={0} | all-to-all | bytes 262144 | tf_op jit(solution)/shard_map/all_to_all | solution.py:260
  131.7 0.1 broadcast_in_dim.13
  131.8 16.4 %all_to_all.76.refs_1_.refs_0_ = f32[8,4,64,128]{3,2,1,0:T(8,128)} all-to-all(f32[8,4,64,128]{3,2,1,0:T(8,128)S(1)} %broadcast_in_dim.13), channel_id=1, replica_groups=mesh['x'=4,'yq'=4,'yp'=2,'z'=8,'core'=2] {'yp','x'}, dimensions={0} | all-to-all | bytes 2097152 | tf_op jit(solution)/shard_map/all_to_all | solution.py:199
  148.2 4.0 %shard_map.56 = (f32[2,64,128]{2,1,0:T(8,128)}, f32[8,64,128]{2,1,0:T(8,128)}) custom-call(s32[1]{0:T(128)} %bitcast.6.refs_0_.quad_ref, f32[8,4,64,128]{3,2,1,0:T(8,128)} %all_to_all.76.refs_1_.refs_0_, f32[3,64,128]{2,1,0:T(8,128)} %get-tuple-element.22.refs_2_, f32[9,1024,128]{2,1,0:T(8,128)} %bitcast.21), custom_call_target="tpu_custom_call" | custom-call | tf_op jit(solution)/shard_map/pallas_call | solution.py:274
  152.2 10.6 %all_to_all.77.got_ref = f32[8,64,128]{2,1,0:T(8,128)S(1)} all-to-all(f32[8,64,128]{2,1,0:T(8,128)} %get-tuple-element.23), channel_id=1, replica_groups=mesh['x'=4,'yq'=4,'yp'=2,'z'=8,'core'=2] {'yp','x'}, dimensions={0} | all-to-all | bytes 524288 | tf_op jit(solution)/shard_map/all_to_all | solution.py:253
  162.9 11.8 %all_to_all.78 = f32[4,64,128]{2,1,0:T(8,128)S(1)} all-to-all(f32[4,64,128]{2,1,0:T(8,128)S(1)} %shard_map.57), channel_id=1, replica_groups=mesh['x'=4,'yq'=4,'yp'=2,'z'=8,'core'=2] {'yq'}, dimensions={0} | all-to-all | bytes 262144 | tf_op jit(solution)/shard_map/all_to_all | solution.py:260
  174.6 1.1 broadcast_in_dim.14
  175.7 4.5 %all-to-all-start.10 = ((f32[8,4,64,128]{3,2,1,0:T(8,128)}), f32[8,4,64,128]{3,2,1,0:T(8,128)S(1)}, u32[]{:S(2)}, u32[]{:S(2)}) async-start(f32[8,4,64,128]{3,2,1,0:T(8,128)} %broadcast_in_dim.14), calls=%async_computation.10 | async-start | bytes 2097152 | tf_op jit(solution)/shard_map/all_to_all | solution.py:199
  180.3 0.0 all-gather.5.cloned.1.call-done.refs_1_.f_ref
  180.3 4.8 %shard_map.58.refs_2_ = f32[256,576]{1,0:T(8,128)} custom-call(f32[8,4,64,128]{3,2,1,0:T(8,128)} %copy-done.3, f32[4,2,512,576]{3,2,1,0:T(8,128)} %all-gather.5.cloned.1.call-done.refs_1_.f_ref), custom_call_target="tpu_custom_call" | custom-call | tf_op jit(solution)/shard_map/pallas_call | solution.py:187
  185.1 5.2 %all-to-all-done.10.refs_1_.refs_0_ = f32[8,4,64,128]{3,2,1,0:T(8,128)S(1)} async-done(((f32[8,4,64,128]{3,2,1,0:T(8,128)}), f32[8,4,64,128]{3,2,1,0:T(8,128)S(1)}, u32[]{:S(2)}, u32[]{:S(2)}) %all-to-all-start.10) | async-done | bytes 1048608 | tf_op jit(solution)/shard_map/all_to_all | solution.py:199
  190.3 0.0 copy-start.2
  190.3 1.0 copy-done.2
  191.3 3.6 %shard_map.59 = (f32[1,64,128]{2,1,0:T(8,128)}, f32[8,64,128]{2,1,0:T(8,128)}) custom-call(s32[1]{0:T(128)} %bitcast.6.refs_0_.quad_ref, f32[8,4,64,128]{3,2,1,0:T(8,128)} %copy-done.2, f32[2,64,128]{2,1,0:T(8,128)} %get-tuple-element.25.refs_2_, f32[9,1024,128]{2,1,0:T(8,128)} %bitcast.22), custom_call_target="tpu_custom_call" | custom-call | tf_op jit(solution)/shard_map/pallas_call | solution.py:274
  194.9 10.0 %all_to_all.79.got_ref = f32[8,64,128]{2,1,0:T(8,128)S(1)} all-to-all(f32[8,64,128]{2,1,0:T(8,128)} %get-tuple-element.26), channel_id=1, replica_groups=mesh['x'=4,'yq'=4,'yp'=2,'z'=8,'core'=2] {'yp','x'}, dimensions={0} | all-to-all | bytes 524288 | tf_op jit(solution)/shard_map/all_to_all | solution.py:253
  204.9 0.7 shard_map.60
  205.6 3.3 %all-to-all-start.12 = ((f32[4,64,128]{2,1,0:T(8,128)}), f32[4,64,128]{2,1,0:T(8,128)S(1)}, u32[]{:S(2)}, u32[]{:S(2)}) async-start(f32[4,64,128]{2,1,0:T(8,128)} %shard_map.60), calls=%async_computation.12 | async-start | bytes 262144 | tf_op jit(solution)/shard_map/all_to_all | solution.py:260
  208.9 5.1 %shard_map.61.refs_2_ = f32[256,576]{1,0:T(8,128)} custom-call(f32[8,4,64,128]{3,2,1,0:T(8,128)} %all_to_all.76.refs_1_.refs_0_, f32[4,2,512,576]{3,2,1,0:T(8,128)} %all-gather.5.cloned.1.call-done.refs_1_.f_ref, f32[256,576]{1,0:T(8,128)} %shard_map.58.refs_2_), custom_call_target="tpu_custom_call" | custom-call | tf_op jit(solution)/shard_map/pallas_call | solution.py:187
  214.0 4.3 %all-to-all-done.12 = f32[4,64,128]{2,1,0:T(8,128)S(1)} async-done(((f32[4,64,128]{2,1,0:T(8,128)}), f32[4,64,128]{2,1,0:T(8,128)S(1)}, u32[]{:S(2)}, u32[]{:S(2)}) %all-to-all-start.12) | async-done | bytes 131104 | tf_op jit(solution)/shard_map/all_to_all | solution.py:260
  218.3 1.1 broadcast_in_dim.15
  219.4 5.3 %all-to-all-start.13 = ((f32[8,4,64,128]{3,2,1,0:T(8,128)}), f32[8,4,64,128]{3,2,1,0:T(8,128)S(1)}, u32[]{:S(2)}, u32[]{:S(2)}) async-start(f32[8,4,64,128]{3,2,1,0:T(8,128)} %broadcast_in_dim.15), calls=%async_computation.13 | async-start | bytes 2097152 | tf_op jit(solution)/shard_map/all_to_all | solution.py:199
  224.7 0.2 fusion
  224.9 0.2 copy.5
  225.1 0.9 broadcast_in_dim_reshape.3
  226.0 5.0 %shard_map.62.acc_ref = f32[256,576]{1,0:T(8,128)} custom-call(f32[8,4,64,128]{3,2,1,0:T(8,128)} %copy-done.2, f32[4,2,512,576]{3,2,1,0:T(8,128)} %all-gather.5.cloned.1.call-done.refs_1_.f_ref, f32[256,576]{1,0:T(8,128)} %shard_map.61.refs_2_), custom_call_target="tpu_custom_call" | custom-call | tf_op jit(solution)/shard_map/pallas_call | solution.py:187
  231.0 3.7 %all-to-all-done.13.x_ref = f32[8,4,64,128]{3,2,1,0:T(8,128)S(1)} async-done(((f32[8,4,64,128]{3,2,1,0:T(8,128)}), f32[8,4,64,128]{3,2,1,0:T(8,128)S(1)}, u32[]{:S(2)}, u32[]{:S(2)}) %all-to-all-start.13) | async-done | bytes 1048608 | tf_op jit(solution)/shard_map/all_to_all | solution.py:199
  234.7 0.0 copy-start.4
  234.7 1.0 broadcast_in_dim.16.turn_ref
  235.7 0.3 copy-done.4
  236.0 5.7 %shard_map.63 = f32[576,256]{1,0:T(8,128)} custom-call(f32[8,4,64,128]{3,2,1,0:T(8,128)} %copy-done.4, f32[4,2,512,576]{3,2,1,0:T(8,128)} %all-gather.5.cloned.1.call-done.refs_1_.f_ref, f32[256,576]{1,0:T(8,128)} %shard_map.62.acc_ref, f32[4,64,576]{2,1,0:T(8,128)} %broadcast_in_dim.16.turn_ref, s32[1]{0:T(128)} %bitcast.6.refs_0_.quad_ref, f32[704,256]{1,0:T(8,128)} %bitcast.28), custom_call_target="tpu_custom_call" | custom-call | tf_op jit(solution)/shard_map/pallas_call | solution.py:187
  (3 shorter events, 0.1 us)
Async XLA Ops:
  7.2 98.2 %all-gather.3.cloned.1.call-start = ((), (), s32[]{:S(2)}) async-start(), calls=%async_computation.14 | async-start | bytes 5013504 | tf_op jit(solution)/shard_map/all_gather | solution.py:234
  9.0 0.8 copy-start.1
  33.0 72.4 %copy-start = (f32[4,64,128]{2,1,0:T(8,128)}, f32[4,64,128]{2,1,0:T(8,128)S(1)}, u32[]{:S(2)}) copy-start(f32[4,64,128]{2,1,0:T(8,128)S(1)} %get-tuple-element.16.head_ref.refs_2_) | copy-start | bytes 393220
  59.2 121.0 %all-gather.5.cloned.1.call-start = ((), (), s32[]{:S(2)}) async-start(), calls=%async_computation.15 | async-start | bytes 11141120 | tf_op jit(solution)/shard_map/all_gather | solution.py:236
  85.7 19.7 %all-to-all-start.4 = ((f32[8,4,64,128]{3,2,1,0:T(8,128)}), f32[8,4,64,128]{3,2,1,0:T(8,128)S(1)}, u32[]{:S(2)}, u32[]{:S(2)}) async-start(f32[8,4,64,128]{3,2,1,0:T(8,128)} %broadcast_in_dim.12), calls=%async_computation.4 | async-start | bytes 2097152 | tf_op jit(solution)/shard_map/all_to_all | solution.py:199
  105.4 1.0 copy-start.3
  175.7 14.6 %all-to-all-start.10 = ((f32[8,4,64,128]{3,2,1,0:T(8,128)}), f32[8,4,64,128]{3,2,1,0:T(8,128)S(1)}, u32[]{:S(2)}, u32[]{:S(2)}) async-start(f32[8,4,64,128]{3,2,1,0:T(8,128)} %broadcast_in_dim.14), calls=%async_computation.10 | async-start | bytes 2097152 | tf_op jit(solution)/shard_map/all_to_all | solution.py:199
  190.3 1.0 copy-start.2
  205.6 12.7 %all-to-all-start.12 = ((f32[4,64,128]{2,1,0:T(8,128)}), f32[4,64,128]{2,1,0:T(8,128)S(1)}, u32[]{:S(2)}, u32[]{:S(2)}) async-start(f32[4,64,128]{2,1,0:T(8,128)} %shard_map.60), calls=%async_computation.12 | async-start | bytes 262144 | tf_op jit(solution)/shard_map/all_to_all | solution.py:260
  219.4 15.4 %all-to-all-start.13 = ((f32[8,4,64,128]{3,2,1,0:T(8,128)}), f32[8,4,64,128]{3,2,1,0:T(8,128)S(1)}, u32[]{:S(2)}, u32[]{:S(2)}) async-start(f32[8,4,64,128]{3,2,1,0:T(8,128)} %broadcast_in_dim.15), calls=%async_computation.13 | async-start | bytes 2097152 | tf_op jit(solution)/shard_map/all_to_all | solution.py:199
  234.7 1.2 copy-start.4
Sparse Core Ops, SparseCore 0:
  59.3 39.7 all-gather.2
  101.3 67.5 all-gather.4

commit v4 on v3

v4 whole, which is shorter than its diff:
```python
import jax
import jax.numpy as jnp
from jax import lax
from jax.experimental import pallas as pl
from jax.experimental.pallas import tpu as pltpu
from jax.sharding import Mesh, PartitionSpec as P

QUADS = 4
RHS = ("z", "core")
GROUP = ("yp", "x")
F32 = jnp.float32


def halves(value):
    high = value.astype(jnp.bfloat16)
    return high, (value - high.astype(F32)).astype(jnp.bfloat16)


def dot(a, b, dims):
    def one(u, v):
        return lax.dot_general(u, v, (dims, ((), ())), preferred_element_type=F32)

    ah, al = halves(a)
    bh, bl = halves(b)
    return one(ah, bh) + (one(ah, bl) + one(al, bh))


NN = ((1,), (0,))
NT = ((1,), (1,))


VMEM = pl.BlockSpec(memory_space=pltpu.VMEM)
SMEM = pl.BlockSpec(memory_space=pltpu.SMEM)
HBM = pl.BlockSpec(memory_space=pltpu.HBM)


def call(kernel, shapes, in_specs, scratch=()):
    return pl.pallas_call(
        kernel,
        out_shape=[jax.ShapeDtypeStruct(s, F32) for s in shapes],
        in_specs=in_specs,
        out_specs=[VMEM] * len(shapes),
        scratch_shapes=scratch,
        compiler_params=pltpu.CompilerParams(vmem_limit_bytes=20 << 20),
    )


def in_hbm(array):
    return pltpu.with_memory_space_constraint(array, pltpu.HBM)


def whole(shape):
    return pl.BlockSpec(shape, lambda i: (0,) * len(shape))


def pack(f_hbm, inv_hbm, r_hbm, out_ref, f_ref, inv_ref, r_ref, sems):
    quads, _, lanes = out_ref.shape
    copies = [
        pltpu.make_async_copy(f_hbm.at[:, :, pl.ds(0, lanes)], f_ref, sems.at[0]),
        pltpu.make_async_copy(inv_hbm, inv_ref, sems.at[1]),
        pltpu.make_async_copy(r_hbm.at[pl.ds(0, lanes)], r_ref, sems.at[2]),
    ]
    for c in copies:
        c.start()
    for c in copies:
        c.wait()
    cols = f_ref.shape[1]
    per = r_ref.shape[1] // quads
    w = inv_ref.shape[1]
    turned = r_ref[...].T
    wide = jnp.concatenate([f_ref[0][:, w:], f_ref[2][:, 3 * w :]], axis=1)
    mid = f_ref[1][:, 2 * w :]
    mid = jnp.concatenate([mid[: cols // 2], mid[cols // 2 :]], axis=1)
    diag = jnp.concatenate([inv_ref[k].T for k in range(4)], axis=1)
    for q in range(quads):
        out_ref[q, :per] = turned[q * per : (q + 1) * per]
        out_ref[q, per : per + cols] = wide
        out_ref[q, per + cols : per + cols + cols // 2] = mid
        out_ref[q, per + cols + cols // 2 :] = diag


def sort(w, per, got_ref, heads_ref, pay_ref, first_ref):
    quads = got_ref.shape[0]
    half = pay_ref.shape[2]
    cols = 2 * half
    a, b, d = per, per + cols, per + cols + half

    def lanes(start, n, at):
        return jnp.concatenate(
            [got_ref[q, start : start + n][:, at : at + w] for q in range(quads)], axis=1
        )

    for k in range(4):
        heads_ref[k] = lanes(0, per, k * w)
    for h in range(2):
        for k in range(1, 4):
            pay_ref[k - 1, h] = lanes(d + h * half, half, k * w)
        for j in range(3):
            pay_ref[3 + j, h] = lanes(a + h * half, half, j * w)
        for j in range(2):
            pay_ref[6 + j, h] = lanes(b, half, h * 2 * w + j * w)
        pay_ref[8, h] = lanes(a + h * half, half, 3 * w)
        piece = lanes(d + h * half, half, 0)
        for c in range(first_ref.shape[0]):
            first_ref[c, h] = piece


def begin(head_ref, first_ref, out_ref):
    blocks, pair, half, rows = first_ref.shape
    head = head_ref[0]
    for p in range(pair):
        block = first_ref[:, p].reshape(blocks * half, rows)
        y = dot(head, block, NT)
        n = blocks * half // rows
        for x in range(n):
            out_ref[p * n + x] = y[:, x * rows : (x + 1) * rows]


def add_up(got_ref, out_ref):
    total = jnp.sum(got_ref[...], axis=0)
    for c in range(out_ref.shape[0]):
        out_ref[c] = total


def advance(base, at, diag_at, quad_ref, solved_ref, head_ref, rest_hbm, y_out, line_ref, diag_ref, sems):
    group, rows = y_out.shape[0], y_out.shape[2]
    first = pltpu.make_async_copy(rest_hbm.at[at], line_ref, sems.at[0])
    second = pltpu.make_async_copy(rest_hbm.at[diag_at], diag_ref, sems.at[1])
    first.start()
    second.start()
    x = chosen(quad_ref, solved_ref)
    first.wait()
    head = head_ref[base] - dot(x, line_ref[...], NN)
    second.wait()
    y = dot(head, diag_ref[...], NT)
    for s in range(group):
        y_out[s] = y[:, s * rows : (s + 1) * rows]


def chosen(quad_ref, solved_ref):
    quad = quad_ref[0]
    return jnp.concatenate([solved_ref[s, quad] for s in range(solved_ref.shape[0])], axis=1)


def follow(base, at, quad_ref, solved_ref, heads_ref, rest_hbm, heads_out, lines_ref, sem):
    left = heads_out.shape[0]
    copy = pltpu.make_async_copy(rest_hbm.at[pl.ds(at, left)], lines_ref, sem)
    copy.start()
    x = chosen(quad_ref, solved_ref)
    copy.wait()
    for b in range(left):
        heads_out[b] = heads_ref[base + b + 1] - dot(x, lines_ref[b], NN)


def stacked(x_refs):
    if len(x_refs) == 1:
        parts = [x_refs[0][s].reshape(-1, x_refs[0].shape[-1]) for s in range(2)]
    else:
        parts = [jnp.concatenate([x[0, s] for x in x_refs], axis=0) for s in range(2)]
    return jnp.concatenate(parts, axis=1)


def trail_sum(n, *refs):
    x_refs, f_ref, init_ref, out_ref = refs[:n], refs[n], refs[n + 1], refs[-1]

    @pl.when(pl.program_id(0) == 0)
    def _():
        if init_ref.shape == out_ref.shape:
            out_ref[...] = init_ref[...]
        else:
            out_ref[...] = init_ref[init_ref.shape[0] - out_ref.shape[1] :].T

    out_ref[...] -= dot(stacked(x_refs), f_ref[0, 0], NN)


def finish(panel, x_ref, f_hbm, base_ref, quad_ref, *refs):
    own_refs, (out_ref, mine_ref, turned_ref, f_ref, sems) = refs[:-5], refs[-5:]
    n = f_ref.shape[0]
    copies = [
        pltpu.make_async_copy(f_hbm.at[panel, b], f_ref.at[b], sems.at[b]) for b in range(n)
    ]
    for c in copies:
        c.start()
    width = mine_ref.shape[0] // len(own_refs)
    at = pl.multiple_of(quad_ref[0] * width, width)
    for k, own_ref in enumerate(own_refs):
        turned_ref[...] = own_ref[...].reshape(-1, own_ref.shape[2]).T
        mine_ref[k * width : (k + 1) * width] = turned_ref[pl.ds(at, width)]
    total = base_ref[...]
    for b, c in enumerate(copies):
        c.wait()
        total -= dot(stacked([x_ref.at[pl.ds(2 * b, 2)]]), f_ref[b], NN)
    out_ref[...] = total.T


def trail_call(kernel, x, f, k, out_shape, extra=(), specs=(), steps=1, scratch=()):
    per_pair = f.shape[2] // 256
    per_panel = f.shape[1] * per_pair
    if len(x) == 1:
        x_specs = [pl.BlockSpec((2, *x[0].shape[1:]), lambda i: (i % per_panel, 0, 0, 0))]
    else:
        x_specs = [
            pl.BlockSpec((1, 2, *p.shape[2:]), lambda i: (i // per_panel, i % per_panel, 0, 0))
            for p in x
        ]
    f_spec = pl.BlockSpec(
        (1, 1, 256, f.shape[3]),
        lambda i: (k + i // per_panel, (i % per_panel) // per_pair, i % per_pair, 0),
    )
    return pl.pallas_call(
        kernel,
        out_shape=jax.ShapeDtypeStruct(out_shape, F32),
        grid=(steps * per_panel,),
        in_specs=[*x_specs, f_spec, *specs],
        out_specs=whole(out_shape),
        scratch_shapes=scratch,
        compiler_params=pltpu.CompilerParams(vmem_limit_bytes=16 << 20),
    )(*x, in_hbm(f), *extra)


def spread(array, axes):
    return lax.all_to_all(
        jnp.broadcast_to(array[None], (lax.axis_size(axes), *array.shape)), axes, 0, 0, tiled=True
    )


def body(factor, inverses, right_side):
    lower = jnp.transpose(factor[0], (1, 2, 0))
    inv = jnp.transpose(inverses[0], (0, 2, 1))
    current = right_side[0]
    panels, cols, _ = lower.shape
    width = inv.shape[1]
    count = current.shape[1]
    tail = panels * width
    quads = lax.axis_size("yq")
    nx, npair = lax.axis_size("x"), lax.axis_size("yp")
    blocks = lax.axis_size(RHS)
    group = nx * npair
    per = count // quads
    rows = quads * width
    half = cols // npair
    quad = lax.axis_index("yq")

    index = quad.reshape(1).astype(jnp.int32)
    (sent,) = call(
        pack,
        [(quads, per + 2 * cols + half, tail)],
        [HBM, HBM, HBM],
        [
            pltpu.VMEM((panels, cols, tail), F32),
            pltpu.VMEM(inv.shape, F32),
            pltpu.VMEM((tail, count), F32),
            pltpu.SemaphoreType.DMA((3,)),
        ],
    )(in_hbm(lower), in_hbm(inv), in_hbm(current))
    got = lax.all_to_all(sent, "yq", 0, 0, tiled=True)
    heads, pay, first = call(
        lambda *refs: sort(width, per, *refs),
        [(panels, per, rows), (9, npair, half, rows), (blocks, npair, half, rows)],
        [VMEM],
    )(got)
    first = lax.all_to_all(first, RHS, 0, 0, tiled=True)
    pay, first = lax.optimization_barrier((pay, first))
    rest = lax.all_gather(pay, RHS, axis=2, tiled=True)
    rest = rest.reshape(9, group * rows, rows)

    (y,) = call(begin, [(group, per, rows)], [VMEM, VMEM])(heads, first)
    length = lower.shape[2] - tail
    own, late = {}, {}
    trail = base = None
    for k in range(panels):
        got = lax.all_to_all(y, GROUP, 0, 0, tiled=True)
        if k == 3:
            base = add_trail(late[1], trail, 1, base)
            got, base = lax.optimization_barrier((got, base))
        (mine,) = call(add_up, [(quads, per, rows)], [VMEM])(got)
        if k == 0:
            lower, mine = lax.optimization_barrier((lower, mine))
            trail = lower[:, :, tail:].reshape(panels, npair, half, -1)
            trail = lax.all_gather(trail, RHS, axis=2, tiled=True)
        mine = lax.all_to_all(mine, "yq", 0, 0, tiled=True)
        if k == 3:
            base = add_trail(late[2], trail, 2, base)
            mine, base = lax.optimization_barrier((mine, base))
        own[k] = mine
        solved = spread(mine, GROUP)
        if k == 2:
            base = add_trail(late[0], trail, 0, current)
            solved, base = lax.optimization_barrier((solved, base))
        late[k] = solved
        if k == panels - 1:
            break
        left = panels - 1 - k
        at = {3: 3, 2: 6, 1: 8}[left]
        one = pltpu.VMEM((group * rows, rows), F32)
        (y,) = call(
            lambda *refs, at=at, k=k: advance(int(k == 0), at, k, *refs),
            [(group, per, rows)],
            [SMEM, VMEM, VMEM, HBM],
            [one, one, pltpu.SemaphoreType.DMA((2,))],
        )(index, solved, heads, in_hbm(rest))
        if left > 1:
            (heads,) = call(
                lambda *refs, at=at, k=k: follow(int(k == 0), at + 1, *refs),
                [(left - 1, per, rows)],
                [SMEM, VMEM, VMEM, HBM],
                [
                    pltpu.VMEM((left - 1, group * rows, rows), F32),
                    pltpu.SemaphoreType.DMA,
                ],
            )(index, solved, heads, in_hbm(rest))

    flat = trail.reshape(panels, -1, 2 * rows, length)
    out, mine = call(
        lambda *refs: finish(panels - 1, *refs),
        [(length, count), (tail, count)],
        [VMEM, HBM, VMEM, SMEM] + [VMEM] * panels,
        [
            pltpu.VMEM((rows, count), F32),
            pltpu.VMEM(flat.shape[1:], F32),
            pltpu.SemaphoreType.DMA((flat.shape[1],)),
        ],
    )(late[3], in_hbm(flat), base, index, *[own[k] for k in range(panels)])
    return (mine[None], out[None])


def add_trail(x, trail, k, init):
    shape = (x.shape[1] * x.shape[2], trail.shape[3])
    return trail_call(
        lambda *refs: trail_sum(1, *refs), [x], trail, k, shape, (init,), (whole(init.shape),)
    )


def solution(mesh):
    nx, ny, nz, nc = SIZES(mesh)
    fine = Mesh(
        mesh.devices.reshape(nx, QUADS, ny // QUADS, nz, nc), ("x", "yq", "yp", "z", "core")
    )
    row = ("x", "yq", "yp")
    in_specs = (P(row, None, None, RHS), P(row, None, RHS, None), P(row, None, RHS))
    out_specs = (P(row, None, RHS), P(row, None, RHS))
    return jax.shard_map(body, mesh=fine, in_specs=in_specs, out_specs=out_specs, check_vma=False)


def SIZES(mesh):
    nrow, nrhs = mesh.shape["row"], mesh.shape["rhs"]
    return nrow // 8, 8, nrhs // 2, 2
```

time: 250 us -> 240 us (0.960)
  blocking collectives: 141 us -> 131 us
  Pallas kernels: 35 us -> 28.1 us
  starting transfers between devices: 18.5 us -> 22 us
  waiting for transfers between devices: 27.7 us -> 30.9 us
    all_to_all x4 -> x3, blocking collectives: 42.4 us -> 31.4 us  [body(): got = lax.all_to_all(y, GROUP, 0, 0, tiled=True)]
    pallas_call x4 -> x3, Pallas kernels: 20.6 us -> 11.7 us  [trail_call(): pl.pallas_call(kernel, out_shape=jax.ShapeDtypeStruct(out_shape, F32), gr...]
    all_to_all x0 -> x1, starting transfers between devices: none -> 4.17 us  [body(): got = lax.all_to_all(y, GROUP, 0, 0, tiled=True)]
    unnamed x10 -> x18, local copies, waits for them, and re-layouts: 3.08 us -> 7.17 us
    all_to_all x3, waiting for transfers between devices: 23.4 us -> 27.3 us  [spread(): lax.all_to_all(jnp.broadcast_to(array[None], (lax.axis_size(axes), *array...]
    pallas_call x8 -> x11, Pallas kernels: 12.8 us -> 14.9 us  [the longest x3 5.86 us: body(): call(lambda *refs, at=at, k=k: advance(int(k == 0), at, k, *refs), [(grou...]
  transfers between devices with their start and end apart: 6 -> 7, of which waited for: 4 -> 4; matrix products, arithmetic and copies ran while one was open for 2% -> 2% of each run, Pallas kernels for 10% -> 8%
where the time goes in v4:
time: 240 us; the launch traced here: 239 us
  blocking collectives  131 us (55%)
  waiting for transfers between devices  30.9 us (13%)
  Pallas kernels  28.1 us (12%)
  starting transfers between devices  22 us (9%)
  between operations  14.2 us (6%)
  local copies, waits for them, and re-layouts  12.7 us (5%)
    all_to_all x3, blocking collectives, body(): mine = lax.all_to_all(mine, 'yq', 0, 0, tiled=True)  34.1 us
    all_to_all x3, blocking collectives, body(): got = lax.all_to_all(y, GROUP, 0, 0, tiled=True)  31.4 us
    all_to_all x3, waiting for transfers between devices, spread(): lax.all_to_all(jnp.broadcast_to(array[None], (lax.axis_size(axes), *array...  27.3 us
    all_to_all x1, blocking collectives, body(): first = lax.all_to_all(first, RHS, 0, 0, tiled=True)  26.1 us
    all_to_all x1, blocking collectives, body(): got = lax.all_to_all(sent, 'yq', 0, 0, tiled=True)  21.8 us
    all_to_all x1, blocking collectives, spread(): lax.all_to_all(jnp.broadcast_to(array[None], (lax.axis_size(axes), *array...  17.4 us
    all_to_all x3, starting transfers between devices, spread(): lax.all_to_all(jnp.broadcast_to(array[None], (lax.axis_size(axes), *array...  14.4 us
    pallas_call x3, Pallas kernels, trail_call(): pl.pallas_call(kernel, out_shape=jax.ShapeDtypeStruct(out_shape, F32), gr...  11.7 us
  transfers between devices with their start and end apart: 7, of which 4 were waited for; matrix products, arithmetic and copies ran while one was open for 2% of the time, Pallas kernels for 8%

profile of v4, /device:TPU:8, one launch (start us, length us, event | category | flops | bytes accessed | tf_op | source)
XLA Modules:
  0.0 238.8 jit_solution(16037599452820502308)
XLA Ops:
  7.2 0.0 all-gather.3.cloned.1.call-start
  7.2 1.2 shard_map.50
  8.5 21.8 %all_to_all.70.refs_0_ = f32[4,224,128]{2,1,0:T(8,128)S(1)} all-to-all(f32[4,224,128]{2,1,0:T(8,128)S(1)} %shard_map.50), channel_id=1, replica_groups=mesh['x'=4,'yq'=4,'yp'=2,'z'=8,'core'=2] {'yq'}, dimensions={0} | all-to-all | bytes 917504 | tf_op jit(solution)/shard_map/all_to_all | solution.py:256
  30.3 1.1 shard_map.51
  31.4 26.1 %all_to_all.71.first_ref = f32[16,2,32,128]{3,2,1,0:T(8,128)S(1)} all-to-all(f32[16,2,32,128]{3,2,1,0:T(8,128)S(1)} %get-tuple-element.19), channel_id=1, replica_groups=mesh['x'=4,'yq'=4,'yp'=2,'z'=8,'core'=2] {'z','core'}, dimensions={0} | all-to-all | bytes 1048576 | tf_op jit(solution)/shard_map/all_to_all | solution.py:262
  57.5 0.0 all-gather.3.cloned.1.call-update
  57.6 0.0 all-gather.5.cloned.1.call-start
  57.6 0.4 shard_map.52
  58.0 11.7 %all_to_all.72.got_ref = f32[8,64,128]{2,1,0:T(8,128)S(1)} all-to-all(f32[8,64,128]{2,1,0:T(8,128)S(1)} %shard_map.52), channel_id=1, replica_groups=mesh['x'=4,'yq'=4,'yp'=2,'z'=8,'core'=2] {'yp','x'}, dimensions={0} | all-to-all | bytes 524288 | tf_op jit(solution)/shard_map/all_to_all | solution.py:272
  69.7 2.0 slice.3
  71.7 0.0 all-gather.5.cloned.1.call-update
  71.7 11.9 %all_to_all.73.refs_4_ = f32[4,64,128]{2,1,0:T(8,128)S(1)} all-to-all(f32[4,64,128]{2,1,0:T(8,128)S(1)} %shard_map.53), channel_id=1, replica_groups=mesh['x'=4,'yq'=4,'yp'=2,'z'=8,'core'=2] {'yq'}, dimensions={0} | all-to-all | bytes 262144 | tf_op jit(solution)/shard_map/all_to_all | solution.py:281
  83.6 1.1 broadcast_in_dim.12
  84.7 4.6 %all-to-all-start.4 = ((f32[8,4,64,128]{3,2,1,0:T(8,128)}), f32[8,4,64,128]{3,2,1,0:T(8,128)S(1)}, u32[]{:S(2)}, u32[]{:S(2)}) async-start(f32[8,4,64,128]{3,2,1,0:T(8,128)} %broadcast_in_dim.12), calls=%async_computation.4 | async-start | bytes 2097152 | tf_op jit(solution)/shard_map/all_to_all | solution.py:222
  89.3 14.3 %all-to-all-done.4.refs_1_.refs_0_ = f32[8,4,64,128]{3,2,1,0:T(8,128)S(1)} async-done(((f32[8,4,64,128]{3,2,1,0:T(8,128)}), f32[8,4,64,128]{3,2,1,0:T(8,128)S(1)}, u32[]{:S(2)}, u32[]{:S(2)}) %all-to-all-start.4) | async-done | bytes 1048608 | tf_op jit(solution)/shard_map/all_to_all | solution.py:222
  103.6 0.0 all-gather.3.cloned.1.call-done
  103.6 1.7 shard_map.54
  105.4 9.9 %all_to_all.74.got_ref = f32[8,64,128]{2,1,0:T(8,128)S(1)} all-to-all(f32[8,64,128]{2,1,0:T(8,128)S(1)} %shard_map.54), channel_id=1, replica_groups=mesh['x'=4,'yq'=4,'yp'=2,'z'=8,'core'=2] {'yp','x'}, dimensions={0} | all-to-all | bytes 524288 | tf_op jit(solution)/shard_map/all_to_all | solution.py:272
  115.3 11.0 %all_to_all.75.refs_5_ = f32[4,64,128]{2,1,0:T(8,128)S(1)} all-to-all(f32[4,64,128]{2,1,0:T(8,128)S(1)} %shard_map.55), channel_id=1, replica_groups=mesh['x'=4,'yq'=4,'yp'=2,'z'=8,'core'=2] {'yq'}, dimensions={0} | all-to-all | bytes 262144 | tf_op jit(solution)/shard_map/all_to_all | solution.py:281
  126.3 1.1 broadcast_in_dim.13
  127.5 4.7 %all-to-all-start.7 = ((f32[8,4,64,128]{3,2,1,0:T(8,128)}), f32[8,4,64,128]{3,2,1,0:T(8,128)S(1)}, u32[]{:S(2)}, u32[]{:S(2)}) async-start(f32[8,4,64,128]{3,2,1,0:T(8,128)} %broadcast_in_dim.13), calls=%async_computation.7 | async-start | bytes 2097152 | tf_op jit(solution)/shard_map/all_to_all | solution.py:222
  132.1 1.6 shard_map.56.refs_2_
  133.8 0.0 copy-start.5
  133.8 10.4 %all-to-all-done.7.refs_1_.refs_0_ = f32[8,4,64,128]{3,2,1,0:T(8,128)S(1)} async-done(((f32[8,4,64,128]{3,2,1,0:T(8,128)}), f32[8,4,64,128]{3,2,1,0:T(8,128)S(1)}, u32[]{:S(2)}, u32[]{:S(2)}) %all-to-all-start.7) | async-done | bytes 1048608 | tf_op jit(solution)/shard_map/all_to_all | solution.py:222
  144.2 1.7 shard_map.57
  145.9 9.8 %all_to_all.76.got_ref = f32[8,64,128]{2,1,0:T(8,128)S(1)} all-to-all(f32[8,64,128]{2,1,0:T(8,128)S(1)} %shard_map.57), channel_id=1, replica_groups=mesh['x'=4,'yq'=4,'yp'=2,'z'=8,'core'=2] {'yp','x'}, dimensions={0} | all-to-all | bytes 524288 | tf_op jit(solution)/shard_map/all_to_all | solution.py:272
  155.7 11.3 %all_to_all.77.refs_6_ = f32[4,64,128]{2,1,0:T(8,128)S(1)} all-to-all(f32[4,64,128]{2,1,0:T(8,128)S(1)} %shard_map.58), channel_id=1, replica_groups=mesh['x'=4,'yq'=4,'yp'=2,'z'=8,'core'=2] {'yq'}, dimensions={0} | all-to-all | bytes 262144 | tf_op jit(solution)/shard_map/all_to_all | solution.py:281
  167.0 1.1 broadcast_in_dim.14
  168.2 0.0 copy-done.5
  168.2 5.1 %all-to-all-start.10 = ((f32[8,4,64,128]{3,2,1,0:T(8,128)}), f32[8,4,64,128]{3,2,1,0:T(8,128)S(1)}, u32[]{:S(2)}, u32[]{:S(2)}) async-start(f32[8,4,64,128]{3,2,1,0:T(8,128)} %broadcast_in_dim.14), calls=%async_computation.10 | async-start | bytes 2097152 | tf_op jit(solution)/shard_map/all_to_all | solution.py:222
  173.3 0.0 copy-start.6
  173.3 0.8 copy-done.6
  174.1 1.3 shard_map.60.refs_2_
  175.4 0.0 copy-start.7
  175.4 0.6 copy-done.7
  176.1 0.0 all-gather.5.cloned.1.call-done.refs_1_
  176.1 0.0 copy-start
  176.1 1.1 copy-done
  177.2 4.0 %shard_map.59.refs_2_ = f32[256,576]{1,0:T(8,128)S(1)} custom-call(f32[8,4,64,128]{3,2,1,0:T(8,128)S(1)} %all-to-all-done.4.refs_1_.refs_0_, f32[4,2,512,576]{3,2,1,0:T(8,128)} %all-gather.5.cloned.1.call-done.refs_1_, f32[704,256]{1,0:T(8,128)S(1)} %bitcast.14), custom_call_target="tpu_custom_call" | custom-call | tf_op jit(solution)/shard_map/pallas_call | solution.py:210
  181.2 0.0 copy-start.1
  181.2 0.8 copy-done.1
  182.0 2.6 %all-to-all-done.10.refs_1_.refs_0_ = f32[8,4,64,128]{3,2,1,0:T(8,128)S(1)} async-done(((f32[8,4,64,128]{3,2,1,0:T(8,128)}), f32[8,4,64,128]{3,2,1,0:T(8,128)S(1)}, u32[]{:S(2)}, u32[]{:S(2)}) %all-to-all-start.10) | async-done | bytes 1048608 | tf_op jit(solution)/shard_map/all_to_all | solution.py:222
  184.6 0.0 copy-start.8
  184.6 0.8 copy-done.8
  185.4 2.4 %shard_map.61 = f32[8,64,128]{2,1,0:T(8,128)} custom-call(s32[1]{0:T(128)} %bitcast.refs_0_.refs_3_, f32[8,4,64,128]{3,2,1,0:T(8,128)S(1)} %all-to-all-done.10.refs_1_.refs_0_, f32[1,64,128]{2,1,0:T(8,128)S(1)} %copy-done.8, f32[9,1024,128]{2,1,0:T(8,128)} %bitcast.20), custom_call_target="tpu_custom_call" | custom-call | tf_op jit(solution)/shard_map/pallas_call | solution.py:296
  187.8 4.2 %all-to-all-start.11 = ((f32[8,64,128]{2,1,0:T(8,128)}), f32[8,64,128]{2,1,0:T(8,128)S(1)}, u32[]{:S(2)}, u32[]{:S(2)}) async-start(f32[8,64,128]{2,1,0:T(8,128)} %shard_map.61), calls=%async_computation.11 | async-start | bytes 524288 | tf_op jit(solution)/shard_map/all_to_all | solution.py:272
  192.0 0.0 copy-start.2
  192.0 1.1 copy-done.2
  193.1 3.8 %shard_map.62.refs_2_ = f32[256,576]{1,0:T(8,128)S(1)} custom-call(f32[8,4,64,128]{3,2,1,0:T(8,128)S(1)} %all-to-all-done.7.refs_1_.refs_0_, f32[4,2,512,576]{3,2,1,0:T(8,128)} %all-gather.5.cloned.1.call-done.refs_1_, f32[256,576]{1,0:T(8,128)S(1)} %copy-done.2), custom_call_target="tpu_custom_call" | custom-call | tf_op jit(solution)/shard_map/pallas_call | solution.py:210
  196.9 0.0 copy-start.3
  196.9 0.8 copy-done.3
  197.8 0.0 all-to-all-done.11.got_ref
  197.8 0.7 shard_map.63
  198.5 3.3 %all-to-all-start.12 = ((f32[4,64,128]{2,1,0:T(8,128)}), f32[4,64,128]{2,1,0:T(8,128)S(1)}, u32[]{:S(2)}, u32[]{:S(2)}) async-start(f32[4,64,128]{2,1,0:T(8,128)} %shard_map.63), calls=%async_computation.12 | async-start | bytes 262144 | tf_op jit(solution)/shard_map/all_to_all | solution.py:281
  201.8 0.0 copy-start.4
  201.8 1.1 copy-done.4
  202.9 3.8 %shard_map.64.refs_2_ = f32[256,576]{1,0:T(8,128)S(1)} custom-call(f32[8,4,64,128]{3,2,1,0:T(8,128)S(1)} %all-to-all-done.10.refs_1_.refs_0_, f32[4,2,512,576]{3,2,1,0:T(8,128)} %all-gather.5.cloned.1.call-done.refs_1_, f32[256,576]{1,0:T(8,128)S(1)} %copy-done.4), custom_call_target="tpu_custom_call" | custom-call | tf_op jit(solution)/shard_map/pallas_call | solution.py:210
  206.7 3.5 %all-to-all-done.12.refs_7_ = f32[4,64,128]{2,1,0:T(8,128)S(1)} async-done(((f32[4,64,128]{2,1,0:T(8,128)}), f32[4,64,128]{2,1,0:T(8,128)S(1)}, u32[]{:S(2)}, u32[]{:S(2)}) %all-to-all-start.12) | async-done | bytes 131104 | tf_op jit(solution)/shard_map/all_to_all | solution.py:281
  210.3 0.1 broadcast_in_dim.15
  210.4 17.4 %all_to_all.78.refs_0_ = f32[8,4,64,128]{3,2,1,0:T(8,128)S(1)} all-to-all(f32[8,4,64,128]{3,2,1,0:T(8,128)S(1)} %broadcast_in_dim.15), channel_id=1, replica_groups=mesh['x'=4,'yq'=4,'yp'=2,'z'=8,'core'=2] {'yp','x'}, dimensions={0} | all-to-all | bytes 2097152 | tf_op jit(solution)/shard_map/all_to_all | solution.py:222
  227.8 4.1 %shard_map.65 = (f32[576,256]{1,0:T(8,128)}, f32[128,256]{1,0:T(8,128)}) custom-call(f32[8,4,64,128]{3,2,1,0:T(8,128)S(1)} %all_to_all.78.refs_0_, f32[4,4,256,576]{3,2,1,0:T(8,128)} %bitcast.15, f32[256,576]{1,0:T(8,128)S(1)} %shard_map.64.refs_2_, s32[1]{0:T(128)} %bitcast.refs_0_.refs_3_, f32[4,64,128]{2,1,0:T(8,128)S(1)} %all_to_all.73.refs_4_, ...), custom_call_target="tpu_custom_call" | custom-call | tf_op jit(solution)/shard_map/pallas_call | solution.py:314
  (3 shorter events, 0.1 us)
Async XLA Ops:
  7.2 96.5 %all-gather.3.cloned.1.call-start = ((), (), s32[]{:S(2)}) async-start(), calls=%async_computation.14 | async-start | bytes 5013504 | tf_op jit(solution)/shard_map/all_gather | solution.py:264
  57.6 118.5 %all-gather.5.cloned.1.call-start = ((), (), s32[]{:S(2)}) async-start(), calls=%async_computation.15 | async-start | bytes 11141120 | tf_op jit(solution)/shard_map/all_gather | solution.py:280
  84.7 18.9 %all-to-all-start.4 = ((f32[8,4,64,128]{3,2,1,0:T(8,128)}), f32[8,4,64,128]{3,2,1,0:T(8,128)S(1)}, u32[]{:S(2)}, u32[]{:S(2)}) async-start(f32[8,4,64,128]{3,2,1,0:T(8,128)} %broadcast_in_dim.12), calls=%async_computation.4 | async-start | bytes 2097152 | tf_op jit(solution)/shard_map/all_to_all | solution.py:222
  127.5 16.8 %all-to-all-start.7 = ((f32[8,4,64,128]{3,2,1,0:T(8,128)}), f32[8,4,64,128]{3,2,1,0:T(8,128)S(1)}, u32[]{:S(2)}, u32[]{:S(2)}) async-start(f32[8,4,64,128]{3,2,1,0:T(8,128)} %broadcast_in_dim.13), calls=%async_computation.7 | async-start | bytes 2097152 | tf_op jit(solution)/shard_map/all_to_all | solution.py:222
  133.8 34.4 %copy-start.5 = (f32[2,64,128]{2,1,0:T(8,128)}, f32[2,64,128]{2,1,0:T(8,128)S(1)}, u32[]{:S(2)}) copy-start(f32[2,64,128]{2,1,0:T(8,128)S(1)} %shard_map.56.refs_2_) | copy-start | bytes 196612
  168.2 16.5 %all-to-all-start.10 = ((f32[8,4,64,128]{3,2,1,0:T(8,128)}), f32[8,4,64,128]{3,2,1,0:T(8,128)S(1)}, u32[]{:S(2)}, u32[]{:S(2)}) async-start(f32[8,4,64,128]{3,2,1,0:T(8,128)} %broadcast_in_dim.14), calls=%async_computation.10 | async-start | bytes 2097152 | tf_op jit(solution)/shard_map/all_to_all | solution.py:222
  173.3 0.8 copy-start.6
  175.4 0.6 copy-start.7
  176.1 1.1 copy-start
  181.2 0.8 copy-start.1
  184.6 0.8 copy-start.8
  187.8 10.0 %all-to-all-start.11 = ((f32[8,64,128]{2,1,0:T(8,128)}), f32[8,64,128]{2,1,0:T(8,128)S(1)}, u32[]{:S(2)}, u32[]{:S(2)}) async-start(f32[8,64,128]{2,1,0:T(8,128)} %shard_map.61), calls=%async_computation.11 | async-start | bytes 524288 | tf_op jit(solution)/shard_map/all_to_all | solution.py:272
  192.0 1.1 copy-start.2
  196.9 0.9 copy-start.3
  198.5 11.8 %all-to-all-start.12 = ((f32[4,64,128]{2,1,0:T(8,128)}), f32[4,64,128]{2,1,0:T(8,128)S(1)}, u32[]{:S(2)}, u32[]{:S(2)}) async-start(f32[4,64,128]{2,1,0:T(8,128)} %shard_map.63), calls=%async_computation.12 | async-start | bytes 262144 | tf_op jit(solution)/shard_map/all_to_all | solution.py:281
  201.8 1.1 copy-start.4
Sparse Core Ops, SparseCore 0:
  57.7 39.7 all-gather.2
  99.6 67.5 all-gather.4

commit v5 on v4

--- a/solution.py
+++ b/solution.py
@@ -6,6 +6,7 @@
 from jax.sharding import Mesh, PartitionSpec as P
 
 QUADS = 4
+BATCHES = ((0, 1), (2,))
 RHS = ("z", "core")
 GROUP = ("yp", "x")
 F32 = jnp.float32
@@ -122,13 +123,13 @@
         out_ref[c] = total
 
 
-def advance(base, at, diag_at, quad_ref, solved_ref, head_ref, rest_hbm, y_out, line_ref, diag_ref, sems):
+def advance(base, at, diag_at, solved_ref, head_ref, rest_hbm, y_out, line_ref, diag_ref, sems):
     group, rows = y_out.shape[0], y_out.shape[2]
     first = pltpu.make_async_copy(rest_hbm.at[at], line_ref, sems.at[0])
     second = pltpu.make_async_copy(rest_hbm.at[diag_at], diag_ref, sems.at[1])
     first.start()
     second.start()
-    x = chosen(quad_ref, solved_ref)
+    x = chosen(solved_ref)
     first.wait()
     head = head_ref[base] - dot(x, line_ref[...], NN)
     second.wait()
@@ -137,16 +138,15 @@
         y_out[s] = y[:, s * rows : (s + 1) * rows]
 
 
-def chosen(quad_ref, solved_ref):
-    quad = quad_ref[0]
-    return jnp.concatenate([solved_ref[s, quad] for s in range(solved_ref.shape[0])], axis=1)
-
-
-def follow(base, at, quad_ref, solved_ref, heads_ref, rest_hbm, heads_out, lines_ref, sem):
+def chosen(solved_ref):
+    return jnp.concatenate([solved_ref[s] for s in range(solved_ref.shape[0])], axis=1)
+
+
+def follow(base, at, solved_ref, heads_ref, rest_hbm, heads_out, lines_ref, sem):
     left = heads_out.shape[0]
     copy = pltpu.make_async_copy(rest_hbm.at[pl.ds(at, left)], lines_ref, sem)
     copy.start()
-    x = chosen(quad_ref, solved_ref)
+    x = chosen(solved_ref)
     copy.wait()
     for b in range(left):
         heads_out[b] = heads_ref[base + b + 1] - dot(x, lines_ref[b], NN)
@@ -161,20 +161,17 @@
 
 
 def trail_sum(n, *refs):
-    x_refs, f_ref, init_ref, out_ref = refs[:n], refs[n], refs[n + 1], refs[-1]
+    x_refs, f_ref, out_ref = refs[:n], refs[n], refs[-1]
 
     @pl.when(pl.program_id(0) == 0)
     def _():
-        if init_ref.shape == out_ref.shape:
-            out_ref[...] = init_ref[...]
-        else:
-            out_ref[...] = init_ref[init_ref.shape[0] - out_ref.shape[1] :].T
-
-    out_ref[...] -= dot(stacked(x_refs), f_ref[0, 0], NN)
-
-
-def finish(panel, x_ref, f_hbm, base_ref, quad_ref, *refs):
-    own_refs, (out_ref, mine_ref, turned_ref, f_ref, sems) = refs[:-5], refs[-5:]
+        out_ref[...] = jnp.zeros_like(out_ref) if len(refs) == n + 2 else refs[n + 1][...]
+
+    out_ref[...] += dot(stacked(x_refs), f_ref[0, 0], NN)
+
+
+def finish(panel, x_ref, f_hbm, sum_ref, quad_ref, r_hbm, *refs):
+    own_refs, (out_ref, mine_ref, turned_ref, f_ref, r_ref, sems) = refs[:-6], refs[-6:]
     n = f_ref.shape[0]
     copies = [
         pltpu.make_async_copy(f_hbm.at[panel, b], f_ref.at[b], sems.at[b]) for b in range(n)
@@ -182,15 +179,30 @@
     for c in copies:
         c.start()
     width = mine_ref.shape[0] // len(own_refs)
-    at = pl.multiple_of(quad_ref[0] * width, width)
+    rows = pltpu.make_async_copy(
+        r_hbm.at[pl.ds(mine_ref.shape[0], r_ref.shape[0])], r_ref, sems.at[n]
+    )
+    rows.start()
+    quad = quad_ref[0]
+    quads, per, _ = own_refs[0].shape
+    at = pl.multiple_of(quad * width, width)
     for k, own_ref in enumerate(own_refs):
-        turned_ref[...] = own_ref[...].reshape(-1, own_ref.shape[2]).T
+        shift = quads - quad if k < panel else 0
+        own = [own_ref[lax.rem(q + shift, quads)] for q in range(quads)]
+        turned_ref[...] = jnp.concatenate(own, axis=0).T
         mine_ref[k * width : (k + 1) * width] = turned_ref[pl.ds(at, width)]
-    total = base_ref[...]
+    total = jnp.concatenate(
+        [
+            sum_ref[pl.ds(pl.multiple_of(lax.rem(q + quads - quad, quads) * per, per), per)]
+            for q in range(quads)
+        ],
+        axis=0,
+    )
     for b, c in enumerate(copies):
         c.wait()
-        total -= dot(stacked([x_ref.at[pl.ds(2 * b, 2)]]), f_ref[b], NN)
-    out_ref[...] = total.T
+        total += dot(stacked([x_ref.at[pl.ds(2 * b, 2)]]), f_ref[b], NN)
+    rows.wait()
+    out_ref[...] = r_ref[...] - total.T
 
 
 def trail_call(kernel, x, f, k, out_shape, extra=(), specs=(), steps=1, scratch=()):
@@ -260,74 +272,83 @@
         [VMEM],
     )(got)
     first = lax.all_to_all(first, RHS, 0, 0, tiled=True)
-    pay, first = lax.optimization_barrier((pay, first))
     rest = lax.all_gather(pay, RHS, axis=2, tiled=True)
     rest = rest.reshape(9, group * rows, rows)
 
     (y,) = call(begin, [(group, per, rows)], [VMEM, VMEM])(heads, first)
     length = lower.shape[2] - tail
-    own, late = {}, {}
-    trail = base = None
+    place = lax.axis_index("yp") * nx + lax.axis_index("x")
+    own, waiting, sent = {}, [], []
+    trail = total = None
     for k in range(panels):
         got = lax.all_to_all(y, GROUP, 0, 0, tiled=True)
-        if k == 3:
-            base = add_trail(late[1], trail, 1, base)
-            got, base = lax.optimization_barrier((got, base))
-        (mine,) = call(add_up, [(quads, per, rows)], [VMEM])(got)
+        copies = group if k < panels - 1 else quads
+        (mine,) = call(add_up, [(copies, per, rows)], [VMEM])(got)
         if k == 0:
             lower, mine = lax.optimization_barrier((lower, mine))
             trail = lower[:, :, tail:].reshape(panels, npair, half, -1)
             trail = lax.all_gather(trail, RHS, axis=2, tiled=True)
-        mine = lax.all_to_all(mine, "yq", 0, 0, tiled=True)
-        if k == 3:
-            base = add_trail(late[2], trail, 2, base)
-            mine, base = lax.optimization_barrier((mine, base))
-        own[k] = mine
-        solved = spread(mine, GROUP)
-        if k == 2:
-            base = add_trail(late[0], trail, 0, current)
-            solved, base = lax.optimization_barrier((solved, base))
-        late[k] = solved
         if k == panels - 1:
+            mine = lax.all_to_all(mine, "yq", 0, 0, tiled=True)
+            own[k] = mine
+            solved = spread(mine, GROUP)
             break
+        solved = lax.all_to_all(mine, GROUP, 0, 0, tiled=True)
+        waiting.append(solved)
+        if len(sent) < len(BATCHES) and BATCHES[len(sent)][-1] == k:
+            batch = jnp.stack(waiting)
+            parts = [batch] + [
+                lax.ppermute(batch, "yq", [(i, (i - t) % quads) for i in range(quads)])
+                for t in range(1, quads)
+            ]
+            sent.append(parts)
+            waiting = []
         left = panels - 1 - k
         at = {3: 3, 2: 6, 1: 8}[left]
         one = pltpu.VMEM((group * rows, rows), F32)
         (y,) = call(
             lambda *refs, at=at, k=k: advance(int(k == 0), at, k, *refs),
             [(group, per, rows)],
-            [SMEM, VMEM, VMEM, HBM],
+            [VMEM, VMEM, HBM],
             [one, one, pltpu.SemaphoreType.DMA((2,))],
-        )(index, solved, heads, in_hbm(rest))
+        )(solved, heads, in_hbm(rest))
         if left > 1:
             (heads,) = call(
                 lambda *refs, at=at, k=k: follow(int(k == 0), at + 1, *refs),
                 [(left - 1, per, rows)],
-                [SMEM, VMEM, VMEM, HBM],
+                [VMEM, VMEM, HBM],
                 [
                     pltpu.VMEM((left - 1, group * rows, rows), F32),
                     pltpu.SemaphoreType.DMA,
                 ],
-            )(index, solved, heads, in_hbm(rest))
-
+            )(solved, heads, in_hbm(rest))
+
+    for batch, parts in zip(BATCHES, sent):
+        total = add_trail(parts, trail, batch[0], len(batch), total)
+        here = [lax.dynamic_index_in_dim(p, place, 1, keepdims=False) for p in parts]
+        for n, k in enumerate(batch):
+            own[k] = jnp.stack([p[n] for p in here])
     flat = trail.reshape(panels, -1, 2 * rows, length)
     out, mine = call(
         lambda *refs: finish(panels - 1, *refs),
         [(length, count), (tail, count)],
-        [VMEM, HBM, VMEM, SMEM] + [VMEM] * panels,
+        [VMEM, HBM, VMEM, SMEM, HBM] + [VMEM] * panels,
         [
             pltpu.VMEM((rows, count), F32),
             pltpu.VMEM(flat.shape[1:], F32),
-            pltpu.SemaphoreType.DMA((flat.shape[1],)),
+            pltpu.VMEM((length, count), F32),
+            pltpu.SemaphoreType.DMA((flat.shape[1] + 1,)),
         ],
-    )(late[3], in_hbm(flat), base, index, *[own[k] for k in range(panels)])
+    )(solved, in_hbm(flat), total, index, in_hbm(current), *[own[k] for k in range(panels)])
     return (mine[None], out[None])
 
 
-def add_trail(x, trail, k, init):
-    shape = (x.shape[1] * x.shape[2], trail.shape[3])
+def add_trail(parts, trail, k, steps, total):
+    shape = (len(parts) * parts[0].shape[2], trail.shape[3])
+    more = () if total is None else (total,)
     return trail_call(
-        lambda *refs: trail_sum(1, *refs), [x], trail, k, shape, (init,), (whole(init.shape),)
+        lambda *refs: trail_sum(len(parts), *refs), parts, trail, k, shape,
+        more, (whole(shape),) * len(more), steps,
     )
 
 

time: 240 us -> 264 us (1.10)
  the two profiles are of different devices: /device:TPU:8 before, /device:TPU:23 now
where the time goes in v5:
time: 264 us; the launch traced here: 263 us
  blocking collectives  104 us (39%)
  waiting for transfers between devices  72.8 us (28%)
  starting transfers between devices  37.4 us (14%)
  Pallas kernels  27.9 us (11%)
  between operations  14.3 us (5%)
  local copies, waits for them, and re-layouts  6.38 us (2%)
    ppermute x6, waiting for transfers between devices, body(): lax.ppermute(batch, 'yq', [(i, (i - t) % quads) for i in range(quads)])  64.6 us
    all_to_all x4, blocking collectives, body(): got = lax.all_to_all(y, GROUP, 0, 0, tiled=True)  33.7 us
    all_to_all x1, blocking collectives, body(): first = lax.all_to_all(first, RHS, 0, 0, tiled=True)  30.8 us
    all_to_all x1, blocking collectives, body(): got = lax.all_to_all(sent, 'yq', 0, 0, tiled=True)  20.8 us
    ppermute x6, starting transfers between devices, body(): lax.ppermute(batch, 'yq', [(i, (i - t) % quads) for i in range(quads)])  20.4 us
    pallas_call x2, Pallas kernels, trail_call(): pl.pallas_call(kernel, out_shape=jax.ShapeDtypeStruct(out_shape, F32), gr...  11.2 us
    all_to_all x2, starting transfers between devices, body(): solved = lax.all_to_all(mine, GROUP, 0, 0, tiled=True)  10.8 us
    all_to_all x1, blocking collectives, body(): mine = lax.all_to_all(mine, 'yq', 0, 0, tiled=True)  9.21 us
  transfers between devices with their start and end apart: 11, of which 8 were waited for; matrix products, arithmetic and copies ran while one was open for 2% of the time, Pallas kernels for 8%

profile of v5, /device:TPU:23, one launch (start us, length us, event | category | flops | bytes accessed | tf_op | source)
XLA Modules:
  0.0 262.6 jit_solution(11676380200787400860)
XLA Ops:
  7.2 0.0 all-gather.3.cloned.1.call-start
  7.2 1.2 shard_map.50
  8.5 20.8 %all_to_all.55.refs_0_ = f32[4,224,128]{2,1,0:T(8,128)S(1)} all-to-all(f32[4,224,128]{2,1,0:T(8,128)S(1)} %shard_map.50), channel_id=1, replica_groups=mesh['x'=4,'yq'=4,'yp'=2,'z'=8,'core'=2] {'yq'}, dimensions={0} | all-to-all | bytes 917504 | tf_op jit(solution)/shard_map/all_to_all | solution.py:268
  29.3 1.1 shard_map.51
  30.4 0.0 all-gather.3.cloned.1.call-update
  30.4 0.0 all-gather.5.cloned.1.call-start
  30.5 30.8 %all_to_all.56.first_ref = f32[16,2,32,128]{3,2,1,0:T(8,128)S(1)} all-to-all(f32[16,2,32,128]{3,2,1,0:T(8,128)S(1)} %get-tuple-element.10), channel_id=1, replica_groups=mesh['x'=4,'yq'=4,'yp'=2,'z'=8,'core'=2] {'z','core'}, dimensions={0} | all-to-all | bytes 1048576 | tf_op jit(solution)/shard_map/all_to_all | solution.py:274
  61.3 0.4 shard_map.52
  61.7 8.3 %all_to_all.57.got_ref = f32[8,64,128]{2,1,0:T(8,128)S(1)} all-to-all(f32[8,64,128]{2,1,0:T(8,128)S(1)} %shard_map.52), channel_id=1, replica_groups=mesh['x'=4,'yq'=4,'yp'=2,'z'=8,'core'=2] {'yp','x'}, dimensions={0} | all-to-all | bytes 524288 | tf_op jit(solution)/shard_map/all_to_all | solution.py:284
  70.0 2.0 slice.51
  72.0 0.0 all-gather.5.cloned.1.call-update
  72.0 9.1 %all_to_all.58.refs_0_ = f32[8,64,128]{2,1,0:T(8,128)S(1)} all-to-all(f32[8,64,128]{2,1,0:T(8,128)S(1)} %shard_map.53), channel_id=1, replica_groups=mesh['x'=4,'yq'=4,'yp'=2,'z'=8,'core'=2] {'yp','x'}, dimensions={0} | all-to-all | bytes 524288 | tf_op jit(solution)/shard_map/all_to_all | solution.py:296
  81.1 2.8 %all-gather.3.cloned.1.call-done = f32[9,2,512,128]{3,2,1,0:T(8,128)} async-done(((f32[9,2,32,128]{3,2,1,0:T(8,128)}), f32[9,2,512,128]{3,2,1,0:T(8,128)}) %all-gather.3.cloned.1.call-update) | async-done | bytes 4718608 | tf_op jit(solution)/shard_map/all_gather | solution.py:275
  84.0 1.7 shard_map.54
  85.7 8.4 %all_to_all.59.got_ref = f32[8,64,128]{2,1,0:T(8,128)S(1)} all-to-all(f32[8,64,128]{2,1,0:T(8,128)S(1)} %shard_map.54), channel_id=1, replica_groups=mesh['x'=4,'yq'=4,'yp'=2,'z'=8,'core'=2] {'yp','x'}, dimensions={0} | all-to-all | bytes 524288 | tf_op jit(solution)/shard_map/all_to_all | solution.py:284
  94.1 0.7 shard_map.55
  94.9 5.5 %all-to-all-start.5 = ((f32[8,64,128]{2,1,0:T(8,128)}), f32[8,64,128]{2,1,0:T(8,128)S(1)}, u32[]{:S(2)}, u32[]{:S(2)}) async-start(f32[8,64,128]{2,1,0:T(8,128)} %shard_map.55), calls=%async_computation.5 | async-start | bytes 524288 | tf_op jit(solution)/shard_map/all_to_all | solution.py:296
  100.4 1.6 shard_map.56.refs_1_
  102.1 2.5 all-to-all-done.5.refs_0_
  104.5 1.7 shard_map.57
  106.3 8.5 %all_to_all.60.got_ref = f32[8,64,128]{2,1,0:T(8,128)S(1)} all-to-all(f32[8,64,128]{2,1,0:T(8,128)S(1)} %shard_map.57), channel_id=1, replica_groups=mesh['x'=4,'yq'=4,'yp'=2,'z'=8,'core'=2] {'yp','x'}, dimensions={0} | all-to-all | bytes 524288 | tf_op jit(solution)/shard_map/all_to_all | solution.py:284
  114.8 0.7 shard_map.58
  115.5 5.3 %all-to-all-start.7 = ((f32[8,64,128]{2,1,0:T(8,128)}), f32[8,64,128]{2,1,0:T(8,128)S(1)}, u32[]{:S(2)}, u32[]{:S(2)}) async-start(f32[8,64,128]{2,1,0:T(8,128)} %shard_map.58), calls=%async_computation.7 | async-start | bytes 524288 | tf_op jit(solution)/shard_map/all_to_all | solution.py:296
  120.8 1.3 shard_map.59.refs_1_
  122.1 2.8 %all-to-all-done.7.refs_0_ = f32[8,64,128]{2,1,0:T(8,128)S(1)} async-done(((f32[8,64,128]{2,1,0:T(8,128)}), f32[8,64,128]{2,1,0:T(8,128)S(1)}, u32[]{:S(2)}, u32[]{:S(2)}) %all-to-all-start.7) | async-done | bytes 262176 | tf_op jit(solution)/shard_map/all_to_all | solution.py:296
  124.9 1.7 shard_map.60
  126.7 8.5 %all_to_all.61.got_ref = f32[8,64,128]{2,1,0:T(8,128)S(1)} all-to-all(f32[8,64,128]{2,1,0:T(8,128)S(1)} %shard_map.60), channel_id=1, replica_groups=mesh['x'=4,'yq'=4,'yp'=2,'z'=8,'core'=2] {'yp','x'}, dimensions={0} | all-to-all | bytes 524288 | tf_op jit(solution)/shard_map/all_to_all | solution.py:284
  135.2 9.2 %all_to_all.62.refs_8_ = f32[4,64,128]{2,1,0:T(8,128)S(1)} all-to-all(f32[4,64,128]{2,1,0:T(8,128)S(1)} %shard_map.61), channel_id=1, replica_groups=mesh['x'=4,'yq'=4,'yp'=2,'z'=8,'core'=2] {'yq'}, dimensions={0} | all-to-all | bytes 262144 | tf_op jit(solution)/shard_map/all_to_all | solution.py:292
  144.4 1.1 broadcast_in_dim.12
  145.5 6.2 %all-to-all-start.10 = ((f32[8,4,64,128]{3,2,1,0:T(8,128)}), f32[8,4,64,128]{3,2,1,0:T(8,128)S(1)}, u32[]{:S(2)}, u32[]{:S(2)}) async-start(f32[8,4,64,128]{3,2,1,0:T(8,128)} %broadcast_in_dim.12), calls=%async_computation.10 | async-start | bytes 2097152 | tf_op jit(solution)/shard_map/all_to_all | solution.py:234
  151.7 2.5 collective-permute-start.5
  154.2 5.9 %collective-permute-start.4 = (f32[2,8,64,128]{3,2,1,0:T(8,128)S(1)}, f32[2,8,64,128]{3,2,1,0:T(8,128)}, u32[]{:S(2)}, u32[]{:S(2)}) collective-permute-start(f32[2,8,64,128]{3,2,1,0:T(8,128)S(1)} %pad_maximum_fusion.refs_0_), channel_id=1, source_target_pairs={{0,64},{32,96},{64,0},{96,32},{1,65},{33,97},{65,1},{97,33},{2,66}... | collective-permute-start | bytes 1572872 | tf_op jit(solution)/shard_map/ppermute | solution.py:301
  160.2 1.9 collective-permute-start.3
  162.1 21.6 %collective-permute-done.5.refs_3_ = f32[2,8,64,128]{3,2,1,0:T(8,128)S(1)} collective-permute-done((f32[2,8,64,128]{3,2,1,0:T(8,128)S(1)}, f32[2,8,64,128]{3,2,1,0:T(8,128)S(1)}, u32[]{:S(2)}, u32[]{:S(2)}) %collective-permute-start.5) | collective-permute-done | bytes 524320 | tf_op jit(solution)/shard_map/ppermute | solution.py:301
  183.7 21.2 %collective-permute-done.4.refs_2_ = f32[2,8,64,128]{3,2,1,0:T(8,128)} collective-permute-done((f32[2,8,64,128]{3,2,1,0:T(8,128)S(1)}, f32[2,8,64,128]{3,2,1,0:T(8,128)}, u32[]{:S(2)}, u32[]{:S(2)}) %collective-permute-start.4) | collective-permute-done | bytes 524320 | tf_op jit(solution)/shard_map/ppermute | solution.py:301
  204.9 0.8 dynamic-slice_bitcast_fusion.1
  205.7 1.9 collective-permute-start.2
  207.6 0.0 collective-permute-done.3.refs_1_
  207.6 0.0 copy-start
  207.6 3.9 %collective-permute-start.1 = (f32[1,8,64,128]{3,2,1,0:T(8,128)S(1)}, f32[1,8,64,128]{3,2,1,0:T(8,128)S(1)}, u32[]{:S(2)}, u32[]{:S(2)}) collective-permute-start(f32[1,8,64,128]{3,2,1,0:T(8,128)S(1)} %bitcast.43), channel_id=1, source_target_pairs={{0,64},{32,96},{64,0},{96,32},{1,65},{33,97},{65,1},{97,33},{2,66}... | collective-permute-start | bytes 786440 | tf_op jit(solution)/shard_map/ppermute | solution.py:301
  211.5 4.3 %collective-permute-start = (f32[1,8,64,128]{3,2,1,0:T(8,128)S(1)}, f32[1,8,64,128]{3,2,1,0:T(8,128)S(1)}, u32[]{:S(2)}, u32[]{:S(2)}) collective-permute-start(f32[1,8,64,128]{3,2,1,0:T(8,128)S(1)} %bitcast.44), channel_id=1, source_target_pairs={{0,96},{32,0},{64,32},{96,64},{1,97},{33,1},{65,33},{97,65},{2,98}... | collective-permute-start | bytes 786440 | tf_op jit(solution)/shard_map/ppermute | solution.py:301
  215.8 2.4 collective-permute-done.2.refs_3_
  218.2 6.4 %collective-permute-done.1.refs_2_ = f32[1,8,64,128]{3,2,1,0:T(8,128)S(1)} collective-permute-done((f32[1,8,64,128]{3,2,1,0:T(8,128)S(1)}, f32[1,8,64,128]{3,2,1,0:T(8,128)S(1)}, u32[]{:S(2)}, u32[]{:S(2)}) %collective-permute-start.1) | collective-permute-done | bytes 262176 | tf_op jit(solution)/shard_map/ppermute | solution.py:301
  224.6 0.0 copy-start.2
  224.6 0.7 copy-done.2
  225.3 13.1 %collective-permute-done.refs_1_ = f32[1,8,64,128]{3,2,1,0:T(8,128)S(1)} collective-permute-done((f32[1,8,64,128]{3,2,1,0:T(8,128)S(1)}, f32[1,8,64,128]{3,2,1,0:T(8,128)S(1)}, u32[]{:S(2)}, u32[]{:S(2)}) %collective-permute-start) | collective-permute-done | bytes 262176 | tf_op jit(solution)/shard_map/ppermute | solution.py:301
  238.4 0.0 copy-done
  238.4 0.0 copy-start.4
  238.4 0.7 copy-done.4
  239.1 0.0 all-gather.5.cloned.1.call-done.refs_4_
  239.2 0.0 copy-start.1
  239.2 1.0 copy-done.1
  240.2 0.0 copy-start.3
  240.2 0.0 copy-start.5
  240.2 7.3 %shard_map.62.refs_5_ = f32[256,576]{1,0:T(8,128)S(1)} custom-call(f32[2,8,64,128]{3,2,1,0:T(8,128)S(1)} %pad_maximum_fusion.refs_0_, f32[2,8,64,128]{3,2,1,0:T(8,128)S(1)} %copy-done.1, f32[2,8,64,128]{3,2,1,0:T(8,128)} %collective-permute-done.4.refs_2_, f32[2,8,64,128]{3,2,1,0:T(8,128)S(1)} %collective-permute-done.5.refs_3_, ...), custom_call_target="tpu_custom_call" | custom-call | tf_op jit(solution)/shard_map/pallas_call | solution.py:222
  247.5 0.0 copy-done.3
  247.6 0.0 copy-done.5
  247.6 3.9 %shard_map.63.refs_2_ = f32[256,576]{1,0:T(8,128)S(1)} custom-call(f32[1,8,64,128]{3,2,1,0:T(8,128)S(1)} %bitcast.45, f32[1,8,64,128]{3,2,1,0:T(8,128)S(1)} %copy-done.5, f32[1,8,64,128]{3,2,1,0:T(8,128)S(1)} %copy-done.3, f32[1,8,64,128]{3,2,1,0:T(8,128)S(1)} %collective-permute-done.2.refs_3_, f32[4,2,512,576]{3,2,1,0:T(8,128)} %all-gather.5.cloned.1.call-done.refs_4_, ...), custom_call_target="tpu_custom_call" | custom-call | tf_op jit(solution)/shard_map/pallas_call | solution.py:222
  251.4 0.0 all-to-all-done.10.refs_0_
  251.5 4.3 %shard_map.64 = (f32[576,256]{1,0:T(8,128)}, f32[128,256]{1,0:T(8,128)}) custom-call(f32[8,4,64,128]{3,2,1,0:T(8,128)S(1)} %all-to-all-done.10.refs_0_, f32[4,4,256,576]{3,2,1,0:T(8,128)} %bitcast.51, f32[256,576]{1,0:T(8,128)S(1)} %shard_map.63.refs_2_, s32[1]{0:T(128)} %bitcast.12.refs_3_, f32[704,256]{1,0:T(8,128)} %bitcast.53, ...), custom_call_target="tpu_custom_call" | custom-call | tf_op jit(solution)/shard_map/pallas_call | solution.py:332
  (13 shorter events, 0.2 us)
Async XLA Ops:
  7.2 76.8 %all-gather.3.cloned.1.call-start = ((), (), s32[]{:S(2)}) async-start(), calls=%async_computation.11 | async-start | bytes 5013504 | tf_op jit(solution)/shard_map/all_gather | solution.py:275
  30.4 208.8 %all-gather.5.cloned.1.call-start = ((), (), s32[]{:S(2)}) async-start(), calls=%async_computation.12 | async-start | bytes 11141120 | tf_op jit(solution)/shard_map/all_gather | solution.py:290
  94.9 9.7 %all-to-all-start.5 = ((f32[8,64,128]{2,1,0:T(8,128)}), f32[8,64,128]{2,1,0:T(8,128)S(1)}, u32[]{:S(2)}, u32[]{:S(2)}) async-start(f32[8,64,128]{2,1,0:T(8,128)} %shard_map.55), calls=%async_computation.5 | async-start | bytes 524288 | tf_op jit(solution)/shard_map/all_to_all | solution.py:296
  115.5 9.4 %all-to-all-start.7 = ((f32[8,64,128]{2,1,0:T(8,128)}), f32[8,64,128]{2,1,0:T(8,128)S(1)}, u32[]{:S(2)}, u32[]{:S(2)}) async-start(f32[8,64,128]{2,1,0:T(8,128)} %shard_map.58), calls=%async_computation.7 | async-start | bytes 524288 | tf_op jit(solution)/shard_map/all_to_all | solution.py:296
  145.5 106.0 %all-to-all-start.10 = ((f32[8,4,64,128]{3,2,1,0:T(8,128)}), f32[8,4,64,128]{3,2,1,0:T(8,128)S(1)}, u32[]{:S(2)}, u32[]{:S(2)}) async-start(f32[8,4,64,128]{3,2,1,0:T(8,128)} %broadcast_in_dim.12), calls=%async_computation.10 | async-start | bytes 2097152 | tf_op jit(solution)/shard_map/all_to_all | solution.py:234
  151.7 32.0 %collective-permute-start.5 = (f32[2,8,64,128]{3,2,1,0:T(8,128)S(1)}, f32[2,8,64,128]{3,2,1,0:T(8,128)S(1)}, u32[]{:S(2)}, u32[]{:S(2)}) collective-permute-start(f32[2,8,64,128]{3,2,1,0:T(8,128)S(1)} %pad_maximum_fusion.refs_0_), channel_id=1, source_target_pairs={{0,32},{32,64},{64,96},{96,0},{1,33},{33,65},{65,97},{97,1},{2,34}... | collective-permute-start | bytes 1572872 | tf_op jit(solution)/shard_map/ppermute | solution.py:301
  154.2 50.6 %collective-permute-start.4 = (f32[2,8,64,128]{3,2,1,0:T(8,128)S(1)}, f32[2,8,64,128]{3,2,1,0:T(8,128)}, u32[]{:S(2)}, u32[]{:S(2)}) collective-permute-start(f32[2,8,64,128]{3,2,1,0:T(8,128)S(1)} %pad_maximum_fusion.refs_0_), channel_id=1, source_target_pairs={{0,64},{32,96},{64,0},{96,32},{1,65},{33,97},{65,1},{97,33},{2,66}... | collective-permute-start | bytes 1572872 | tf_op jit(solution)/shard_map/ppermute | solution.py:301
  160.2 47.4 %collective-permute-start.3 = (f32[2,8,64,128]{3,2,1,0:T(8,128)S(1)}, f32[2,8,64,128]{3,2,1,0:T(8,128)S(1)}, u32[]{:S(2)}, u32[]{:S(2)}) collective-permute-start(f32[2,8,64,128]{3,2,1,0:T(8,128)S(1)} %pad_maximum_fusion.refs_0_), channel_id=1, source_target_pairs={{0,96},{32,0},{64,32},{96,64},{1,97},{33,1},{65,33},{97,65},{2,98}... | collective-permute-start | bytes 1572872 | tf_op jit(solution)/shard_map/ppermute | solution.py:301
  205.7 12.6 %collective-permute-start.2 = (f32[1,8,64,128]{3,2,1,0:T(8,128)S(1)}, f32[1,8,64,128]{3,2,1,0:T(8,128)S(1)}, u32[]{:S(2)}, u32[]{:S(2)}) collective-permute-start(f32[1,8,64,128]{3,2,1,0:T(8,128)S(1)} %bitcast.42), channel_id=1, source_target_pairs={{0,32},{32,64},{64,96},{96,0},{1,33},{33,65},{65,97},{97,1},{2,34}... | collective-permute-start | bytes 786440 | tf_op jit(solution)/shard_map/ppermute | solution.py:301
  207.6 30.8 %copy-start = (f32[2,8,64,128]{3,2,1,0:T(8,128)}, f32[2,8,64,128]{3,2,1,0:T(8,128)S(1)}, u32[]{:S(2)}) copy-start(f32[2,8,64,128]{3,2,1,0:T(8,128)S(1)} %collective-permute-done.3.refs_1_) | copy-start | bytes 1572868
  207.6 17.0 %collective-permute-start.1 = (f32[1,8,64,128]{3,2,1,0:T(8,128)S(1)}, f32[1,8,64,128]{3,2,1,0:T(8,128)S(1)}, u32[]{:S(2)}, u32[]{:S(2)}) collective-permute-start(f32[1,8,64,128]{3,2,1,0:T(8,128)S(1)} %bitcast.43), channel_id=1, source_target_pairs={{0,64},{32,96},{64,0},{96,32},{1,65},{33,97},{65,1},{97,33},{2,66}... | collective-permute-start | bytes 786440 | tf_op jit(solution)/shard_map/ppermute | solution.py:301
  211.5 26.9 %collective-permute-start = (f32[1,8,64,128]{3,2,1,0:T(8,128)S(1)}, f32[1,8,64,128]{3,2,1,0:T(8,128)S(1)}, u32[]{:S(2)}, u32[]{:S(2)}) collective-permute-start(f32[1,8,64,128]{3,2,1,0:T(8,128)S(1)} %bitcast.44), channel_id=1, source_target_pairs={{0,96},{32,0},{64,32},{96,64},{1,97},{33,1},{65,33},{97,65},{2,98}... | collective-permute-start | bytes 786440 | tf_op jit(solution)/shard_map/ppermute | solution.py:301
  224.6 0.7 copy-start.2
  238.4 0.7 copy-start.4
  239.2 1.0 copy-start.1
  240.2 7.3 %copy-start.3 = (f32[1,8,64,128]{3,2,1,0:T(8,128)S(1)}, f32[1,8,64,128]{3,2,1,0:T(8,128)}, u32[]{:S(2)}) copy-start(f32[1,8,64,128]{3,2,1,0:T(8,128)} %copy-done.2) | copy-start | bytes 786436
  240.2 7.3 %copy-start.5 = (f32[1,8,64,128]{3,2,1,0:T(8,128)S(1)}, f32[1,8,64,128]{3,2,1,0:T(8,128)}, u32[]{:S(2)}) copy-start(f32[1,8,64,128]{3,2,1,0:T(8,128)} %copy-done.4) | copy-start | bytes 786436
Sparse Core Ops, SparseCore 0:
  30.5 53.3 all-gather.2
  86.1 64.4 all-gather.4

commit v6 on v5

--- a/solution.py
+++ b/solution.py
@@ -6,7 +6,6 @@
 from jax.sharding import Mesh, PartitionSpec as P
 
 QUADS = 4
-BATCHES = ((0, 1), (2,))
 RHS = ("z", "core")
 GROUP = ("yp", "x")
 F32 = jnp.float32
@@ -152,44 +151,53 @@
         heads_out[b] = heads_ref[base + b + 1] - dot(x, lines_ref[b], NN)
 
 
-def stacked(x_refs):
-    if len(x_refs) == 1:
-        parts = [x_refs[0][s].reshape(-1, x_refs[0].shape[-1]) for s in range(2)]
-    else:
-        parts = [jnp.concatenate([x[0, s] for x in x_refs], axis=0) for s in range(2)]
-    return jnp.concatenate(parts, axis=1)
-
-
-def trail_sum(n, *refs):
-    x_refs, f_ref, out_ref = refs[:n], refs[n], refs[-1]
-
+def others(quad_ref, got_ref, out_ref):
+    copies, panels, turns = out_ref.shape[:3]
+    quads = got_ref.shape[0]
+    for t in range(turns):
+        q = lax.rem(quad_ref[0] + (t + 1), quads)
+        for k in range(panels):
+            block = got_ref[q, k]
+            for c in range(copies):
+                out_ref[c, k, t] = block
+
+
+def last_copies(panel, got_ref, out_ref):
+    for c in range(out_ref.shape[0]):
+        for q in range(got_ref.shape[0]):
+            out_ref[c, q] = got_ref[q, panel]
+
+
+def trail_sum(own_ref, x_ref, f_ref, out_ref):
     @pl.when(pl.program_id(0) == 0)
     def _():
-        out_ref[...] = jnp.zeros_like(out_ref) if len(refs) == n + 2 else refs[n + 1][...]
-
-    out_ref[...] += dot(stacked(x_refs), f_ref[0, 0], NN)
-
-
-def finish(panel, x_ref, f_hbm, sum_ref, quad_ref, r_hbm, *refs):
-    own_refs, (out_ref, mine_ref, turned_ref, f_ref, r_ref, sems) = refs[:-6], refs[-6:]
+        out_ref[...] = jnp.zeros_like(out_ref)
+
+    parts = []
+    for s in range(2):
+        turns = [x_ref[s, 0, t] for t in range(x_ref.shape[2])]
+        parts.append(jnp.concatenate([own_ref[0, s], *turns], axis=0))
+    out_ref[...] += dot(jnp.concatenate(parts, axis=1), f_ref[0, 0], NN)
+
+
+def finish(panel, x_ref, f_hbm, sum_ref, quad_ref, r_hbm, own_ref, *refs):
+    out_ref, mine_ref, turned_ref, f_ref, r_ref, sems = refs
     n = f_ref.shape[0]
     copies = [
         pltpu.make_async_copy(f_hbm.at[panel, b], f_ref.at[b], sems.at[b]) for b in range(n)
     ]
     for c in copies:
         c.start()
-    width = mine_ref.shape[0] // len(own_refs)
+    quads, panels, per, _ = own_ref.shape
+    width = mine_ref.shape[0] // panels
     rows = pltpu.make_async_copy(
         r_hbm.at[pl.ds(mine_ref.shape[0], r_ref.shape[0])], r_ref, sems.at[n]
     )
     rows.start()
     quad = quad_ref[0]
-    quads, per, _ = own_refs[0].shape
     at = pl.multiple_of(quad * width, width)
-    for k, own_ref in enumerate(own_refs):
-        shift = quads - quad if k < panel else 0
-        own = [own_ref[lax.rem(q + shift, quads)] for q in range(quads)]
-        turned_ref[...] = jnp.concatenate(own, axis=0).T
+    for k in range(panels):
+        turned_ref[...] = jnp.concatenate([own_ref[q, k] for q in range(quads)], axis=0).T
         mine_ref[k * width : (k + 1) * width] = turned_ref[pl.ds(at, width)]
     total = jnp.concatenate(
         [
@@ -200,34 +208,10 @@
     )
     for b, c in enumerate(copies):
         c.wait()
-        total += dot(stacked([x_ref.at[pl.ds(2 * b, 2)]]), f_ref[b], NN)
+        x = [x_ref[2 * b + s].reshape(-1, x_ref.shape[3]) for s in range(2)]
+        total += dot(jnp.concatenate(x, axis=1), f_ref[b], NN)
     rows.wait()
     out_ref[...] = r_ref[...] - total.T
-
-
-def trail_call(kernel, x, f, k, out_shape, extra=(), specs=(), steps=1, scratch=()):
-    per_pair = f.shape[2] // 256
-    per_panel = f.shape[1] * per_pair
-    if len(x) == 1:
-        x_specs = [pl.BlockSpec((2, *x[0].shape[1:]), lambda i: (i % per_panel, 0, 0, 0))]
-    else:
-        x_specs = [
-            pl.BlockSpec((1, 2, *p.shape[2:]), lambda i: (i // per_panel, i % per_panel, 0, 0))
-            for p in x
-        ]
-    f_spec = pl.BlockSpec(
-        (1, 1, 256, f.shape[3]),
-        lambda i: (k + i // per_panel, (i % per_panel) // per_pair, i % per_pair, 0),
-    )
-    return pl.pallas_call(
-        kernel,
-        out_shape=jax.ShapeDtypeStruct(out_shape, F32),
-        grid=(steps * per_panel,),
-        in_specs=[*x_specs, f_spec, *specs],
-        out_specs=whole(out_shape),
-        scratch_shapes=scratch,
-        compiler_params=pltpu.CompilerParams(vmem_limit_bytes=16 << 20),
-    )(*x, in_hbm(f), *extra)
 
 
 def spread(array, axes):
@@ -273,36 +257,21 @@
     )(got)
     first = lax.all_to_all(first, RHS, 0, 0, tiled=True)
     rest = lax.all_gather(pay, RHS, axis=2, tiled=True)
+    trail = lower[:, :, tail:].reshape(panels, npair, half, -1)
+    trail = lax.all_gather(trail, RHS, axis=2, tiled=True)
     rest = rest.reshape(9, group * rows, rows)
 
     (y,) = call(begin, [(group, per, rows)], [VMEM, VMEM])(heads, first)
     length = lower.shape[2] - tail
-    place = lax.axis_index("yp") * nx + lax.axis_index("x")
-    own, waiting, sent = {}, [], []
-    trail = total = None
+    mine, solved = [], []
     for k in range(panels):
         got = lax.all_to_all(y, GROUP, 0, 0, tiled=True)
-        copies = group if k < panels - 1 else quads
-        (mine,) = call(add_up, [(copies, per, rows)], [VMEM])(got)
-        if k == 0:
-            lower, mine = lax.optimization_barrier((lower, mine))
-            trail = lower[:, :, tail:].reshape(panels, npair, half, -1)
-            trail = lax.all_gather(trail, RHS, axis=2, tiled=True)
+        copies = group if k < panels - 1 else 1
+        (copied,) = call(add_up, [(copies, per, rows)], [VMEM])(got)
+        mine.append(copied[0])
         if k == panels - 1:
-            mine = lax.all_to_all(mine, "yq", 0, 0, tiled=True)
-            own[k] = mine
-            solved = spread(mine, GROUP)
             break
-        solved = lax.all_to_all(mine, GROUP, 0, 0, tiled=True)
-        waiting.append(solved)
-        if len(sent) < len(BATCHES) and BATCHES[len(sent)][-1] == k:
-            batch = jnp.stack(waiting)
-            parts = [batch] + [
-                lax.ppermute(batch, "yq", [(i, (i - t) % quads) for i in range(quads)])
-                for t in range(1, quads)
-            ]
-            sent.append(parts)
-            waiting = []
+        solved.append(lax.all_to_all(copied, GROUP, 0, 0, tiled=True))
         left = panels - 1 - k
         at = {3: 3, 2: 6, 1: 8}[left]
         one = pltpu.VMEM((group * rows, rows), F32)
@@ -311,7 +280,7 @@
             [(group, per, rows)],
             [VMEM, VMEM, HBM],
             [one, one, pltpu.SemaphoreType.DMA((2,))],
-        )(solved, heads, in_hbm(rest))
+        )(solved[k], heads, in_hbm(rest))
         if left > 1:
             (heads,) = call(
                 lambda *refs, at=at, k=k: follow(int(k == 0), at + 1, *refs),
@@ -321,35 +290,47 @@
                     pltpu.VMEM((left - 1, group * rows, rows), F32),
                     pltpu.SemaphoreType.DMA,
                 ],
-            )(solved, heads, in_hbm(rest))
-
-    for batch, parts in zip(BATCHES, sent):
-        total = add_trail(parts, trail, batch[0], len(batch), total)
-        here = [lax.dynamic_index_in_dim(p, place, 1, keepdims=False) for p in parts]
-        for n, k in enumerate(batch):
-            own[k] = jnp.stack([p[n] for p in here])
+            )(solved[k], heads, in_hbm(rest))
+
+    own = spread(jnp.stack(mine), "yq")
+    (sent,) = call(others, [(group, panels - 1, quads - 1, per, rows)], [SMEM, VMEM])(index, own)
+    early = lax.all_to_all(sent, GROUP, 0, 0, tiled=True)
+    own, early = lax.optimization_barrier((own, early))
+    (sent,) = call(lambda *refs: last_copies(panels - 1, *refs), [(group, quads, per, rows)], [VMEM])(own)
+    late = lax.all_to_all(sent, GROUP, 0, 0, tiled=True)
+
+    per_pair = trail.shape[2] // (2 * rows)
+    per_panel = npair * per_pair
+    total = pl.pallas_call(
+        trail_sum,
+        out_shape=jax.ShapeDtypeStruct((count, length), F32),
+        grid=((panels - 1) * per_panel,),
+        in_specs=[
+            pl.BlockSpec((1, 2, per, rows), lambda i: (i // per_panel, i % per_panel, 0, 0)),
+            pl.BlockSpec(
+                (2, 1, quads - 1, per, rows), lambda i: (i % per_panel, i // per_panel, 0, 0, 0)
+            ),
+            pl.BlockSpec(
+                (1, 1, 2 * rows, length),
+                lambda i: (i // per_panel, (i % per_panel) // per_pair, i % per_pair, 0),
+            ),
+        ],
+        out_specs=whole((count, length)),
+        compiler_params=pltpu.CompilerParams(vmem_limit_bytes=16 << 20),
+    )(in_hbm(jnp.stack(solved)), early, in_hbm(trail))
     flat = trail.reshape(panels, -1, 2 * rows, length)
     out, mine = call(
         lambda *refs: finish(panels - 1, *refs),
         [(length, count), (tail, count)],
-        [VMEM, HBM, VMEM, SMEM, HBM] + [VMEM] * panels,
+        [VMEM, HBM, VMEM, SMEM, HBM, VMEM],
         [
             pltpu.VMEM((rows, count), F32),
             pltpu.VMEM(flat.shape[1:], F32),
             pltpu.VMEM((length, count), F32),
             pltpu.SemaphoreType.DMA((flat.shape[1] + 1,)),
         ],
-    )(solved, in_hbm(flat), total, index, in_hbm(current), *[own[k] for k in range(panels)])
+    )(late, in_hbm(flat), total, index, in_hbm(current), own)
     return (mine[None], out[None])
-
-
-def add_trail(parts, trail, k, steps, total):
-    shape = (len(parts) * parts[0].shape[2], trail.shape[3])
-    more = () if total is None else (total,)
-    return trail_call(
-        lambda *refs: trail_sum(len(parts), *refs), parts, trail, k, shape,
-        more, (whole(shape),) * len(more), steps,
-    )
 
 
 def solution(mesh):

time: 264 us -> 222 us (0.84)
  the two profiles are of different devices: /device:TPU:23 before, /device:TPU:2 now
where the time goes in v6:
time: 222 us; the launch traced here: 221 us
  blocking collectives  122 us (55%)
  Pallas kernels  29.6 us (13%)
  starting transfers between devices  24.9 us (11%)
  waiting for transfers between devices  23.5 us (11%)
  between operations  14.2 us (6%)
  local copies, waits for them, and re-layouts  5.37 us (2%)
    all_to_all x3, blocking collectives, body(): got = lax.all_to_all(y, GROUP, 0, 0, tiled=True)  31.8 us
    all_to_all x1, blocking collectives, body(): first = lax.all_to_all(first, RHS, 0, 0, tiled=True)  30.3 us
    all_to_all x1, blocking collectives, body(): early = lax.all_to_all(sent, GROUP, 0, 0, tiled=True)  26.3 us
    all_to_all x1, blocking collectives, body(): got = lax.all_to_all(sent, 'yq', 0, 0, tiled=True)  22 us
    all_to_all x1, waiting for transfers between devices, spread(): lax.all_to_all(jnp.broadcast_to(array[None], (lax.axis_size(axes), *array...  11.6 us
    all_to_all x1, blocking collectives, body(): solved.append(lax.all_to_all(copied, GROUP, 0, 0, tiled=True))  11.2 us
    pallas_call x1, Pallas kernels, body(): pl.pallas_call(trail_sum, out_shape=jax.ShapeDtypeStruct((count, length),...  10.7 us
    all_to_all x2, starting transfers between devices, body(): solved.append(lax.all_to_all(copied, GROUP, 0, 0, tiled=True))  10.3 us
  transfers between devices with their start and end apart: 7, of which 4 were waited for; matrix products, arithmetic and copies ran while one was open for 3% of the time, Pallas kernels for 10%

profile of v6, /device:TPU:2, one launch (start us, length us, event | category | flops | bytes accessed | tf_op | source)
XLA Modules:
  0.0 221.1 jit_solution(16802372919779669538)
XLA Ops:
  7.2 0.0 all-gather.3.cloned.1.call-start
  7.2 1.2 shard_map.50
  8.5 22.0 %all_to_all.60.refs_0_ = f32[4,224,128]{2,1,0:T(8,128)S(1)} all-to-all(f32[4,224,128]{2,1,0:T(8,128)S(1)} %shard_map.50), channel_id=1, replica_groups=mesh['x'=4,'yq'=4,'yp'=2,'z'=8,'core'=2] {'yq'}, dimensions={0} | all-to-all | bytes 917504 | tf_op jit(solution)/shard_map/all_to_all | solution.py:252
  30.5 1.1 shard_map.51
  31.6 0.0 all-gather.3.cloned.1.call-update
  31.6 0.0 all-gather.5.cloned.1.call-start
  31.7 2.0 slice.19
  33.7 0.0 all-gather.5.cloned.1.call-update
  33.7 30.3 %all_to_all.61.first_ref = f32[16,2,32,128]{3,2,1,0:T(8,128)S(1)} all-to-all(f32[16,2,32,128]{3,2,1,0:T(8,128)S(1)} %get-tuple-element.10), channel_id=1, replica_groups=mesh['x'=4,'yq'=4,'yp'=2,'z'=8,'core'=2] {'z','core'}, dimensions={0} | all-to-all | bytes 1048576 | tf_op jit(solution)/shard_map/all_to_all | solution.py:258
  64.0 0.4 shard_map.52
  64.4 10.8 %all_to_all.62.got_ref = f32[8,64,128]{2,1,0:T(8,128)S(1)} all-to-all(f32[8,64,128]{2,1,0:T(8,128)S(1)} %shard_map.52), channel_id=1, replica_groups=mesh['x'=4,'yq'=4,'yp'=2,'z'=8,'core'=2] {'yp','x'}, dimensions={0} | all-to-all | bytes 524288 | tf_op jit(solution)/shard_map/all_to_all | solution.py:268
  75.3 11.2 %all_to_all.63.refs_0_ = f32[8,64,128]{2,1,0:T(8,128)S(1)} all-to-all(f32[8,64,128]{2,1,0:T(8,128)S(1)} %shard_map.53), channel_id=1, replica_groups=mesh['x'=4,'yq'=4,'yp'=2,'z'=8,'core'=2] {'yp','x'}, dimensions={0} | all-to-all | bytes 524288 | tf_op jit(solution)/shard_map/all_to_all | solution.py:274
  86.4 0.0 all-gather.3.cloned.1.call-done
  86.4 1.7 shard_map.54
  88.2 11.1 %all_to_all.64.got_ref = f32[8,64,128]{2,1,0:T(8,128)S(1)} all-to-all(f32[8,64,128]{2,1,0:T(8,128)S(1)} %shard_map.54), channel_id=1, replica_groups=mesh['x'=4,'yq'=4,'yp'=2,'z'=8,'core'=2] {'yp','x'}, dimensions={0} | all-to-all | bytes 524288 | tf_op jit(solution)/shard_map/all_to_all | solution.py:268
  99.3 0.7 shard_map.55
  100.0 5.1 %all-to-all-start.5 = ((f32[8,64,128]{2,1,0:T(8,128)}), f32[8,64,128]{2,1,0:T(8,128)S(1)}, u32[]{:S(2)}, u32[]{:S(2)}) async-start(f32[8,64,128]{2,1,0:T(8,128)} %shard_map.55), calls=%async_computation.5 | async-start | bytes 524288 | tf_op jit(solution)/shard_map/all_to_all | solution.py:274
  105.2 1.6 shard_map.56.refs_1_
  106.8 3.8 %all-to-all-done.5.refs_0_ = f32[8,64,128]{2,1,0:T(8,128)S(1)} async-done(((f32[8,64,128]{2,1,0:T(8,128)}), f32[8,64,128]{2,1,0:T(8,128)S(1)}, u32[]{:S(2)}, u32[]{:S(2)}) %all-to-all-start.5) | async-done | bytes 262176 | tf_op jit(solution)/shard_map/all_to_all | solution.py:274
  110.6 1.7 shard_map.57
  112.3 9.8 %all_to_all.65.got_ref = f32[8,64,128]{2,1,0:T(8,128)S(1)} all-to-all(f32[8,64,128]{2,1,0:T(8,128)S(1)} %shard_map.57), channel_id=1, replica_groups=mesh['x'=4,'yq'=4,'yp'=2,'z'=8,'core'=2] {'yp','x'}, dimensions={0} | all-to-all | bytes 524288 | tf_op jit(solution)/shard_map/all_to_all | solution.py:268
  122.1 0.7 shard_map.58
  122.9 5.1 %all-to-all-start.7 = ((f32[8,64,128]{2,1,0:T(8,128)}), f32[8,64,128]{2,1,0:T(8,128)S(1)}, u32[]{:S(2)}, u32[]{:S(2)}) async-start(f32[8,64,128]{2,1,0:T(8,128)} %shard_map.58), calls=%async_computation.7 | async-start | bytes 524288 | tf_op jit(solution)/shard_map/all_to_all | solution.py:274
  128.0 1.3 shard_map.59.refs_1_
  129.3 4.1 %all-to-all-done.7.refs_0_ = f32[8,64,128]{2,1,0:T(8,128)S(1)} async-done(((f32[8,64,128]{2,1,0:T(8,128)}), f32[8,64,128]{2,1,0:T(8,128)S(1)}, u32[]{:S(2)}, u32[]{:S(2)}) %all-to-all-start.7) | async-done | bytes 262176 | tf_op jit(solution)/shard_map/all_to_all | solution.py:274
  133.4 0.0 copy-start.1
  133.4 2.5 %shard_map.60 = f32[8,64,128]{2,1,0:T(8,128)} custom-call(f32[8,64,128]{2,1,0:T(8,128)S(1)} %all-to-all-done.7.refs_0_, f32[1,64,128]{2,1,0:T(8,128)S(1)} %shard_map.59.refs_1_, f32[9,1024,128]{2,1,0:T(8,128)} %bitcast.23), custom_call_target="tpu_custom_call" | custom-call | tf_op jit(solution)/shard_map/pallas_call | solution.py:278
  136.0 5.1 %all-to-all-start.8 = ((f32[8,64,128]{2,1,0:T(8,128)}), f32[8,64,128]{2,1,0:T(8,128)S(1)}, u32[]{:S(2)}, u32[]{:S(2)}) async-start(f32[8,64,128]{2,1,0:T(8,128)} %shard_map.60), calls=%async_computation.8 | async-start | bytes 524288 | tf_op jit(solution)/shard_map/all_to_all | solution.py:268
  141.1 0.8 slice.17
  141.9 0.8 slice.18
  142.6 3.9 %all-to-all-done.8.got_ref = f32[8,64,128]{2,1,0:T(8,128)S(1)} async-done(((f32[8,64,128]{2,1,0:T(8,128)}), f32[8,64,128]{2,1,0:T(8,128)S(1)}, u32[]{:S(2)}, u32[]{:S(2)}) %all-to-all-start.8) | async-done | bytes 262176 | tf_op jit(solution)/shard_map/all_to_all | solution.py:268
  146.6 0.8 broadcast_in_dim.12
  147.4 0.0 copy-done.1
  147.4 3.5 %all-to-all-start.9 = ((f32[4,4,64,128]{3,2,1,0:T(8,128)}), f32[4,4,64,128]{3,2,1,0:T(8,128)S(1)}, u32[]{:S(2)}, u32[]{:S(2)}) async-start(f32[4,4,64,128]{3,2,1,0:T(8,128)} %broadcast_in_dim.12), calls=%async_computation.9 | async-start | bytes 1048576 | tf_op jit(solution)/shard_map/all_to_all | solution.py:218
  150.9 11.6 %all-to-all-done.9.got_ref.refs_0_.refs_5_ = f32[4,4,64,128]{3,2,1,0:T(8,128)S(1)} async-done(((f32[4,4,64,128]{3,2,1,0:T(8,128)}), f32[4,4,64,128]{3,2,1,0:T(8,128)S(1)}, u32[]{:S(2)}, u32[]{:S(2)}) %all-to-all-start.9) | async-done | bytes 524320 | tf_op jit(solution)/shard_map/all_to_all | solution.py:218
  162.5 0.2 shard_map.62
  162.7 26.3 %all_to_all.66.x_ref = f32[8,3,3,64,128]{4,3,2,1,0:T(8,128)S(1)} all-to-all(f32[8,3,3,64,128]{4,3,2,1,0:T(8,128)S(1)} %shard_map.62), channel_id=1, replica_groups=mesh['x'=4,'yq'=4,'yp'=2,'z'=8,'core'=2] {'yp','x'}, dimensions={0} | all-to-all | bytes 4718592 | tf_op jit(solution)/shard_map/all_to_all | solution.py:297
  189.0 0.1 shard_map.63
  189.0 0.0 copy-start
  189.1 1.0 copy-done
  190.1 6.0 %all-to-all-start.11 = ((f32[8,4,64,128]{3,2,1,0:T(8,128)}), f32[8,4,64,128]{3,2,1,0:T(8,128)}, u32[]{:S(2)}, u32[]{:S(2)}) async-start(f32[8,4,64,128]{3,2,1,0:T(8,128)} %copy-done), calls=%async_computation.11 | async-start | bytes 2097152 | tf_op jit(solution)/shard_map/all_to_all | solution.py:300
  196.0 2.0 pad_maximum_fusion.own_ref
  198.0 0.0 all-gather.5.cloned.1.call-done.f_ref
  198.0 10.7 %shard_map.64.refs_2_ = f32[256,576]{1,0:T(8,128)S(1)} custom-call(f32[3,8,64,128]{3,2,1,0:T(8,128)} %pad_maximum_fusion.own_ref, f32[8,3,3,64,128]{4,3,2,1,0:T(8,128)S(1)} %all_to_all.66.x_ref, f32[4,2,512,576]{3,2,1,0:T(8,128)} %all-gather.5.cloned.1.call-done.f_ref), custom_call_target="tpu_custom_call" | custom-call | tf_op jit(solution)/shard_map/pallas_call | solution.py:304
  208.7 0.0 all-to-all-done.11.refs_0_
  208.7 5.5 %shard_map.65 = (f32[576,256]{1,0:T(8,128)}, f32[128,256]{1,0:T(8,128)}) custom-call(f32[8,4,64,128]{3,2,1,0:T(8,128)} %all-to-all-done.11.refs_0_, f32[4,4,256,576]{3,2,1,0:T(8,128)} %bitcast.24, f32[256,576]{1,0:T(8,128)S(1)} %shard_map.64.refs_2_, s32[1]{0:T(128)} %bitcast.6.quad_ref.refs_3_, f32[704,256]{1,0:T(8,128)} %bitcast.26, ...), custom_call_target="tpu_custom_call" | custom-call | tf_op jit(solution)/shard_map/pallas_call | solution.py:322
  (4 shorter events, 0.1 us)
Async XLA Ops:
  7.2 79.3 %all-gather.3.cloned.1.call-start = ((), (), s32[]{:S(2)}) async-start(), calls=%async_computation.12 | async-start | bytes 5013504 | tf_op jit(solution)/shard_map/all_gather | solution.py:259
  31.6 166.3 %all-gather.5.cloned.1.call-start = ((), (), s32[]{:S(2)}) async-start(), calls=%async_computation.13 | async-start | bytes 11141120 | tf_op jit(solution)/shard_map/all_gather | solution.py:261
  100.0 10.6 %all-to-all-start.5 = ((f32[8,64,128]{2,1,0:T(8,128)}), f32[8,64,128]{2,1,0:T(8,128)S(1)}, u32[]{:S(2)}, u32[]{:S(2)}) async-start(f32[8,64,128]{2,1,0:T(8,128)} %shard_map.55), calls=%async_computation.5 | async-start | bytes 524288 | tf_op jit(solution)/shard_map/all_to_all | solution.py:274
  122.9 10.6 %all-to-all-start.7 = ((f32[8,64,128]{2,1,0:T(8,128)}), f32[8,64,128]{2,1,0:T(8,128)S(1)}, u32[]{:S(2)}, u32[]{:S(2)}) async-start(f32[8,64,128]{2,1,0:T(8,128)} %shard_map.58), calls=%async_computation.7 | async-start | bytes 524288 | tf_op jit(solution)/shard_map/all_to_all | solution.py:274
  133.4 14.0 %copy-start.1 = (f32[8,64,128]{2,1,0:T(8,128)}, f32[8,64,128]{2,1,0:T(8,128)S(1)}, u32[]{:S(2)}) copy-start(f32[8,64,128]{2,1,0:T(8,128)S(1)} %all-to-all-done.7.refs_0_) | copy-start | bytes 786436
  136.0 10.6 %all-to-all-start.8 = ((f32[8,64,128]{2,1,0:T(8,128)}), f32[8,64,128]{2,1,0:T(8,128)S(1)}, u32[]{:S(2)}, u32[]{:S(2)}) async-start(f32[8,64,128]{2,1,0:T(8,128)} %shard_map.60), calls=%async_computation.8 | async-start | bytes 524288 | tf_op jit(solution)/shard_map/all_to_all | solution.py:268
  147.4 15.1 %all-to-all-start.9 = ((f32[4,4,64,128]{3,2,1,0:T(8,128)}), f32[4,4,64,128]{3,2,1,0:T(8,128)S(1)}, u32[]{:S(2)}, u32[]{:S(2)}) async-start(f32[4,4,64,128]{3,2,1,0:T(8,128)} %broadcast_in_dim.12), calls=%async_computation.9 | async-start | bytes 1048576 | tf_op jit(solution)/shard_map/all_to_all | solution.py:218
  189.0 1.0 copy-start
  190.1 18.6 %all-to-all-start.11 = ((f32[8,4,64,128]{3,2,1,0:T(8,128)}), f32[8,4,64,128]{3,2,1,0:T(8,128)}, u32[]{:S(2)}, u32[]{:S(2)}) async-start(f32[8,4,64,128]{3,2,1,0:T(8,128)} %copy-done), calls=%async_computation.11 | async-start | bytes 2097152 | tf_op jit(solution)/shard_map/all_to_all | solution.py:300
Sparse Core Ops, SparseCore 0:
  31.8 54.5 all-gather.2
  88.5 63.6 all-gather.4

commit v7 on v6

--- a/solution.py
+++ b/solution.py
@@ -105,19 +105,33 @@
             first_ref[c, h] = piece
 
 
-def begin(head_ref, first_ref, out_ref):
-    blocks, pair, half, rows = first_ref.shape
+def begin(core_ref, head_ref, mine_ref, other_ref, out_ref):
+    n, pair, half, rows = mine_ref.shape
     head = head_ref[0]
+    even = core_ref[0] == 0
     for p in range(pair):
-        block = first_ref[:, p].reshape(blocks * half, rows)
-        y = dot(head, block, NT)
-        n = blocks * half // rows
-        for x in range(n):
-            out_ref[p * n + x] = y[:, x * rows : (x + 1) * rows]
-
-
-def add_up(got_ref, out_ref):
+        mine, other = mine_ref[:, p], other_ref[:, p]
+        low = jnp.where(even, mine, other)
+        high = jnp.where(even, other, mine)
+        block = jnp.concatenate([low[:, None], high[:, None]], axis=1)
+        y = dot(head, block.reshape(2 * n * half, rows), NT)
+        m = 2 * n * half // rows
+        for x in range(m):
+            out_ref[p * m + x] = y[:, x * rows : (x + 1) * rows]
+
+
+def add_all(got_ref, *refs):
+    mine_refs, out_ref = refs[:-1], refs[-1]
     total = jnp.sum(got_ref[...], axis=0)
+    for c in range(out_ref.shape[0]):
+        for k, mine_ref in enumerate(mine_refs):
+            out_ref[c, k] = mine_ref[...]
+        out_ref[c, len(mine_refs)] = total
+
+
+def add_up(got_ref, out_ref, mine_ref):
+    total = jnp.sum(got_ref[...], axis=0)
+    mine_ref[...] = total
     for c in range(out_ref.shape[0]):
         out_ref[c] = total
 
@@ -168,56 +182,65 @@
             out_ref[c, q] = got_ref[q, panel]
 
 
-def trail_sum(own_ref, x_ref, f_ref, out_ref):
-    @pl.when(pl.program_id(0) == 0)
+def trail_sum(steps, *refs):
+    own_refs, (x_ref, f_ref, out_ref) = refs[:-3], refs[-3:]
+    step = pl.program_id(0)
+
+    @pl.when(step == 0)
     def _():
         out_ref[...] = jnp.zeros_like(out_ref)
 
-    parts = []
-    for s in range(2):
-        turns = [x_ref[s, 0, t] for t in range(x_ref.shape[2])]
-        parts.append(jnp.concatenate([own_ref[0, s], *turns], axis=0))
-    out_ref[...] += dot(jnp.concatenate(parts, axis=1), f_ref[0, 0], NN)
-
-
-def finish(panel, x_ref, f_hbm, sum_ref, quad_ref, r_hbm, own_ref, *refs):
-    out_ref, mine_ref, turned_ref, f_ref, r_ref, sems = refs
+    for k, own_ref in enumerate(own_refs):
+
+        @pl.when(step // steps == k)
+        def _():
+            parts = []
+            for s in range(2):
+                turns = [x_ref[s, 0, t] for t in range(x_ref.shape[2])]
+                parts.append(jnp.concatenate([own_ref[2 * (step % steps) + s], *turns], axis=0))
+            out_ref[...] += dot(jnp.concatenate(parts, axis=1), f_ref[0, 0], NN)
+
+
+def finish(panel, x_hbm, f_hbm, sum_hbm, quad_ref, r_hbm, own_ref, *refs):
+    out_ref, mine_ref, turned_ref, f_ref, x_ref, sum_ref, r_ref, sems = refs
     n = f_ref.shape[0]
-    copies = [
-        pltpu.make_async_copy(f_hbm.at[panel, b], f_ref.at[b], sems.at[b]) for b in range(n)
-    ]
-    for c in copies:
-        c.start()
     quads, panels, per, _ = own_ref.shape
     width = mine_ref.shape[0] // panels
+    copies = []
+    for b in range(n):
+        pair = pl.ds(2 * b, 2)
+        copies += [
+            pltpu.make_async_copy(x_hbm.at[pair], x_ref.at[pair], sems.at[2 * b]),
+            pltpu.make_async_copy(f_hbm.at[panel, b], f_ref.at[b], sems.at[2 * b + 1]),
+        ]
+    sums = pltpu.make_async_copy(sum_hbm, sum_ref, sems.at[2 * n])
     rows = pltpu.make_async_copy(
-        r_hbm.at[pl.ds(mine_ref.shape[0], r_ref.shape[0])], r_ref, sems.at[n]
+        r_hbm.at[pl.ds(mine_ref.shape[0], r_ref.shape[0])], r_ref, sems.at[2 * n + 1]
     )
-    rows.start()
+    for c in (*copies, sums, rows):
+        c.start()
     quad = quad_ref[0]
     at = pl.multiple_of(quad * width, width)
     for k in range(panels):
         turned_ref[...] = jnp.concatenate([own_ref[q, k] for q in range(quads)], axis=0).T
         mine_ref[k * width : (k + 1) * width] = turned_ref[pl.ds(at, width)]
-    total = jnp.concatenate(
+    total = None
+    for b in range(n):
+        copies[2 * b].wait()
+        copies[2 * b + 1].wait()
+        x = [x_ref[2 * b + s].reshape(-1, x_ref.shape[3]) for s in range(2)]
+        product = dot(jnp.concatenate(x, axis=1), f_ref[b], NN)
+        total = product if b == 0 else total + product
+    sums.wait()
+    total += jnp.concatenate(
         [
             sum_ref[pl.ds(pl.multiple_of(lax.rem(q + quads - quad, quads) * per, per), per)]
             for q in range(quads)
         ],
         axis=0,
     )
-    for b, c in enumerate(copies):
-        c.wait()
-        x = [x_ref[2 * b + s].reshape(-1, x_ref.shape[3]) for s in range(2)]
-        total += dot(jnp.concatenate(x, axis=1), f_ref[b], NN)
     rows.wait()
     out_ref[...] = r_ref[...] - total.T
-
-
-def spread(array, axes):
-    return lax.all_to_all(
-        jnp.broadcast_to(array[None], (lax.axis_size(axes), *array.shape)), axes, 0, 0, tiled=True
-    )
 
 
 def body(factor, inverses, right_side):
@@ -250,27 +273,29 @@
         ],
     )(in_hbm(lower), in_hbm(inv), in_hbm(current))
     got = lax.all_to_all(sent, "yq", 0, 0, tiled=True)
+    trail = lower[:, :, tail:].reshape(panels, npair, half, -1)
+    got, trail = lax.optimization_barrier((got, trail))
     heads, pay, first = call(
         lambda *refs: sort(width, per, *refs),
-        [(panels, per, rows), (9, npair, half, rows), (blocks, npair, half, rows)],
+        [(panels, per, rows), (9, npair, half, rows), (blocks // 2, npair, half, rows)],
         [VMEM],
     )(got)
-    first = lax.all_to_all(first, RHS, 0, 0, tiled=True)
+    first = lax.all_to_all(first, "z", 0, 0, tiled=True)
+    other = lax.ppermute(first, "core", [(0, 1), (1, 0)])
+    core = lax.axis_index("core").reshape(1).astype(jnp.int32)
     rest = lax.all_gather(pay, RHS, axis=2, tiled=True)
-    trail = lower[:, :, tail:].reshape(panels, npair, half, -1)
     trail = lax.all_gather(trail, RHS, axis=2, tiled=True)
     rest = rest.reshape(9, group * rows, rows)
 
-    (y,) = call(begin, [(group, per, rows)], [VMEM, VMEM])(heads, first)
+    (y,) = call(begin, [(group, per, rows)], [SMEM, VMEM, VMEM, VMEM])(core, heads, first, other)
     length = lower.shape[2] - tail
     mine, solved = [], []
     for k in range(panels):
         got = lax.all_to_all(y, GROUP, 0, 0, tiled=True)
-        copies = group if k < panels - 1 else 1
-        (copied,) = call(add_up, [(copies, per, rows)], [VMEM])(got)
-        mine.append(copied[0])
         if k == panels - 1:
             break
+        copied, single = call(add_up, [(group, per, rows), (per, rows)], [VMEM])(got)
+        mine.append(single)
         solved.append(lax.all_to_all(copied, GROUP, 0, 0, tiled=True))
         left = panels - 1 - k
         at = {3: 3, 2: 6, 1: 8}[left]
@@ -292,7 +317,8 @@
                 ],
             )(solved[k], heads, in_hbm(rest))
 
-    own = spread(jnp.stack(mine), "yq")
+    (sent,) = call(add_all, [(quads, panels, per, rows)], [VMEM] * panels)(got, *mine)
+    own = lax.all_to_all(sent, "yq", 0, 0, tiled=True)
     (sent,) = call(others, [(group, panels - 1, quads - 1, per, rows)], [SMEM, VMEM])(index, own)
     early = lax.all_to_all(sent, GROUP, 0, 0, tiled=True)
     own, early = lax.optimization_barrier((own, early))
@@ -302,11 +328,11 @@
     per_pair = trail.shape[2] // (2 * rows)
     per_panel = npair * per_pair
     total = pl.pallas_call(
-        trail_sum,
+        lambda *refs: trail_sum(per_panel, *refs),
         out_shape=jax.ShapeDtypeStruct((count, length), F32),
         grid=((panels - 1) * per_panel,),
         in_specs=[
-            pl.BlockSpec((1, 2, per, rows), lambda i: (i // per_panel, i % per_panel, 0, 0)),
+            *[whole((group, per, rows))] * (panels - 1),
             pl.BlockSpec(
                 (2, 1, quads - 1, per, rows), lambda i: (i % per_panel, i // per_panel, 0, 0, 0)
             ),
@@ -317,19 +343,21 @@
         ],
         out_specs=whole((count, length)),
         compiler_params=pltpu.CompilerParams(vmem_limit_bytes=16 << 20),
-    )(in_hbm(jnp.stack(solved)), early, in_hbm(trail))
+    )(*solved, early, in_hbm(trail))
     flat = trail.reshape(panels, -1, 2 * rows, length)
     out, mine = call(
         lambda *refs: finish(panels - 1, *refs),
         [(length, count), (tail, count)],
-        [VMEM, HBM, VMEM, SMEM, HBM, VMEM],
+        [HBM, HBM, HBM, SMEM, HBM, VMEM],
         [
             pltpu.VMEM((rows, count), F32),
             pltpu.VMEM(flat.shape[1:], F32),
+            pltpu.VMEM(late.shape, F32),
+            pltpu.VMEM(total.shape, F32),
             pltpu.VMEM((length, count), F32),
-            pltpu.SemaphoreType.DMA((flat.shape[1] + 1,)),
+            pltpu.SemaphoreType.DMA((2 * flat.shape[1] + 2,)),
         ],
-    )(late, in_hbm(flat), total, index, in_hbm(current), own)
+    )(in_hbm(late), in_hbm(flat), in_hbm(total), index, in_hbm(current), own)
     return (mine[None], out[None])
 
 

time: 222 us -> 214 us (0.964)
  blocking collectives: 122 us -> 97.2 us
  waiting for transfers between devices: 23.5 us -> 36.2 us
  starting transfers between devices: 24.9 us -> 31 us
    all_to_all x2 -> x1, blocking collectives: 52.3 us -> 20.6 us  [body(): first = lax.all_to_all(first, 'z', 0, 0, tiled=True)]
    all_to_all x3 -> x4, blocking collectives: 31.8 us -> 40.9 us  [body(): got = lax.all_to_all(y, GROUP, 0, 0, tiled=True)]
    all_to_all x2, waiting for transfers between devices: 15.5 us -> 23.7 us  [the longest x1 12.1 us: body(): got = lax.all_to_all(sent, 'yq', 0, 0, tiled=True)]
    all_to_all x2, starting transfers between devices: 8.61 us -> 12.9 us  [the longest x1 7.11 us: body(): got = lax.all_to_all(sent, 'yq', 0, 0, tiled=True)]
  transfers between devices with their start and end apart: 7 -> 8, of which waited for: 4 -> 6; matrix products, arithmetic and copies ran while one was open for 3% -> 1% of each run, Pallas kernels for 10% -> 10%
where the time goes in v7:
time: 214 us; the launch traced here: 213 us
  blocking collectives  97.2 us (45%)
  waiting for transfers between devices  36.2 us (17%)
  starting transfers between devices  31 us (14%)
  Pallas kernels  29.4 us (14%)
  between operations  14.2 us (7%)
  local copies, waits for them, and re-layouts  4.81 us (2%)
    all_to_all x4, blocking collectives, body(): got = lax.all_to_all(y, GROUP, 0, 0, tiled=True)  40.9 us
    all_to_all x1, blocking collectives, body(): early = lax.all_to_all(sent, GROUP, 0, 0, tiled=True)  25.9 us
    all_to_all x1, blocking collectives, body(): first = lax.all_to_all(first, 'z', 0, 0, tiled=True)  20.6 us
    all_to_all x1, waiting for transfers between devices, body(): got = lax.all_to_all(sent, 'yq', 0, 0, tiled=True)  12.1 us
    all_to_all x1, waiting for transfers between devices, body(): own = lax.all_to_all(sent, 'yq', 0, 0, tiled=True)  11.6 us
    pallas_call x1, Pallas kernels, body(): pl.pallas_call(lambda *refs: trail_sum(per_panel, *refs), out_shape=jax.S...  10.6 us
    all_to_all x2, starting transfers between devices, body(): solved.append(lax.all_to_all(copied, GROUP, 0, 0, tiled=True))  10.3 us
    all_to_all x1, blocking collectives, body(): solved.append(lax.all_to_all(copied, GROUP, 0, 0, tiled=True))  9.82 us
  transfers between devices with their start and end apart: 8, of which 6 were waited for; matrix products, arithmetic and copies ran while one was open for 1% of the time, Pallas kernels for 10%

profile of v7, /device:TPU:2, one launch (start us, length us, event | category | flops | bytes accessed | tf_op | source)
XLA Modules:
  0.0 212.7 jit_solution(9550817380114881195)
XLA Ops:
  7.2 2.0 shard_map.50
  9.2 7.1 %all-to-all-start = ((f32[4,224,128]{2,1,0:T(8,128)}), f32[4,224,128]{2,1,0:T(8,128)S(1)}, u32[]{:S(2)}, u32[]{:S(2)}) async-start(f32[4,224,128]{2,1,0:T(8,128)} %shard_map.50), calls=%async_computation | async-start | bytes 917504 | tf_op jit(solution)/shard_map/all_to_all | solution.py:275
  16.3 0.0 all-gather.3.cloned.1.call-start
  16.3 2.0 slice.4
  18.3 12.1 %all-to-all-done.refs_0_ = f32[4,224,128]{2,1,0:T(8,128)S(1)} async-done(((f32[4,224,128]{2,1,0:T(8,128)}), f32[4,224,128]{2,1,0:T(8,128)S(1)}, u32[]{:S(2)}, u32[]{:S(2)}) %all-to-all-start) | async-done | bytes 458784 | tf_op jit(solution)/shard_map/all_to_all | solution.py:275
  30.4 1.1 shard_map.51
  31.5 0.0 all-gather.3.cloned.1.call-update
  31.5 0.0 all-gather.5.cloned.1.call-start
  31.6 0.7 all-gather.5.cloned.1.call-update
  32.3 20.6 %all_to_all.60.mine_ref = f32[8,2,32,128]{3,2,1,0:T(8,128)S(1)} all-to-all(f32[8,2,32,128]{3,2,1,0:T(8,128)S(1)} %get-tuple-element.19), channel_id=1, replica_groups=mesh['x'=4,'yq'=4,'yp'=2,'z'=8,'core'=2] {'z'}, dimensions={0} | all-to-all | bytes 524288 | tf_op jit(solution)/shard_map/all_to_all | solution.py:283
  52.9 1.9 collective-permute-start
  54.8 1.6 collective-permute-done.other_ref
  56.4 0.4 shard_map.52
  56.8 10.3 %all_to_all.61.got_ref = f32[8,64,128]{2,1,0:T(8,128)S(1)} all-to-all(f32[8,64,128]{2,1,0:T(8,128)S(1)} %shard_map.52), channel_id=1, replica_groups=mesh['x'=4,'yq'=4,'yp'=2,'z'=8,'core'=2] {'yp','x'}, dimensions={0} | all-to-all | bytes 524288 | tf_op jit(solution)/shard_map/all_to_all | solution.py:294
  67.2 9.8 %all_to_all.62.refs_0_ = f32[8,64,128]{2,1,0:T(8,128)S(1)} all-to-all(f32[8,64,128]{2,1,0:T(8,128)S(1)} %get-tuple-element.20), channel_id=1, replica_groups=mesh['x'=4,'yq'=4,'yp'=2,'z'=8,'core'=2] {'yp','x'}, dimensions={0} | all-to-all | bytes 524288 | tf_op jit(solution)/shard_map/all_to_all | solution.py:299
  77.0 2.2 %all-gather.3.cloned.1.call-done = f32[9,2,512,128]{3,2,1,0:T(8,128)} async-done(((f32[9,2,32,128]{3,2,1,0:T(8,128)}), f32[9,2,512,128]{3,2,1,0:T(8,128)}) %all-gather.3.cloned.1.call-update) | async-done | bytes 4718608 | tf_op jit(solution)/shard_map/all_gather | solution.py:286
  79.1 1.7 shard_map.54
  80.9 11.0 %all_to_all.63.got_ref = f32[8,64,128]{2,1,0:T(8,128)S(1)} all-to-all(f32[8,64,128]{2,1,0:T(8,128)S(1)} %shard_map.54), channel_id=1, replica_groups=mesh['x'=4,'yq'=4,'yp'=2,'z'=8,'core'=2] {'yp','x'}, dimensions={0} | all-to-all | bytes 524288 | tf_op jit(solution)/shard_map/all_to_all | solution.py:294
  91.9 0.7 shard_map.55
  92.6 5.1 %all-to-all-start.5 = ((f32[8,64,128]{2,1,0:T(8,128)}), f32[8,64,128]{2,1,0:T(8,128)S(1)}, u32[]{:S(2)}, u32[]{:S(2)}) async-start(f32[8,64,128]{2,1,0:T(8,128)} %get-tuple-element.22), calls=%async_computation.5 | async-start | bytes 524288 | tf_op jit(solution)/shard_map/all_to_all | solution.py:299
  97.7 1.6 shard_map.56.refs_1_
  99.4 3.8 %all-to-all-done.5.refs_0_.refs_1_ = f32[8,64,128]{2,1,0:T(8,128)S(1)} async-done(((f32[8,64,128]{2,1,0:T(8,128)}), f32[8,64,128]{2,1,0:T(8,128)S(1)}, u32[]{:S(2)}, u32[]{:S(2)}) %all-to-all-start.5) | async-done | bytes 262176 | tf_op jit(solution)/shard_map/all_to_all | solution.py:299
  103.2 1.7 shard_map.57
  104.9 9.8 %all_to_all.64.got_ref = f32[8,64,128]{2,1,0:T(8,128)S(1)} all-to-all(f32[8,64,128]{2,1,0:T(8,128)S(1)} %shard_map.57), channel_id=1, replica_groups=mesh['x'=4,'yq'=4,'yp'=2,'z'=8,'core'=2] {'yp','x'}, dimensions={0} | all-to-all | bytes 524288 | tf_op jit(solution)/shard_map/all_to_all | solution.py:294
  114.7 0.7 shard_map.58
  115.4 5.1 %all-to-all-start.7 = ((f32[8,64,128]{2,1,0:T(8,128)}), f32[8,64,128]{2,1,0:T(8,128)S(1)}, u32[]{:S(2)}, u32[]{:S(2)}) async-start(f32[8,64,128]{2,1,0:T(8,128)} %get-tuple-element.23), calls=%async_computation.7 | async-start | bytes 524288 | tf_op jit(solution)/shard_map/all_to_all | solution.py:299
  120.6 1.3 shard_map.59.refs_1_
  121.9 4.1 %all-to-all-done.7.refs_0_.refs_2_ = f32[8,64,128]{2,1,0:T(8,128)S(1)} async-done(((f32[8,64,128]{2,1,0:T(8,128)}), f32[8,64,128]{2,1,0:T(8,128)S(1)}, u32[]{:S(2)}, u32[]{:S(2)}) %all-to-all-start.7) | async-done | bytes 262176 | tf_op jit(solution)/shard_map/all_to_all | solution.py:299
  126.0 0.0 copy-start.2
  126.0 1.8 shard_map.60
  127.8 9.8 %all_to_all.65.got_ref = f32[8,64,128]{2,1,0:T(8,128)S(1)} all-to-all(f32[8,64,128]{2,1,0:T(8,128)S(1)} %shard_map.60), channel_id=1, replica_groups=mesh['x'=4,'yq'=4,'yp'=2,'z'=8,'core'=2] {'yp','x'}, dimensions={0} | all-to-all | bytes 524288 | tf_op jit(solution)/shard_map/all_to_all | solution.py:294
  137.6 0.8 shard_map.61
  138.5 0.0 copy-done.2
  138.5 5.8 %all-to-all-start.9 = ((f32[4,4,64,128]{3,2,1,0:T(8,128)}), f32[4,4,64,128]{3,2,1,0:T(8,128)S(1)}, u32[]{:S(2)}, u32[]{:S(2)}) async-start(f32[4,4,64,128]{3,2,1,0:T(8,128)} %shard_map.61), calls=%async_computation.9 | async-start | bytes 1048576 | tf_op jit(solution)/shard_map/all_to_all | solution.py:321
  144.2 11.6 %all-to-all-done.9.got_ref.refs_0_.refs_5_ = f32[4,4,64,128]{3,2,1,0:T(8,128)S(1)} async-done(((f32[4,4,64,128]{3,2,1,0:T(8,128)}), f32[4,4,64,128]{3,2,1,0:T(8,128)S(1)}, u32[]{:S(2)}, u32[]{:S(2)}) %all-to-all-start.9) | async-done | bytes 524320 | tf_op jit(solution)/shard_map/all_to_all | solution.py:321
  155.9 0.2 shard_map.62
  156.0 25.9 %all_to_all.66.refs_3_ = f32[8,3,3,64,128]{4,3,2,1,0:T(8,128)S(1)} all-to-all(f32[8,3,3,64,128]{4,3,2,1,0:T(8,128)S(1)} %shard_map.62), channel_id=1, replica_groups=mesh['x'=4,'yq'=4,'yp'=2,'z'=8,'core'=2] {'yp','x'}, dimensions={0} | all-to-all | bytes 4718592 | tf_op jit(solution)/shard_map/all_to_all | solution.py:323
  181.9 0.1 shard_map.63
  182.0 0.0 copy-start
  182.0 1.0 copy-done
  183.0 5.9 %all-to-all-start.11 = ((f32[8,4,64,128]{3,2,1,0:T(8,128)}), f32[8,4,64,128]{3,2,1,0:T(8,128)}, u32[]{:S(2)}, u32[]{:S(2)}) async-start(f32[8,4,64,128]{3,2,1,0:T(8,128)} %copy-done), calls=%async_computation.11 | async-start | bytes 2097152 | tf_op jit(solution)/shard_map/all_to_all | solution.py:326
  188.9 0.0 all-gather.5.cloned.1.call-done.refs_4_
  188.9 0.0 copy-start.3
  188.9 0.9 copy-done.3
  189.9 10.6 %shard_map.64.refs_2_ = f32[256,576]{1,0:T(8,128)S(1)} custom-call(f32[8,64,128]{2,1,0:T(8,128)S(1)} %all_to_all.62.refs_0_, f32[8,64,128]{2,1,0:T(8,128)S(1)} %all-to-all-done.5.refs_0_.refs_1_, f32[8,64,128]{2,1,0:T(8,128)S(1)} %copy-done.3, f32[8,3,3,64,128]{4,3,2,1,0:T(8,128)S(1)} %all_to_all.66.refs_3_, ...), custom_call_target="tpu_custom_call" | custom-call | tf_op jit(solution)/shard_map/pallas_call | solution.py:330
  200.5 0.0 copy-start.1
  200.5 0.9 copy-done.1
  201.4 0.0 all-to-all-done.11.refs_0_
  201.4 4.4 %shard_map.65 = (f32[576,256]{1,0:T(8,128)}, f32[128,256]{1,0:T(8,128)}) custom-call(f32[8,4,64,128]{3,2,1,0:T(8,128)} %all-to-all-done.11.refs_0_, f32[4,4,256,576]{3,2,1,0:T(8,128)} %bitcast.19, f32[256,576]{1,0:T(8,128)} %copy-done.1, s32[1]{0:T(128)} %bitcast.9.quad_ref.refs_3_, f32[704,256]{1,0:T(8,128)} %bitcast.21, ...), custom_call_target="tpu_custom_call" | custom-call | tf_op jit(solution)/shard_map/pallas_call | solution.py:348
  (1 shorter events, 0.0 us)
Async XLA Ops:
  9.2 21.2 %all-to-all-start = ((f32[4,224,128]{2,1,0:T(8,128)}), f32[4,224,128]{2,1,0:T(8,128)S(1)}, u32[]{:S(2)}, u32[]{:S(2)}) async-start(f32[4,224,128]{2,1,0:T(8,128)} %shard_map.50), calls=%async_computation | async-start | bytes 917504 | tf_op jit(solution)/shard_map/all_to_all | solution.py:275
  16.3 62.9 %all-gather.3.cloned.1.call-start = ((), (), s32[]{:S(2)}) async-start(), calls=%async_computation.12 | async-start | bytes 5013504 | tf_op jit(solution)/shard_map/all_gather | solution.py:286
  31.5 157.4 %all-gather.5.cloned.1.call-start = ((), (), s32[]{:S(2)}) async-start(), calls=%async_computation.13 | async-start | bytes 11141120 | tf_op jit(solution)/shard_map/all_gather | solution.py:287
  52.9 3.5 %collective-permute-start = (f32[8,2,32,128]{3,2,1,0:T(8,128)S(1)}, f32[8,2,32,128]{3,2,1,0:T(8,128)S(1)}, u32[]{:S(2)}, u32[]{:S(2)}) collective-permute-start(f32[8,2,32,128]{3,2,1,0:T(8,128)S(1)} %all_to_all.60.mine_ref), channel_id=1, source_target_pairs={{0,1},{1,0},{2,3},{3,2},{4,5},{5,4},{6,7},{7,6},{8,9},{9,8},{10,11... | collective-permute-start | bytes 786440 | tf_op jit(solution)/shard_map/ppermute | solution.py:284
  92.6 10.6 %all-to-all-start.5 = ((f32[8,64,128]{2,1,0:T(8,128)}), f32[8,64,128]{2,1,0:T(8,128)S(1)}, u32[]{:S(2)}, u32[]{:S(2)}) async-start(f32[8,64,128]{2,1,0:T(8,128)} %get-tuple-element.22), calls=%async_computation.5 | async-start | bytes 524288 | tf_op jit(solution)/shard_map/all_to_all | solution.py:299
  115.4 10.6 %all-to-all-start.7 = ((f32[8,64,128]{2,1,0:T(8,128)}), f32[8,64,128]{2,1,0:T(8,128)S(1)}, u32[]{:S(2)}, u32[]{:S(2)}) async-start(f32[8,64,128]{2,1,0:T(8,128)} %get-tuple-element.23), calls=%async_computation.7 | async-start | bytes 524288 | tf_op jit(solution)/shard_map/all_to_all | solution.py:299
  126.0 12.4 %copy-start.2 = (f32[8,64,128]{2,1,0:T(8,128)}, f32[8,64,128]{2,1,0:T(8,128)S(1)}, u32[]{:S(2)}) copy-start(f32[8,64,128]{2,1,0:T(8,128)S(1)} %all-to-all-done.7.refs_0_.refs_2_) | copy-start | bytes 786436
  138.5 17.4 %all-to-all-start.9 = ((f32[4,4,64,128]{3,2,1,0:T(8,128)}), f32[4,4,64,128]{3,2,1,0:T(8,128)S(1)}, u32[]{:S(2)}, u32[]{:S(2)}) async-start(f32[4,4,64,128]{3,2,1,0:T(8,128)} %shard_map.61), calls=%async_computation.9 | async-start | bytes 1048576 | tf_op jit(solution)/shard_map/all_to_all | solution.py:321
  182.0 1.0 copy-start
  183.0 18.4 %all-to-all-start.11 = ((f32[8,4,64,128]{3,2,1,0:T(8,128)}), f32[8,4,64,128]{3,2,1,0:T(8,128)}, u32[]{:S(2)}, u32[]{:S(2)}) async-start(f32[8,4,64,128]{3,2,1,0:T(8,128)} %copy-done), calls=%async_computation.11 | async-start | bytes 2097152 | tf_op jit(solution)/shard_map/all_to_all | solution.py:326
  188.9 1.0 copy-start.3
  200.5 0.9 copy-start.1
Sparse Core Ops, SparseCore 0:
  31.6 47.4 all-gather.2
  81.3 67.2 all-gather.4

commit v8 on v7

--- a/solution.py
+++ b/solution.py
@@ -183,12 +183,12 @@
 
 
 def trail_sum(steps, *refs):
-    own_refs, (x_ref, f_ref, out_ref) = refs[:-3], refs[-3:]
+    own_refs, (x_ref, f_ref, out_hbm, acc_ref, sem) = refs[:-5], refs[-5:]
     step = pl.program_id(0)
 
     @pl.when(step == 0)
     def _():
-        out_ref[...] = jnp.zeros_like(out_ref)
+        acc_ref[...] = jnp.zeros_like(acc_ref)
 
     for k, own_ref in enumerate(own_refs):
 
@@ -198,7 +198,13 @@
             for s in range(2):
                 turns = [x_ref[s, 0, t] for t in range(x_ref.shape[2])]
                 parts.append(jnp.concatenate([own_ref[2 * (step % steps) + s], *turns], axis=0))
-            out_ref[...] += dot(jnp.concatenate(parts, axis=1), f_ref[0, 0], NN)
+            acc_ref[...] += dot(jnp.concatenate(parts, axis=1), f_ref[0, 0], NN)
+
+    @pl.when(step == pl.num_programs(0) - 1)
+    def _():
+        copy = pltpu.make_async_copy(acc_ref, out_hbm, sem)
+        copy.start()
+        copy.wait()
 
 
 def finish(panel, x_hbm, f_hbm, sum_hbm, quad_ref, r_hbm, own_ref, *refs):
@@ -274,7 +280,8 @@
     )(in_hbm(lower), in_hbm(inv), in_hbm(current))
     got = lax.all_to_all(sent, "yq", 0, 0, tiled=True)
     trail = lower[:, :, tail:].reshape(panels, npair, half, -1)
-    got, trail = lax.optimization_barrier((got, trail))
+    core = lax.axis_index("core").reshape(1).astype(jnp.int32)
+    got, trail, index, core = lax.optimization_barrier((got, trail, index, core))
     heads, pay, first = call(
         lambda *refs: sort(width, per, *refs),
         [(panels, per, rows), (9, npair, half, rows), (blocks // 2, npair, half, rows)],
@@ -282,7 +289,6 @@
     )(got)
     first = lax.all_to_all(first, "z", 0, 0, tiled=True)
     other = lax.ppermute(first, "core", [(0, 1), (1, 0)])
-    core = lax.axis_index("core").reshape(1).astype(jnp.int32)
     rest = lax.all_gather(pay, RHS, axis=2, tiled=True)
     trail = lax.all_gather(trail, RHS, axis=2, tiled=True)
     rest = rest.reshape(9, group * rows, rows)
@@ -329,7 +335,7 @@
     per_panel = npair * per_pair
     total = pl.pallas_call(
         lambda *refs: trail_sum(per_panel, *refs),
-        out_shape=jax.ShapeDtypeStruct((count, length), F32),
+        out_shape=pltpu.HBM((count, length), F32),
         grid=((panels - 1) * per_panel,),
         in_specs=[
             *[whole((group, per, rows))] * (panels - 1),
@@ -341,9 +347,10 @@
                 lambda i: (i // per_panel, (i % per_panel) // per_pair, i % per_pair, 0),
             ),
         ],
-        out_specs=whole((count, length)),
+        out_specs=HBM,
+        scratch_shapes=[pltpu.VMEM((count, length), F32), pltpu.SemaphoreType.DMA],
         compiler_params=pltpu.CompilerParams(vmem_limit_bytes=16 << 20),
-    )(*solved, early, in_hbm(trail))
+    )(*[in_hbm(x) for x in solved], early, in_hbm(trail))
     flat = trail.reshape(panels, -1, 2 * rows, length)
     out, mine = call(
         lambda *refs: finish(panels - 1, *refs),

time: 214 us -> 213 us (level)
  the two profiles are of different devices: /device:TPU:2 before, /device:TPU:8 now
where the time goes in v8:
time: 213 us; the launch traced here: 211 us
  blocking collectives  117 us (55%)
  Pallas kernels  29.9 us (14%)
  waiting for transfers between devices  24.3 us (11%)
  starting transfers between devices  23.2 us (11%)
  between operations  14.2 us (7%)
  local copies, waits for them, and re-layouts  2.98 us (1%)
    all_to_all x4, blocking collectives, body(): got = lax.all_to_all(y, GROUP, 0, 0, tiled=True)  42.9 us
    all_to_all x1, blocking collectives, body(): early = lax.all_to_all(sent, GROUP, 0, 0, tiled=True)  23.5 us
    all_to_all x1, blocking collectives, body(): first = lax.all_to_all(first, 'z', 0, 0, tiled=True)  20.7 us
    all_to_all x1, blocking collectives, body(): own = lax.all_to_all(sent, 'yq', 0, 0, tiled=True)  19.8 us
    all_to_all x1, waiting for transfers between devices, body(): got = lax.all_to_all(sent, 'yq', 0, 0, tiled=True)  11.8 us
    pallas_call x1, Pallas kernels, body(): pl.pallas_call(lambda *refs: trail_sum(per_panel, *refs), out_shape=pltpu...  11.8 us
    all_to_all x1, blocking collectives, body(): solved.append(lax.all_to_all(copied, GROUP, 0, 0, tiled=True))  9.82 us
    all_to_all x2, starting transfers between devices, body(): solved.append(lax.all_to_all(copied, GROUP, 0, 0, tiled=True))  9.48 us
  transfers between devices with their start and end apart: 7, of which 5 were waited for; matrix products, arithmetic and copies ran while one was open for 1% of the time, Pallas kernels for 11%

profile of v8, /device:TPU:8, one launch (start us, length us, event | category | flops | bytes accessed | tf_op | source)
XLA Modules:
  0.0 211.4 jit_solution(11272638389787289715)
XLA Ops:
  7.2 2.0 shard_map.50
  9.2 6.2 %all-to-all-start = ((f32[4,224,128]{2,1,0:T(8,128)}), f32[4,224,128]{2,1,0:T(8,128)S(1)}, u32[]{:S(2)}, u32[]{:S(2)}) async-start(f32[4,224,128]{2,1,0:T(8,128)} %shard_map.50), calls=%async_computation | async-start | bytes 917504 | tf_op jit(solution)/shard_map/all_to_all | solution.py:281
  15.4 0.0 all-gather.3.cloned.1.call-start
  15.4 2.0 slice.4
  17.4 11.8 %all-to-all-done.refs_0_ = f32[4,224,128]{2,1,0:T(8,128)S(1)} async-done(((f32[4,224,128]{2,1,0:T(8,128)}), f32[4,224,128]{2,1,0:T(8,128)S(1)}, u32[]{:S(2)}, u32[]{:S(2)}) %all-to-all-start) | async-done | bytes 458784 | tf_op jit(solution)/shard_map/all_to_all | solution.py:281
  29.2 1.1 shard_map.51
  30.3 0.0 all-gather.3.cloned.1.call-update
  30.4 0.0 all-gather.5.cloned.1.call-start
  30.4 0.7 all-gather.5.cloned.1.call-update
  31.1 20.7 %all_to_all.60.mine_ref = f32[8,2,32,128]{3,2,1,0:T(8,128)S(1)} all-to-all(f32[8,2,32,128]{3,2,1,0:T(8,128)S(1)} %get-tuple-element.22), channel_id=1, replica_groups=mesh['x'=4,'yq'=4,'yp'=2,'z'=8,'core'=2] {'z'}, dimensions={0} | all-to-all | bytes 524288 | tf_op jit(solution)/shard_map/all_to_all | solution.py:290
  51.8 1.9 collective-permute-start
  53.7 1.6 collective-permute-done.other_ref
  55.3 0.4 shard_map.52
  55.7 11.7 %all_to_all.61.got_ref = f32[8,64,128]{2,1,0:T(8,128)S(1)} all-to-all(f32[8,64,128]{2,1,0:T(8,128)S(1)} %shard_map.52), channel_id=1, replica_groups=mesh['x'=4,'yq'=4,'yp'=2,'z'=8,'core'=2] {'yp','x'}, dimensions={0} | all-to-all | bytes 524288 | tf_op jit(solution)/shard_map/all_to_all | solution.py:300
  67.5 9.8 %all_to_all.62.refs_0_ = f32[8,64,128]{2,1,0:T(8,128)S(1)} all-to-all(f32[8,64,128]{2,1,0:T(8,128)S(1)} %get-tuple-element.23), channel_id=1, replica_groups=mesh['x'=4,'yq'=4,'yp'=2,'z'=8,'core'=2] {'yp','x'}, dimensions={0} | all-to-all | bytes 524288 | tf_op jit(solution)/shard_map/all_to_all | solution.py:305
  77.3 0.0 copy-start
  77.3 1.5 all-gather.3.cloned.1.call-done
  78.8 1.7 shard_map.54
  80.5 11.7 %all_to_all.63.got_ref = f32[8,64,128]{2,1,0:T(8,128)S(1)} all-to-all(f32[8,64,128]{2,1,0:T(8,128)S(1)} %shard_map.54), channel_id=1, replica_groups=mesh['x'=4,'yq'=4,'yp'=2,'z'=8,'core'=2] {'yp','x'}, dimensions={0} | all-to-all | bytes 524288 | tf_op jit(solution)/shard_map/all_to_all | solution.py:300
  92.2 0.7 shard_map.55
  92.9 4.7 %all-to-all-start.5 = ((f32[8,64,128]{2,1,0:T(8,128)}), f32[8,64,128]{2,1,0:T(8,128)S(1)}, u32[]{:S(2)}, u32[]{:S(2)}) async-start(f32[8,64,128]{2,1,0:T(8,128)} %get-tuple-element.25), calls=%async_computation.5 | async-start | bytes 524288 | tf_op jit(solution)/shard_map/all_to_all | solution.py:305
  97.7 1.6 shard_map.56.refs_1_
  99.3 0.0 copy-done
  99.3 4.2 %all-to-all-done.5.refs_0_.refs_1_ = f32[8,64,128]{2,1,0:T(8,128)S(1)} async-done(((f32[8,64,128]{2,1,0:T(8,128)}), f32[8,64,128]{2,1,0:T(8,128)S(1)}, u32[]{:S(2)}, u32[]{:S(2)}) %all-to-all-start.5) | async-done | bytes 262176 | tf_op jit(solution)/shard_map/all_to_all | solution.py:305
  103.5 0.0 copy-start.1
  103.5 1.9 shard_map.57
  105.4 9.7 %all_to_all.64.got_ref = f32[8,64,128]{2,1,0:T(8,128)S(1)} all-to-all(f32[8,64,128]{2,1,0:T(8,128)S(1)} %shard_map.57), channel_id=1, replica_groups=mesh['x'=4,'yq'=4,'yp'=2,'z'=8,'core'=2] {'yp','x'}, dimensions={0} | all-to-all | bytes 524288 | tf_op jit(solution)/shard_map/all_to_all | solution.py:300
  115.1 0.7 shard_map.58
  115.9 4.7 %all-to-all-start.7 = ((f32[8,64,128]{2,1,0:T(8,128)}), f32[8,64,128]{2,1,0:T(8,128)S(1)}, u32[]{:S(2)}, u32[]{:S(2)}) async-start(f32[8,64,128]{2,1,0:T(8,128)} %get-tuple-element.26), calls=%async_computation.7 | async-start | bytes 524288 | tf_op jit(solution)/shard_map/all_to_all | solution.py:305
  120.6 1.3 shard_map.59.refs_1_
  121.9 0.0 copy-done.1
  121.9 4.5 %all-to-all-done.7.refs_0_.refs_2_ = f32[8,64,128]{2,1,0:T(8,128)S(1)} async-done(((f32[8,64,128]{2,1,0:T(8,128)}), f32[8,64,128]{2,1,0:T(8,128)S(1)}, u32[]{:S(2)}, u32[]{:S(2)}) %all-to-all-start.7) | async-done | bytes 262176 | tf_op jit(solution)/shard_map/all_to_all | solution.py:305
  126.4 0.0 copy-start.3
  126.4 1.8 shard_map.60
  128.3 9.8 %all_to_all.65.got_ref = f32[8,64,128]{2,1,0:T(8,128)S(1)} all-to-all(f32[8,64,128]{2,1,0:T(8,128)S(1)} %shard_map.60), channel_id=1, replica_groups=mesh['x'=4,'yq'=4,'yp'=2,'z'=8,'core'=2] {'yp','x'}, dimensions={0} | all-to-all | bytes 524288 | tf_op jit(solution)/shard_map/all_to_all | solution.py:300
  138.1 19.8 %all_to_all.66.got_ref.refs_0_.refs_5_ = f32[4,4,64,128]{3,2,1,0:T(8,128)S(1)} all-to-all(f32[4,4,64,128]{3,2,1,0:T(8,128)S(1)} %shard_map.61), channel_id=1, replica_groups=mesh['x'=4,'yq'=4,'yp'=2,'z'=8,'core'=2] {'yq'}, dimensions={0} | all-to-all | bytes 1048576 | tf_op jit(solution)/shard_map/all_to_all | solution.py:327
  157.9 0.2 shard_map.62
  158.1 0.0 copy-done.3
  158.1 23.5 %all_to_all.67.refs_3_ = f32[8,3,3,64,128]{4,3,2,1,0:T(8,128)S(1)} all-to-all(f32[8,3,3,64,128]{4,3,2,1,0:T(8,128)S(1)} %shard_map.62), channel_id=1, replica_groups=mesh['x'=4,'yq'=4,'yp'=2,'z'=8,'core'=2] {'yp','x'}, dimensions={0} | all-to-all | bytes 4718592 | tf_op jit(solution)/shard_map/all_to_all | solution.py:329
  181.6 0.1 shard_map.63
  181.7 0.0 copy-start.2
  181.7 1.0 copy-done.2
  182.7 5.6 %all-to-all-start.11 = ((f32[8,4,64,128]{3,2,1,0:T(8,128)}), f32[8,4,64,128]{3,2,1,0:T(8,128)}, u32[]{:S(2)}, u32[]{:S(2)}) async-start(f32[8,4,64,128]{3,2,1,0:T(8,128)} %copy-done.2), calls=%async_computation.11 | async-start | bytes 2097152 | tf_op jit(solution)/shard_map/all_to_all | solution.py:332
  188.3 0.0 all-gather.5.cloned.1.call-done.refs_4_
  188.3 11.8 %shard_map.64.refs_2_ = f32[256,576]{1,0:T(8,128)} custom-call(f32[8,64,128]{2,1,0:T(8,128)} %copy-done, f32[8,64,128]{2,1,0:T(8,128)} %copy-done.1, f32[8,64,128]{2,1,0:T(8,128)} %copy-done.3, f32[8,3,3,64,128]{4,3,2,1,0:T(8,128)S(1)} %all_to_all.67.refs_3_, f32[4,2,512,576]{3,2,1,0:T(8,128)} %all-gather.5.cloned.1.call-done.refs_4_), custom_call_target="tpu_custom_call" | custom-call | tf_op jit(solution)/shard_map/pallas_call | solution.py:336
  200.1 0.0 all-to-all-done.11.refs_0_
  200.1 4.5 %shard_map.65 = (f32[576,256]{1,0:T(8,128)}, f32[128,256]{1,0:T(8,128)}) custom-call(f32[8,4,64,128]{3,2,1,0:T(8,128)} %all-to-all-done.11.refs_0_, f32[4,4,256,576]{3,2,1,0:T(8,128)} %bitcast.19, f32[256,576]{1,0:T(8,128)} %shard_map.64.refs_2_, s32[1]{0:T(128)} %bitcast.7.quad_ref.refs_3_, f32[704,256]{1,0:T(8,128)} %bitcast.21, ...), custom_call_target="tpu_custom_call" | custom-call | tf_op jit(solution)/shard_map/pallas_call | solution.py:355
  (2 shorter events, 0.1 us)
Async XLA Ops:
  9.2 20.0 %all-to-all-start = ((f32[4,224,128]{2,1,0:T(8,128)}), f32[4,224,128]{2,1,0:T(8,128)S(1)}, u32[]{:S(2)}, u32[]{:S(2)}) async-start(f32[4,224,128]{2,1,0:T(8,128)} %shard_map.50), calls=%async_computation | async-start | bytes 917504 | tf_op jit(solution)/shard_map/all_to_all | solution.py:281
  15.4 63.4 %all-gather.3.cloned.1.call-start = ((), (), s32[]{:S(2)}) async-start(), calls=%async_computation.12 | async-start | bytes 5013504 | tf_op jit(solution)/shard_map/all_gather | solution.py:292
  30.4 157.9 %all-gather.5.cloned.1.call-start = ((), (), s32[]{:S(2)}) async-start(), calls=%async_computation.13 | async-start | bytes 11141120 | tf_op jit(solution)/shard_map/all_gather | solution.py:293
  51.8 3.5 %collective-permute-start = (f32[8,2,32,128]{3,2,1,0:T(8,128)S(1)}, f32[8,2,32,128]{3,2,1,0:T(8,128)S(1)}, u32[]{:S(2)}, u32[]{:S(2)}) collective-permute-start(f32[8,2,32,128]{3,2,1,0:T(8,128)S(1)} %all_to_all.60.mine_ref), channel_id=1, source_target_pairs={{0,1},{1,0},{2,3},{3,2},{4,5},{5,4},{6,7},{7,6},{8,9},{9,8},{10,11... | collective-permute-start | bytes 786440 | tf_op jit(solution)/shard_map/ppermute | solution.py:291
  77.3 22.0 %copy-start = (f32[8,64,128]{2,1,0:T(8,128)}, f32[8,64,128]{2,1,0:T(8,128)S(1)}, u32[]{:S(2)}) copy-start(f32[8,64,128]{2,1,0:T(8,128)S(1)} %all_to_all.62.refs_0_) | copy-start | bytes 786436
  92.9 10.6 %all-to-all-start.5 = ((f32[8,64,128]{2,1,0:T(8,128)}), f32[8,64,128]{2,1,0:T(8,128)S(1)}, u32[]{:S(2)}, u32[]{:S(2)}) async-start(f32[8,64,128]{2,1,0:T(8,128)} %get-tuple-element.25), calls=%async_computation.5 | async-start | bytes 524288 | tf_op jit(solution)/shard_map/all_to_all | solution.py:305
  103.5 18.4 %copy-start.1 = (f32[8,64,128]{2,1,0:T(8,128)}, f32[8,64,128]{2,1,0:T(8,128)S(1)}, u32[]{:S(2)}) copy-start(f32[8,64,128]{2,1,0:T(8,128)S(1)} %all-to-all-done.5.refs_0_.refs_1_) | copy-start | bytes 786436
  115.9 10.6 %all-to-all-start.7 = ((f32[8,64,128]{2,1,0:T(8,128)}), f32[8,64,128]{2,1,0:T(8,128)S(1)}, u32[]{:S(2)}, u32[]{:S(2)}) async-start(f32[8,64,128]{2,1,0:T(8,128)} %get-tuple-element.26), calls=%async_computation.7 | async-start | bytes 524288 | tf_op jit(solution)/shard_map/all_to_all | solution.py:305
  126.4 31.6 %copy-start.3 = (f32[8,64,128]{2,1,0:T(8,128)}, f32[8,64,128]{2,1,0:T(8,128)S(1)}, u32[]{:S(2)}) copy-start(f32[8,64,128]{2,1,0:T(8,128)S(1)} %all-to-all-done.7.refs_0_.refs_2_) | copy-start | bytes 786436
  181.7 1.0 copy-start.2
  182.7 17.4 %all-to-all-start.11 = ((f32[8,4,64,128]{3,2,1,0:T(8,128)}), f32[8,4,64,128]{3,2,1,0:T(8,128)}, u32[]{:S(2)}, u32[]{:S(2)}) async-start(f32[8,4,64,128]{3,2,1,0:T(8,128)} %copy-done.2), calls=%async_computation.11 | async-start | bytes 2097152 | tf_op jit(solution)/shard_map/all_to_all | solution.py:332
Sparse Core Ops, SparseCore 0:
  30.5 48.2 all-gather.2
  80.9 67.4 all-gather.4

commit v9 on v8

--- a/solution.py
+++ b/solution.py
@@ -79,9 +79,9 @@
         out_ref[q, per + cols + cols // 2 :] = diag
 
 
-def sort(w, per, got_ref, heads_ref, pay_ref, first_ref):
+def sort(w, per, got_ref, heads_ref, soon_ref, later_ref, first_ref):
     quads = got_ref.shape[0]
-    half = pay_ref.shape[2]
+    half = soon_ref.shape[2]
     cols = 2 * half
     a, b, d = per, per + cols, per + cols + half
 
@@ -93,13 +93,14 @@
     for k in range(4):
         heads_ref[k] = lanes(0, per, k * w)
     for h in range(2):
-        for k in range(1, 4):
-            pay_ref[k - 1, h] = lanes(d + h * half, half, k * w)
+        soon_ref[0, h] = lanes(d + h * half, half, w)
+        soon_ref[1, h] = lanes(d + h * half, half, 2 * w)
         for j in range(3):
-            pay_ref[3 + j, h] = lanes(a + h * half, half, j * w)
-        for j in range(2):
-            pay_ref[6 + j, h] = lanes(b, half, h * 2 * w + j * w)
-        pay_ref[8, h] = lanes(a + h * half, half, 3 * w)
+            soon_ref[2 + j, h] = lanes(a + h * half, half, j * w)
+        soon_ref[5, h] = lanes(b, half, h * 2 * w)
+        later_ref[0, h] = lanes(d + h * half, half, 3 * w)
+        later_ref[1, h] = lanes(b, half, h * 2 * w + w)
+        later_ref[2, h] = lanes(a + h * half, half, 3 * w)
         piece = lanes(d + h * half, half, 0)
         for c in range(first_ref.shape[0]):
             first_ref[c, h] = piece
@@ -282,16 +283,23 @@
     trail = lower[:, :, tail:].reshape(panels, npair, half, -1)
     core = lax.axis_index("core").reshape(1).astype(jnp.int32)
     got, trail, index, core = lax.optimization_barrier((got, trail, index, core))
-    heads, pay, first = call(
+    heads, soon, later, first = call(
         lambda *refs: sort(width, per, *refs),
-        [(panels, per, rows), (9, npair, half, rows), (blocks // 2, npair, half, rows)],
+        [
+            (panels, per, rows),
+            (6, npair, half, rows),
+            (3, npair, half, rows),
+            (blocks // 2, npair, half, rows),
+        ],
         [VMEM],
     )(got)
     first = lax.all_to_all(first, "z", 0, 0, tiled=True)
     other = lax.ppermute(first, "core", [(0, 1), (1, 0)])
-    rest = lax.all_gather(pay, RHS, axis=2, tiled=True)
+    soon = lax.all_gather(soon, RHS, axis=2, tiled=True)
+    later = lax.all_gather(later, RHS, axis=2, tiled=True)
     trail = lax.all_gather(trail, RHS, axis=2, tiled=True)
-    rest = rest.reshape(9, group * rows, rows)
+    soon = soon.reshape(6, group * rows, rows)
+    later = later.reshape(3, group * rows, rows)
 
     (y,) = call(begin, [(group, per, rows)], [SMEM, VMEM, VMEM, VMEM])(core, heads, first, other)
     length = lower.shape[2] - tail
@@ -304,24 +312,24 @@
         mine.append(single)
         solved.append(lax.all_to_all(copied, GROUP, 0, 0, tiled=True))
         left = panels - 1 - k
-        at = {3: 3, 2: 6, 1: 8}[left]
+        block, at, diag_at = ((soon, 2, 0), (soon, 5, 1), (later, 2, 0))[k]
         one = pltpu.VMEM((group * rows, rows), F32)
         (y,) = call(
-            lambda *refs, at=at, k=k: advance(int(k == 0), at, k, *refs),
+            lambda *refs, at=at, diag_at=diag_at, k=k: advance(int(k == 0), at, diag_at, *refs),
             [(group, per, rows)],
             [VMEM, VMEM, HBM],
             [one, one, pltpu.SemaphoreType.DMA((2,))],
-        )(solved[k], heads, in_hbm(rest))
+        )(solved[k], heads, in_hbm(block))
         if left > 1:
             (heads,) = call(
-                lambda *refs, at=at, k=k: follow(int(k == 0), at + 1, *refs),
+                lambda *refs, k=k: follow(int(k == 0), (3, 1)[k], *refs),
                 [(left - 1, per, rows)],
                 [VMEM, VMEM, HBM],
                 [
                     pltpu.VMEM((left - 1, group * rows, rows), F32),
                     pltpu.SemaphoreType.DMA,
                 ],
-            )(solved[k], heads, in_hbm(rest))
+            )(solved[k], heads, in_hbm((soon, later)[k]))
 
     (sent,) = call(add_all, [(quads, panels, per, rows)], [VMEM] * panels)(got, *mine)
     own = lax.all_to_all(sent, "yq", 0, 0, tiled=True)

time: 213 us -> 218 us (1.023)
  the two profiles are of different devices: /device:TPU:8 before, /device:TPU:16 now
where the time goes in v9:
time: 218 us; the launch traced here: 217 us
  blocking collectives  123 us (56%)
  Pallas kernels  30 us (14%)
  waiting for transfers between devices  26.7 us (12%)
  starting transfers between devices  22.2 us (10%)
  between operations  13.9 us (6%)
    all_to_all x4, blocking collectives, body(): got = lax.all_to_all(y, GROUP, 0, 0, tiled=True)  41.1 us
    all_to_all x1, blocking collectives, body(): early = lax.all_to_all(sent, GROUP, 0, 0, tiled=True)  32.3 us
    all_to_all x1, blocking collectives, body(): first = lax.all_to_all(first, 'z', 0, 0, tiled=True)  22.5 us
    all_to_all x1, blocking collectives, body(): own = lax.all_to_all(sent, 'yq', 0, 0, tiled=True)  16.9 us
    pallas_call x1, Pallas kernels, body(): pl.pallas_call(lambda *refs: trail_sum(per_panel, *refs), out_shape=pltpu...  11.8 us
    all_to_all x1, waiting for transfers between devices, body(): got = lax.all_to_all(sent, 'yq', 0, 0, tiled=True)  11.2 us
    all_to_all x2, waiting for transfers between devices, body(): solved.append(lax.all_to_all(copied, GROUP, 0, 0, tiled=True))  10.7 us
    all_to_all x1, blocking collectives, body(): solved.append(lax.all_to_all(copied, GROUP, 0, 0, tiled=True))  9.82 us
  transfers between devices with their start and end apart: 8, of which 6 were waited for; matrix products, arithmetic and copies ran while one was open for 0% of the time, Pallas kernels for 10%

profile of v9, /device:TPU:16, one launch (start us, length us, event | category | flops | bytes accessed | tf_op | source)
XLA Modules:
  0.0 217.2 jit_solution(7348356277165575351)
XLA Ops:
  7.2 0.0 copy-start.4
  7.2 2.1 shard_map.50
  9.3 9.1 %all-to-all-start = ((f32[4,224,128]{2,1,0:T(8,128)}), f32[4,224,128]{2,1,0:T(8,128)S(1)}, u32[]{:S(2)}, u32[]{:S(2)}) async-start(f32[4,224,128]{2,1,0:T(8,128)} %shard_map.50), calls=%async_computation | async-start | bytes 917504 | tf_op jit(solution)/shard_map/all_to_all | solution.py:282
  18.4 0.0 all-gather.4.cloned.1.call-start
  18.4 0.0 copy-done.4
  18.4 0.9 slice.4
  19.3 11.2 %all-to-all-done.refs_0_ = f32[4,224,128]{2,1,0:T(8,128)S(1)} async-done(((f32[4,224,128]{2,1,0:T(8,128)}), f32[4,224,128]{2,1,0:T(8,128)S(1)}, u32[]{:S(2)}, u32[]{:S(2)}) %all-to-all-start) | async-done | bytes 458784 | tf_op jit(solution)/shard_map/all_to_all | solution.py:282
  30.5 1.1 shard_map.51
  31.6 0.0 all-gather.4.cloned.1.call-update
  31.6 0.0 all-gather.6.cloned.1.call-start
  31.6 0.7 all-gather.6.cloned.1.call-update
  32.3 0.0 all-gather.8.cloned.1.call-start
  32.4 0.7 all-gather.8.cloned.1.call-update
  33.1 22.5 %all_to_all.60.mine_ref = f32[8,2,32,128]{3,2,1,0:T(8,128)S(1)} all-to-all(f32[8,2,32,128]{3,2,1,0:T(8,128)S(1)} %get-tuple-element.23), channel_id=1, replica_groups=mesh['x'=4,'yq'=4,'yp'=2,'z'=8,'core'=2] {'z'}, dimensions={0} | all-to-all | bytes 524288 | tf_op jit(solution)/shard_map/all_to_all | solution.py:296
  55.6 1.9 collective-permute-start
  57.5 1.6 collective-permute-done.other_ref
  59.1 0.4 shard_map.52
  59.5 11.7 %all_to_all.61.got_ref = f32[8,64,128]{2,1,0:T(8,128)S(1)} all-to-all(f32[8,64,128]{2,1,0:T(8,128)S(1)} %shard_map.52), channel_id=1, replica_groups=mesh['x'=4,'yq'=4,'yp'=2,'z'=8,'core'=2] {'yp','x'}, dimensions={0} | all-to-all | bytes 524288 | tf_op jit(solution)/shard_map/all_to_all | solution.py:308
  71.2 9.8 %all_to_all.62.refs_0_ = f32[8,64,128]{2,1,0:T(8,128)S(1)} all-to-all(f32[8,64,128]{2,1,0:T(8,128)S(1)} %get-tuple-element.24), channel_id=1, replica_groups=mesh['x'=4,'yq'=4,'yp'=2,'z'=8,'core'=2] {'yp','x'}, dimensions={0} | all-to-all | bytes 524288 | tf_op jit(solution)/shard_map/all_to_all | solution.py:313
  81.0 0.0 copy-start.1
  81.0 0.0 all-gather.4.cloned.1.call-done
  81.0 1.8 shard_map.54
  82.8 9.8 %all_to_all.63.got_ref = f32[8,64,128]{2,1,0:T(8,128)S(1)} all-to-all(f32[8,64,128]{2,1,0:T(8,128)S(1)} %shard_map.54), channel_id=1, replica_groups=mesh['x'=4,'yq'=4,'yp'=2,'z'=8,'core'=2] {'yp','x'}, dimensions={0} | all-to-all | bytes 524288 | tf_op jit(solution)/shard_map/all_to_all | solution.py:308
  92.6 0.7 shard_map.55
  93.4 3.4 %all-to-all-start.5 = ((f32[8,64,128]{2,1,0:T(8,128)}), f32[8,64,128]{2,1,0:T(8,128)S(1)}, u32[]{:S(2)}, u32[]{:S(2)}) async-start(f32[8,64,128]{2,1,0:T(8,128)} %get-tuple-element.26), calls=%async_computation.5 | async-start | bytes 524288 | tf_op jit(solution)/shard_map/all_to_all | solution.py:313
  96.8 0.0 copy-done.1
  96.8 1.7 shard_map.56.refs_1_
  98.5 5.5 %all-to-all-done.5.refs_0_.refs_1_ = f32[8,64,128]{2,1,0:T(8,128)S(1)} async-done(((f32[8,64,128]{2,1,0:T(8,128)}), f32[8,64,128]{2,1,0:T(8,128)S(1)}, u32[]{:S(2)}, u32[]{:S(2)}) %all-to-all-start.5) | async-done | bytes 262176 | tf_op jit(solution)/shard_map/all_to_all | solution.py:313
  103.9 0.0 copy-start
  104.0 1.8 shard_map.57
  105.8 9.8 %all_to_all.64.got_ref = f32[8,64,128]{2,1,0:T(8,128)S(1)} all-to-all(f32[8,64,128]{2,1,0:T(8,128)S(1)} %shard_map.57), channel_id=1, replica_groups=mesh['x'=4,'yq'=4,'yp'=2,'z'=8,'core'=2] {'yp','x'}, dimensions={0} | all-to-all | bytes 524288 | tf_op jit(solution)/shard_map/all_to_all | solution.py:308
  115.6 0.7 shard_map.58
  116.3 3.4 %all-to-all-start.7 = ((f32[8,64,128]{2,1,0:T(8,128)}), f32[8,64,128]{2,1,0:T(8,128)S(1)}, u32[]{:S(2)}, u32[]{:S(2)}) async-start(f32[8,64,128]{2,1,0:T(8,128)} %get-tuple-element.27), calls=%async_computation.7 | async-start | bytes 524288 | tf_op jit(solution)/shard_map/all_to_all | solution.py:313
  119.7 0.6 all-gather.6.cloned.1.call-done
  120.3 0.0 copy-done
  120.3 1.3 shard_map.59.refs_1_
  121.6 5.2 %all-to-all-done.7.refs_0_.refs_2_ = f32[8,64,128]{2,1,0:T(8,128)S(1)} async-done(((f32[8,64,128]{2,1,0:T(8,128)}), f32[8,64,128]{2,1,0:T(8,128)S(1)}, u32[]{:S(2)}, u32[]{:S(2)}) %all-to-all-start.7) | async-done | bytes 262176 | tf_op jit(solution)/shard_map/all_to_all | solution.py:313
  126.9 0.0 copy-start.3
  126.9 1.8 shard_map.60
  128.7 9.8 %all_to_all.65.got_ref = f32[8,64,128]{2,1,0:T(8,128)S(1)} all-to-all(f32[8,64,128]{2,1,0:T(8,128)S(1)} %shard_map.60), channel_id=1, replica_groups=mesh['x'=4,'yq'=4,'yp'=2,'z'=8,'core'=2] {'yp','x'}, dimensions={0} | all-to-all | bytes 524288 | tf_op jit(solution)/shard_map/all_to_all | solution.py:308
  138.5 16.9 %all_to_all.66.got_ref.refs_0_.refs_5_ = f32[4,4,64,128]{3,2,1,0:T(8,128)S(1)} all-to-all(f32[4,4,64,128]{3,2,1,0:T(8,128)S(1)} %shard_map.61), channel_id=1, replica_groups=mesh['x'=4,'yq'=4,'yp'=2,'z'=8,'core'=2] {'yq'}, dimensions={0} | all-to-all | bytes 1048576 | tf_op jit(solution)/shard_map/all_to_all | solution.py:335
  155.4 0.2 shard_map.62
  155.6 0.0 copy-done.3
  155.6 32.3 %all_to_all.67.refs_3_ = f32[8,3,3,64,128]{4,3,2,1,0:T(8,128)S(1)} all-to-all(f32[8,3,3,64,128]{4,3,2,1,0:T(8,128)S(1)} %shard_map.62), channel_id=1, replica_groups=mesh['x'=4,'yq'=4,'yp'=2,'z'=8,'core'=2] {'yp','x'}, dimensions={0} | all-to-all | bytes 4718592 | tf_op jit(solution)/shard_map/all_to_all | solution.py:337
  187.8 0.1 shard_map.63
  187.9 0.0 copy-start.2
  187.9 1.0 copy-done.2
  188.9 4.2 %all-to-all-start.11 = ((f32[8,4,64,128]{3,2,1,0:T(8,128)}), f32[8,4,64,128]{3,2,1,0:T(8,128)}, u32[]{:S(2)}, u32[]{:S(2)}) async-start(f32[8,4,64,128]{3,2,1,0:T(8,128)} %copy-done.2), calls=%async_computation.11 | async-start | bytes 2097152 | tf_op jit(solution)/shard_map/all_to_all | solution.py:340
  193.1 0.0 all-gather.8.cloned.1.call-done.refs_4_
  193.2 11.8 %shard_map.64.refs_2_ = f32[256,576]{1,0:T(8,128)} custom-call(f32[8,64,128]{2,1,0:T(8,128)} %copy-done.1, f32[8,64,128]{2,1,0:T(8,128)} %copy-done, f32[8,64,128]{2,1,0:T(8,128)} %copy-done.3, f32[8,3,3,64,128]{4,3,2,1,0:T(8,128)S(1)} %all_to_all.67.refs_3_, f32[4,2,512,576]{3,2,1,0:T(8,128)} %all-gather.8.cloned.1.call-done.refs_4_), custom_call_target="tpu_custom_call" | custom-call | tf_op jit(solution)/shard_map/pallas_call | solution.py:344
  205.0 1.2 all-to-all-done.11.refs_0_
  206.2 4.4 %shard_map.65 = (f32[576,256]{1,0:T(8,128)}, f32[128,256]{1,0:T(8,128)}) custom-call(f32[8,4,64,128]{3,2,1,0:T(8,128)} %all-to-all-done.11.refs_0_, f32[4,4,256,576]{3,2,1,0:T(8,128)} %bitcast.15, f32[256,576]{1,0:T(8,128)} %shard_map.64.refs_2_, s32[1]{0:T(128)} %bitcast.7.quad_ref.refs_3_, f32[704,256]{1,0:T(8,128)} %bitcast.22, ...), custom_call_target="tpu_custom_call" | custom-call | tf_op jit(solution)/shard_map/pallas_call | solution.py:363
  (2 shorter events, 0.1 us)
Async XLA Ops:
  7.2 11.2 %copy-start.4 = (f32[1,704,4,64]{1,3,2,0:T(8,128)S(1)}, f32[1,704,4,64]{1,3,2,0:T(8,128)}, u32[]{:S(2)}) copy-start(f32[1,704,4,64]{1,3,2,0:T(8,128)} %param.3) | copy-start | bytes 2162692
  9.3 21.2 %all-to-all-start = ((f32[4,224,128]{2,1,0:T(8,128)}), f32[4,224,128]{2,1,0:T(8,128)S(1)}, u32[]{:S(2)}, u32[]{:S(2)}) async-start(f32[4,224,128]{2,1,0:T(8,128)} %shard_map.50), calls=%async_computation | async-start | bytes 917504 | tf_op jit(solution)/shard_map/all_to_all | solution.py:282
  18.4 62.6 %all-gather.4.cloned.1.call-start = ((), (), s32[]{:S(2)}) async-start(), calls=%async_computation.12 | async-start | bytes 3342336 | tf_op jit(solution)/shard_map/all_gather | solution.py:298
  31.6 88.7 %all-gather.6.cloned.1.call-start = ((), (), s32[]{:S(2)}) async-start(), calls=%async_computation.13 | async-start | bytes 1671168 | tf_op jit(solution)/shard_map/all_gather | solution.py:299
  32.3 160.8 %all-gather.8.cloned.1.call-start = ((), (), s32[]{:S(2)}) async-start(), calls=%async_computation.14 | async-start | bytes 11141120 | tf_op jit(solution)/shard_map/all_gather | solution.py:300
  55.6 3.5 %collective-permute-start = (f32[8,2,32,128]{3,2,1,0:T(8,128)S(1)}, f32[8,2,32,128]{3,2,1,0:T(8,128)S(1)}, u32[]{:S(2)}, u32[]{:S(2)}) collective-permute-start(f32[8,2,32,128]{3,2,1,0:T(8,128)S(1)} %all_to_all.60.mine_ref), channel_id=1, source_target_pairs={{0,1},{1,0},{2,3},{3,2},{4,5},{5,4},{6,7},{7,6},{8,9},{9,8},{10,11... | collective-permute-start | bytes 786440 | tf_op jit(solution)/shard_map/ppermute | solution.py:297
  81.0 15.8 %copy-start.1 = (f32[8,64,128]{2,1,0:T(8,128)}, f32[8,64,128]{2,1,0:T(8,128)S(1)}, u32[]{:S(2)}) copy-start(f32[8,64,128]{2,1,0:T(8,128)S(1)} %all_to_all.62.refs_0_) | copy-start | bytes 786436
  93.4 10.6 %all-to-all-start.5 = ((f32[8,64,128]{2,1,0:T(8,128)}), f32[8,64,128]{2,1,0:T(8,128)S(1)}, u32[]{:S(2)}, u32[]{:S(2)}) async-start(f32[8,64,128]{2,1,0:T(8,128)} %get-tuple-element.26), calls=%async_computation.5 | async-start | bytes 524288 | tf_op jit(solution)/shard_map/all_to_all | solution.py:313
  103.9 16.4 %copy-start = (f32[8,64,128]{2,1,0:T(8,128)}, f32[8,64,128]{2,1,0:T(8,128)S(1)}, u32[]{:S(2)}) copy-start(f32[8,64,128]{2,1,0:T(8,128)S(1)} %all-to-all-done.5.refs_0_.refs_1_) | copy-start | bytes 786436
  116.3 10.6 %all-to-all-start.7 = ((f32[8,64,128]{2,1,0:T(8,128)}), f32[8,64,128]{2,1,0:T(8,128)S(1)}, u32[]{:S(2)}, u32[]{:S(2)}) async-start(f32[8,64,128]{2,1,0:T(8,128)} %get-tuple-element.27), calls=%async_computation.7 | async-start | bytes 524288 | tf_op jit(solution)/shard_map/all_to_all | solution.py:313
  126.9 28.7 %copy-start.3 = (f32[8,64,128]{2,1,0:T(8,128)}, f32[8,64,128]{2,1,0:T(8,128)S(1)}, u32[]{:S(2)}) copy-start(f32[8,64,128]{2,1,0:T(8,128)S(1)} %all-to-all-done.7.refs_0_.refs_2_) | copy-start | bytes 786436
  187.9 1.0 copy-start.2
  188.9 17.3 %all-to-all-start.11 = ((f32[8,4,64,128]{3,2,1,0:T(8,128)}), f32[8,4,64,128]{3,2,1,0:T(8,128)}, u32[]{:S(2)}, u32[]{:S(2)}) async-start(f32[8,4,64,128]{3,2,1,0:T(8,128)} %copy-done.2), calls=%async_computation.11 | async-start | bytes 2097152 | tf_op jit(solution)/shard_map/all_to_all | solution.py:340
Sparse Core Ops, SparseCore 0:
  31.7 45.7 all-gather.3
  80.2 40.0 all-gather.5
  122.5 67.1 all-gather.7

commit v10 on v8

--- a/solution.py
+++ b/solution.py
@@ -195,9 +195,9 @@
         @pl.when(step // steps == k)
         def _():
             parts = []
-            for s in range(2):
+            for s in range(x_ref.shape[0]):
                 turns = [x_ref[s, 0, t] for t in range(x_ref.shape[2])]
-                parts.append(jnp.concatenate([own_ref[2 * (step % steps) + s], *turns], axis=0))
+                parts.append(jnp.concatenate([own_ref[x_ref.shape[0] * (step % steps) + s], *turns], axis=0))
             acc_ref[...] += dot(jnp.concatenate(parts, axis=1), f_ref[0, 0], NN)
 
     @pl.when(step == pl.num_programs(0) - 1)
@@ -331,8 +331,7 @@
     (sent,) = call(lambda *refs: last_copies(panels - 1, *refs), [(group, quads, per, rows)], [VMEM])(own)
     late = lax.all_to_all(sent, GROUP, 0, 0, tiled=True)
 
-    per_pair = trail.shape[2] // (2 * rows)
-    per_panel = npair * per_pair
+    per_panel = npair
     total = pl.pallas_call(
         lambda *refs: trail_sum(per_panel, *refs),
         out_shape=pltpu.HBM((count, length), F32),
@@ -340,16 +339,15 @@
         in_specs=[
             *[whole((group, per, rows))] * (panels - 1),
             pl.BlockSpec(
-                (2, 1, quads - 1, per, rows), lambda i: (i % per_panel, i // per_panel, 0, 0, 0)
+                (nx, 1, quads - 1, per, rows), lambda i: (i % per_panel, i // per_panel, 0, 0, 0)
             ),
             pl.BlockSpec(
-                (1, 1, 2 * rows, length),
-                lambda i: (i // per_panel, (i % per_panel) // per_pair, i % per_pair, 0),
+                (1, 1, nx * rows, length), lambda i: (i // per_panel, i % per_panel, 0, 0)
             ),
         ],
         out_specs=HBM,
         scratch_shapes=[pltpu.VMEM((count, length), F32), pltpu.SemaphoreType.DMA],
-        compiler_params=pltpu.CompilerParams(vmem_limit_bytes=16 << 20),
+        compiler_params=pltpu.CompilerParams(vmem_limit_bytes=24 << 20),
     )(*[in_hbm(x) for x in solved], early, in_hbm(trail))
     flat = trail.reshape(panels, -1, 2 * rows, length)
     out, mine = call(

time: 213 us -> 211 us (level)
  Pallas kernels: 29.9 us -> 26.8 us
    pallas_call x1, Pallas kernels: 11.8 us -> 8.72 us  [body(): pl.pallas_call(lambda *refs: trail_sum(per_panel, *refs), out_shape=pltpu...]
  transfers between devices with their start and end apart: 7 -> 7, of which waited for: 5 -> 6; matrix products, arithmetic and copies ran while one was open for 1% -> 1% of each run, Pallas kernels for 11% -> 9%
where the time goes in v10:
time: 211 us; the launch traced here: 210 us
  blocking collectives  117 us (55%)
  Pallas kernels  26.8 us (13%)
  waiting for transfers between devices  25.8 us (12%)
  starting transfers between devices  23.2 us (11%)
  between operations  14.2 us (7%)
  local copies, waits for them, and re-layouts  2.98 us (1%)
    all_to_all x4, blocking collectives, body(): got = lax.all_to_all(y, GROUP, 0, 0, tiled=True)  42.9 us
    all_to_all x1, blocking collectives, body(): early = lax.all_to_all(sent, GROUP, 0, 0, tiled=True)  23.5 us
    all_to_all x1, blocking collectives, body(): first = lax.all_to_all(first, 'z', 0, 0, tiled=True)  20.7 us
    all_to_all x1, blocking collectives, body(): own = lax.all_to_all(sent, 'yq', 0, 0, tiled=True)  19.8 us
    all_to_all x1, waiting for transfers between devices, body(): got = lax.all_to_all(sent, 'yq', 0, 0, tiled=True)  11.8 us
    all_to_all x1, blocking collectives, body(): solved.append(lax.all_to_all(copied, GROUP, 0, 0, tiled=True))  9.82 us
    all_to_all x2, starting transfers between devices, body(): solved.append(lax.all_to_all(copied, GROUP, 0, 0, tiled=True))  9.48 us
    pallas_call x1, Pallas kernels, body(): pl.pallas_call(lambda *refs: trail_sum(per_panel, *refs), out_shape=pltpu...  8.72 us
  transfers between devices with their start and end apart: 7, of which 6 were waited for; matrix products, arithmetic and copies ran while one was open for 1% of the time, Pallas kernels for 9%

profile of v10, /device:TPU:8, one launch (start us, length us, event | category | flops | bytes accessed | tf_op | source)
XLA Modules:
  0.0 209.7 jit_solution(12775475912515220960)
XLA Ops:
  7.2 2.0 shard_map.50
  9.2 6.2 %all-to-all-start = ((f32[4,224,128]{2,1,0:T(8,128)}), f32[4,224,128]{2,1,0:T(8,128)S(1)}, u32[]{:S(2)}, u32[]{:S(2)}) async-start(f32[4,224,128]{2,1,0:T(8,128)} %shard_map.50), calls=%async_computation | async-start | bytes 917504 | tf_op jit(solution)/shard_map/all_to_all | solution.py:281
  15.4 0.0 all-gather.3.cloned.1.call-start
  15.4 2.0 slice.4
  17.4 11.8 %all-to-all-done.refs_0_ = f32[4,224,128]{2,1,0:T(8,128)S(1)} async-done(((f32[4,224,128]{2,1,0:T(8,128)}), f32[4,224,128]{2,1,0:T(8,128)S(1)}, u32[]{:S(2)}, u32[]{:S(2)}) %all-to-all-start) | async-done | bytes 458784 | tf_op jit(solution)/shard_map/all_to_all | solution.py:281
  29.2 1.1 shard_map.51
  30.3 0.0 all-gather.3.cloned.1.call-update
  30.4 0.0 all-gather.5.cloned.1.call-start
  30.4 0.7 all-gather.5.cloned.1.call-update
  31.1 20.7 %all_to_all.60.mine_ref = f32[8,2,32,128]{3,2,1,0:T(8,128)S(1)} all-to-all(f32[8,2,32,128]{3,2,1,0:T(8,128)S(1)} %get-tuple-element.22), channel_id=1, replica_groups=mesh['x'=4,'yq'=4,'yp'=2,'z'=8,'core'=2] {'z'}, dimensions={0} | all-to-all | bytes 524288 | tf_op jit(solution)/shard_map/all_to_all | solution.py:290
  51.8 1.9 collective-permute-start
  53.7 1.6 collective-permute-done.other_ref
  55.3 0.4 shard_map.52
  55.7 11.7 %all_to_all.61.got_ref = f32[8,64,128]{2,1,0:T(8,128)S(1)} all-to-all(f32[8,64,128]{2,1,0:T(8,128)S(1)} %shard_map.52), channel_id=1, replica_groups=mesh['x'=4,'yq'=4,'yp'=2,'z'=8,'core'=2] {'yp','x'}, dimensions={0} | all-to-all | bytes 524288 | tf_op jit(solution)/shard_map/all_to_all | solution.py:300
  67.5 9.8 %all_to_all.62.refs_0_ = f32[8,64,128]{2,1,0:T(8,128)S(1)} all-to-all(f32[8,64,128]{2,1,0:T(8,128)S(1)} %get-tuple-element.23), channel_id=1, replica_groups=mesh['x'=4,'yq'=4,'yp'=2,'z'=8,'core'=2] {'yp','x'}, dimensions={0} | all-to-all | bytes 524288 | tf_op jit(solution)/shard_map/all_to_all | solution.py:305
  77.3 0.0 copy-start
  77.3 1.5 all-gather.3.cloned.1.call-done
  78.8 1.7 shard_map.54
  80.5 11.7 %all_to_all.63.got_ref = f32[8,64,128]{2,1,0:T(8,128)S(1)} all-to-all(f32[8,64,128]{2,1,0:T(8,128)S(1)} %shard_map.54), channel_id=1, replica_groups=mesh['x'=4,'yq'=4,'yp'=2,'z'=8,'core'=2] {'yp','x'}, dimensions={0} | all-to-all | bytes 524288 | tf_op jit(solution)/shard_map/all_to_all | solution.py:300
  92.2 0.7 shard_map.55
  92.9 4.7 %all-to-all-start.5 = ((f32[8,64,128]{2,1,0:T(8,128)}), f32[8,64,128]{2,1,0:T(8,128)S(1)}, u32[]{:S(2)}, u32[]{:S(2)}) async-start(f32[8,64,128]{2,1,0:T(8,128)} %get-tuple-element.25), calls=%async_computation.5 | async-start | bytes 524288 | tf_op jit(solution)/shard_map/all_to_all | solution.py:305
  97.7 1.6 shard_map.56.refs_1_
  99.3 0.0 copy-done
  99.3 4.2 %all-to-all-done.5.refs_0_.refs_1_ = f32[8,64,128]{2,1,0:T(8,128)S(1)} async-done(((f32[8,64,128]{2,1,0:T(8,128)}), f32[8,64,128]{2,1,0:T(8,128)S(1)}, u32[]{:S(2)}, u32[]{:S(2)}) %all-to-all-start.5) | async-done | bytes 262176 | tf_op jit(solution)/shard_map/all_to_all | solution.py:305
  103.5 0.0 copy-start.1
  103.5 1.9 shard_map.57
  105.4 9.7 %all_to_all.64.got_ref = f32[8,64,128]{2,1,0:T(8,128)S(1)} all-to-all(f32[8,64,128]{2,1,0:T(8,128)S(1)} %shard_map.57), channel_id=1, replica_groups=mesh['x'=4,'yq'=4,'yp'=2,'z'=8,'core'=2] {'yp','x'}, dimensions={0} | all-to-all | bytes 524288 | tf_op jit(solution)/shard_map/all_to_all | solution.py:300
  115.1 0.7 shard_map.58
  115.9 4.7 %all-to-all-start.7 = ((f32[8,64,128]{2,1,0:T(8,128)}), f32[8,64,128]{2,1,0:T(8,128)S(1)}, u32[]{:S(2)}, u32[]{:S(2)}) async-start(f32[8,64,128]{2,1,0:T(8,128)} %get-tuple-element.26), calls=%async_computation.7 | async-start | bytes 524288 | tf_op jit(solution)/shard_map/all_to_all | solution.py:305
  120.6 1.3 shard_map.59.refs_1_
  121.9 0.0 copy-done.1
  121.9 4.5 %all-to-all-done.7.refs_0_.refs_2_ = f32[8,64,128]{2,1,0:T(8,128)S(1)} async-done(((f32[8,64,128]{2,1,0:T(8,128)}), f32[8,64,128]{2,1,0:T(8,128)S(1)}, u32[]{:S(2)}, u32[]{:S(2)}) %all-to-all-start.7) | async-done | bytes 262176 | tf_op jit(solution)/shard_map/all_to_all | solution.py:305
  126.4 0.0 copy-start.3
  126.4 1.8 shard_map.60
  128.3 9.8 %all_to_all.65.got_ref = f32[8,64,128]{2,1,0:T(8,128)S(1)} all-to-all(f32[8,64,128]{2,1,0:T(8,128)S(1)} %shard_map.60), channel_id=1, replica_groups=mesh['x'=4,'yq'=4,'yp'=2,'z'=8,'core'=2] {'yp','x'}, dimensions={0} | all-to-all | bytes 524288 | tf_op jit(solution)/shard_map/all_to_all | solution.py:300
  138.1 19.8 %all_to_all.66.got_ref.refs_0_.refs_5_ = f32[4,4,64,128]{3,2,1,0:T(8,128)S(1)} all-to-all(f32[4,4,64,128]{3,2,1,0:T(8,128)S(1)} %shard_map.61), channel_id=1, replica_groups=mesh['x'=4,'yq'=4,'yp'=2,'z'=8,'core'=2] {'yq'}, dimensions={0} | all-to-all | bytes 1048576 | tf_op jit(solution)/shard_map/all_to_all | solution.py:327
  157.9 0.2 shard_map.62
  158.1 0.0 copy-done.3
  158.1 23.5 %all_to_all.67.refs_3_ = f32[8,3,3,64,128]{4,3,2,1,0:T(8,128)S(1)} all-to-all(f32[8,3,3,64,128]{4,3,2,1,0:T(8,128)S(1)} %shard_map.62), channel_id=1, replica_groups=mesh['x'=4,'yq'=4,'yp'=2,'z'=8,'core'=2] {'yp','x'}, dimensions={0} | all-to-all | bytes 4718592 | tf_op jit(solution)/shard_map/all_to_all | solution.py:329
  181.6 0.1 shard_map.63
  181.7 0.0 copy-start.2
  181.7 1.0 copy-done.2
  182.7 5.6 %all-to-all-start.11 = ((f32[8,4,64,128]{3,2,1,0:T(8,128)}), f32[8,4,64,128]{3,2,1,0:T(8,128)}, u32[]{:S(2)}, u32[]{:S(2)}) async-start(f32[8,4,64,128]{3,2,1,0:T(8,128)} %copy-done.2), calls=%async_computation.11 | async-start | bytes 2097152 | tf_op jit(solution)/shard_map/all_to_all | solution.py:332
  188.3 0.0 all-gather.5.cloned.1.call-done.refs_4_
  188.3 8.7 %shard_map.64.refs_2_ = f32[256,576]{1,0:T(8,128)} custom-call(f32[8,64,128]{2,1,0:T(8,128)} %copy-done, f32[8,64,128]{2,1,0:T(8,128)} %copy-done.1, f32[8,64,128]{2,1,0:T(8,128)} %copy-done.3, f32[8,3,3,64,128]{4,3,2,1,0:T(8,128)S(1)} %all_to_all.67.refs_3_, f32[4,2,512,576]{3,2,1,0:T(8,128)} %all-gather.5.cloned.1.call-done.refs_4_), custom_call_target="tpu_custom_call" | custom-call | tf_op jit(solution)/shard_map/pallas_call | solution.py:335
  197.0 1.4 all-to-all-done.11.refs_0_
  198.4 4.4 %shard_map.65 = (f32[576,256]{1,0:T(8,128)}, f32[128,256]{1,0:T(8,128)}) custom-call(f32[8,4,64,128]{3,2,1,0:T(8,128)} %all-to-all-done.11.refs_0_, f32[4,4,256,576]{3,2,1,0:T(8,128)} %bitcast.19, f32[256,576]{1,0:T(8,128)} %shard_map.64.refs_2_, s32[1]{0:T(128)} %bitcast.7.quad_ref.refs_3_, f32[704,256]{1,0:T(8,128)} %bitcast.21, ...), custom_call_target="tpu_custom_call" | custom-call | tf_op jit(solution)/shard_map/pallas_call | solution.py:353
  (2 shorter events, 0.1 us)
Async XLA Ops:
  9.2 20.0 %all-to-all-start = ((f32[4,224,128]{2,1,0:T(8,128)}), f32[4,224,128]{2,1,0:T(8,128)S(1)}, u32[]{:S(2)}, u32[]{:S(2)}) async-start(f32[4,224,128]{2,1,0:T(8,128)} %shard_map.50), calls=%async_computation | async-start | bytes 917504 | tf_op jit(solution)/shard_map/all_to_all | solution.py:281
  15.4 63.4 %all-gather.3.cloned.1.call-start = ((), (), s32[]{:S(2)}) async-start(), calls=%async_computation.12 | async-start | bytes 5013504 | tf_op jit(solution)/shard_map/all_gather | solution.py:292
  30.4 157.9 %all-gather.5.cloned.1.call-start = ((), (), s32[]{:S(2)}) async-start(), calls=%async_computation.13 | async-start | bytes 11141120 | tf_op jit(solution)/shard_map/all_gather | solution.py:293
  51.8 3.5 %collective-permute-start = (f32[8,2,32,128]{3,2,1,0:T(8,128)S(1)}, f32[8,2,32,128]{3,2,1,0:T(8,128)S(1)}, u32[]{:S(2)}, u32[]{:S(2)}) collective-permute-start(f32[8,2,32,128]{3,2,1,0:T(8,128)S(1)} %all_to_all.60.mine_ref), channel_id=1, source_target_pairs={{0,1},{1,0},{2,3},{3,2},{4,5},{5,4},{6,7},{7,6},{8,9},{9,8},{10,11... | collective-permute-start | bytes 786440 | tf_op jit(solution)/shard_map/ppermute | solution.py:291
  77.3 22.0 %copy-start = (f32[8,64,128]{2,1,0:T(8,128)}, f32[8,64,128]{2,1,0:T(8,128)S(1)}, u32[]{:S(2)}) copy-start(f32[8,64,128]{2,1,0:T(8,128)S(1)} %all_to_all.62.refs_0_) | copy-start | bytes 786436
  92.9 10.6 %all-to-all-start.5 = ((f32[8,64,128]{2,1,0:T(8,128)}), f32[8,64,128]{2,1,0:T(8,128)S(1)}, u32[]{:S(2)}, u32[]{:S(2)}) async-start(f32[8,64,128]{2,1,0:T(8,128)} %get-tuple-element.25), calls=%async_computation.5 | async-start | bytes 524288 | tf_op jit(solution)/shard_map/all_to_all | solution.py:305
  103.5 18.4 %copy-start.1 = (f32[8,64,128]{2,1,0:T(8,128)}, f32[8,64,128]{2,1,0:T(8,128)S(1)}, u32[]{:S(2)}) copy-start(f32[8,64,128]{2,1,0:T(8,128)S(1)} %all-to-all-done.5.refs_0_.refs_1_) | copy-start | bytes 786436
  115.9 10.6 %all-to-all-start.7 = ((f32[8,64,128]{2,1,0:T(8,128)}), f32[8,64,128]{2,1,0:T(8,128)S(1)}, u32[]{:S(2)}, u32[]{:S(2)}) async-start(f32[8,64,128]{2,1,0:T(8,128)} %get-tuple-element.26), calls=%async_computation.7 | async-start | bytes 524288 | tf_op jit(solution)/shard_map/all_to_all | solution.py:305
  126.4 31.6 %copy-start.3 = (f32[8,64,128]{2,1,0:T(8,128)}, f32[8,64,128]{2,1,0:T(8,128)S(1)}, u32[]{:S(2)}) copy-start(f32[8,64,128]{2,1,0:T(8,128)S(1)} %all-to-all-done.7.refs_0_.refs_2_) | copy-start | bytes 786436
  181.7 1.0 copy-start.2
  182.7 15.7 %all-to-all-start.11 = ((f32[8,4,64,128]{3,2,1,0:T(8,128)}), f32[8,4,64,128]{3,2,1,0:T(8,128)}, u32[]{:S(2)}, u32[]{:S(2)}) async-start(f32[8,4,64,128]{3,2,1,0:T(8,128)} %copy-done.2), calls=%async_computation.11 | async-start | bytes 2097152 | tf_op jit(solution)/shard_map/all_to_all | solution.py:332
Sparse Core Ops, SparseCore 0:
  30.5 48.2 all-gather.2
  80.9 67.4 all-gather.4

commit v11 on v10

--- a/solution.py
+++ b/solution.py
@@ -183,12 +183,21 @@
 
 
 def trail_sum(steps, *refs):
-    own_refs, (x_ref, f_ref, out_hbm, acc_ref, sem) = refs[:-5], refs[-5:]
+    own_refs, (x_ref, f_ref, quad_ref, r_ref, out_hbm, acc_ref, turned_ref, sem) = (
+        refs[:-8],
+        refs[-8:],
+    )
     step = pl.program_id(0)
 
     @pl.when(step == 0)
     def _():
-        acc_ref[...] = jnp.zeros_like(acc_ref)
+        turned_ref[...] = r_ref[r_ref.shape[0] - turned_ref.shape[1] :].T
+        quads, per = x_ref.shape[2] + 1, x_ref.shape[3]
+        for t in range(quads):
+            q = lax.rem(quad_ref[0] + t, quads)
+            acc_ref[t * per : (t + 1) * per] = turned_ref[
+                pl.ds(pl.multiple_of(q * per, per), per)
+            ]
 
     for k, own_ref in enumerate(own_refs):
 
@@ -198,7 +207,7 @@
             for s in range(x_ref.shape[0]):
                 turns = [x_ref[s, 0, t] for t in range(x_ref.shape[2])]
                 parts.append(jnp.concatenate([own_ref[x_ref.shape[0] * (step % steps) + s], *turns], axis=0))
-            acc_ref[...] += dot(jnp.concatenate(parts, axis=1), f_ref[0, 0], NN)
+            acc_ref[...] -= dot(jnp.concatenate(parts, axis=1), f_ref[0, 0], NN)
 
     @pl.when(step == pl.num_programs(0) - 1)
     def _():
@@ -207,8 +216,8 @@
         copy.wait()
 
 
-def finish(panel, x_hbm, f_hbm, sum_hbm, quad_ref, r_hbm, own_ref, *refs):
-    out_ref, mine_ref, turned_ref, f_ref, x_ref, sum_ref, r_ref, sems = refs
+def finish(panel, x_hbm, f_hbm, sum_hbm, quad_ref, own_ref, *refs):
+    out_ref, mine_ref, turned_ref, f_ref, x_ref, sum_ref, sems = refs
     n = f_ref.shape[0]
     quads, panels, per, _ = own_ref.shape
     width = mine_ref.shape[0] // panels
@@ -220,10 +229,7 @@
             pltpu.make_async_copy(f_hbm.at[panel, b], f_ref.at[b], sems.at[2 * b + 1]),
         ]
     sums = pltpu.make_async_copy(sum_hbm, sum_ref, sems.at[2 * n])
-    rows = pltpu.make_async_copy(
-        r_hbm.at[pl.ds(mine_ref.shape[0], r_ref.shape[0])], r_ref, sems.at[2 * n + 1]
-    )
-    for c in (*copies, sums, rows):
+    for c in (*copies, sums):
         c.start()
     quad = quad_ref[0]
     at = pl.multiple_of(quad * width, width)
@@ -238,15 +244,14 @@
         product = dot(jnp.concatenate(x, axis=1), f_ref[b], NN)
         total = product if b == 0 else total + product
     sums.wait()
-    total += jnp.concatenate(
+    left = jnp.concatenate(
         [
             sum_ref[pl.ds(pl.multiple_of(lax.rem(q + quads - quad, quads) * per, per), per)]
             for q in range(quads)
         ],
         axis=0,
     )
-    rows.wait()
-    out_ref[...] = r_ref[...] - total.T
+    out_ref[...] = (left - total).T
 
 
 def body(factor, inverses, right_side):
@@ -344,25 +349,26 @@
             pl.BlockSpec(
                 (1, 1, nx * rows, length), lambda i: (i // per_panel, i % per_panel, 0, 0)
             ),
+            SMEM,
+            whole(current.shape),
         ],
         out_specs=HBM,
-        scratch_shapes=[pltpu.VMEM((count, length), F32), pltpu.SemaphoreType.DMA],
+        scratch_shapes=[pltpu.VMEM((count, length), F32)] * 2 + [pltpu.SemaphoreType.DMA],
         compiler_params=pltpu.CompilerParams(vmem_limit_bytes=24 << 20),
-    )(*[in_hbm(x) for x in solved], early, in_hbm(trail))
+    )(*[in_hbm(x) for x in solved], early, in_hbm(trail), index, in_hbm(current))
     flat = trail.reshape(panels, -1, 2 * rows, length)
     out, mine = call(
         lambda *refs: finish(panels - 1, *refs),
         [(length, count), (tail, count)],
-        [HBM, HBM, HBM, SMEM, HBM, VMEM],
+        [HBM, HBM, HBM, SMEM, VMEM],
         [
             pltpu.VMEM((rows, count), F32),
             pltpu.VMEM(flat.shape[1:], F32),
             pltpu.VMEM(late.shape, F32),
             pltpu.VMEM(total.shape, F32),
-            pltpu.VMEM((length, count), F32),
-            pltpu.SemaphoreType.DMA((2 * flat.shape[1] + 2,)),
+            pltpu.SemaphoreType.DMA((2 * flat.shape[1] + 1,)),
         ],
-    )(in_hbm(late), in_hbm(flat), in_hbm(total), index, in_hbm(current), own)
+    )(in_hbm(late), in_hbm(flat), in_hbm(total), index, own)
     return (mine[None], out[None])
 
 

time: 211 us -> 211 us (level)
  no operation moved by 1% of the time
where the time goes in v11:
time: 211 us; the launch traced here: 210 us
  blocking collectives  117 us (55%)
  Pallas kernels  27.3 us (13%)
  waiting for transfers between devices  25.2 us (12%)
  starting transfers between devices  23.2 us (11%)
  between operations  14.2 us (7%)
  local copies, waits for them, and re-layouts  2.98 us (1%)
    all_to_all x4, blocking collectives, body(): got = lax.all_to_all(y, GROUP, 0, 0, tiled=True)  42.9 us
    all_to_all x1, blocking collectives, body(): early = lax.all_to_all(sent, GROUP, 0, 0, tiled=True)  23.5 us
    all_to_all x1, blocking collectives, body(): first = lax.all_to_all(first, 'z', 0, 0, tiled=True)  20.7 us
    all_to_all x1, blocking collectives, body(): own = lax.all_to_all(sent, 'yq', 0, 0, tiled=True)  19.8 us
    all_to_all x1, waiting for transfers between devices, body(): got = lax.all_to_all(sent, 'yq', 0, 0, tiled=True)  11.8 us
    all_to_all x1, blocking collectives, body(): solved.append(lax.all_to_all(copied, GROUP, 0, 0, tiled=True))  9.82 us
    all_to_all x2, starting transfers between devices, body(): solved.append(lax.all_to_all(copied, GROUP, 0, 0, tiled=True))  9.48 us
    pallas_call x1, Pallas kernels, body(): pl.pallas_call(lambda *refs: trail_sum(per_panel, *refs), out_shape=pltpu...  9.25 us
  transfers between devices with their start and end apart: 7, of which 6 were waited for; matrix products, arithmetic and copies ran while one was open for 1% of the time, Pallas kernels for 9%

profile of v11, /device:TPU:8, one launch (start us, length us, event | category | flops | bytes accessed | tf_op | source)
XLA Modules:
  0.0 209.7 jit_solution(14620019709822161451)
XLA Ops:
  7.2 2.0 shard_map.50
  9.2 6.2 %all-to-all-start = ((f32[4,224,128]{2,1,0:T(8,128)}), f32[4,224,128]{2,1,0:T(8,128)S(1)}, u32[]{:S(2)}, u32[]{:S(2)}) async-start(f32[4,224,128]{2,1,0:T(8,128)} %shard_map.50), calls=%async_computation | async-start | bytes 917504 | tf_op jit(solution)/shard_map/all_to_all | solution.py:286
  15.4 0.0 all-gather.3.cloned.1.call-start
  15.4 2.0 slice.4
  17.4 11.8 %all-to-all-done.refs_0_ = f32[4,224,128]{2,1,0:T(8,128)S(1)} async-done(((f32[4,224,128]{2,1,0:T(8,128)}), f32[4,224,128]{2,1,0:T(8,128)S(1)}, u32[]{:S(2)}, u32[]{:S(2)}) %all-to-all-start) | async-done | bytes 458784 | tf_op jit(solution)/shard_map/all_to_all | solution.py:286
  29.2 1.1 shard_map.51
  30.3 0.0 all-gather.3.cloned.1.call-update
  30.4 0.0 all-gather.5.cloned.1.call-start
  30.4 0.7 all-gather.5.cloned.1.call-update
  31.1 20.7 %all_to_all.60.mine_ref = f32[8,2,32,128]{3,2,1,0:T(8,128)S(1)} all-to-all(f32[8,2,32,128]{3,2,1,0:T(8,128)S(1)} %get-tuple-element.22), channel_id=1, replica_groups=mesh['x'=4,'yq'=4,'yp'=2,'z'=8,'core'=2] {'z'}, dimensions={0} | all-to-all | bytes 524288 | tf_op jit(solution)/shard_map/all_to_all | solution.py:295
  51.8 1.9 collective-permute-start
  53.7 1.6 collective-permute-done.other_ref
  55.3 0.4 shard_map.52
  55.7 11.7 %all_to_all.61.got_ref = f32[8,64,128]{2,1,0:T(8,128)S(1)} all-to-all(f32[8,64,128]{2,1,0:T(8,128)S(1)} %shard_map.52), channel_id=1, replica_groups=mesh['x'=4,'yq'=4,'yp'=2,'z'=8,'core'=2] {'yp','x'}, dimensions={0} | all-to-all | bytes 524288 | tf_op jit(solution)/shard_map/all_to_all | solution.py:305
  67.5 9.8 %all_to_all.62.refs_0_ = f32[8,64,128]{2,1,0:T(8,128)S(1)} all-to-all(f32[8,64,128]{2,1,0:T(8,128)S(1)} %get-tuple-element.23), channel_id=1, replica_groups=mesh['x'=4,'yq'=4,'yp'=2,'z'=8,'core'=2] {'yp','x'}, dimensions={0} | all-to-all | bytes 524288 | tf_op jit(solution)/shard_map/all_to_all | solution.py:310
  77.3 0.0 copy-start
  77.3 1.5 all-gather.3.cloned.1.call-done
  78.8 1.7 shard_map.54
  80.5 11.7 %all_to_all.63.got_ref = f32[8,64,128]{2,1,0:T(8,128)S(1)} all-to-all(f32[8,64,128]{2,1,0:T(8,128)S(1)} %shard_map.54), channel_id=1, replica_groups=mesh['x'=4,'yq'=4,'yp'=2,'z'=8,'core'=2] {'yp','x'}, dimensions={0} | all-to-all | bytes 524288 | tf_op jit(solution)/shard_map/all_to_all | solution.py:305
  92.2 0.7 shard_map.55
  92.9 4.7 %all-to-all-start.5 = ((f32[8,64,128]{2,1,0:T(8,128)}), f32[8,64,128]{2,1,0:T(8,128)S(1)}, u32[]{:S(2)}, u32[]{:S(2)}) async-start(f32[8,64,128]{2,1,0:T(8,128)} %get-tuple-element.25), calls=%async_computation.5 | async-start | bytes 524288 | tf_op jit(solution)/shard_map/all_to_all | solution.py:310
  97.7 1.6 shard_map.56.refs_1_
  99.3 0.0 copy-done
  99.3 4.2 %all-to-all-done.5.refs_0_.refs_1_ = f32[8,64,128]{2,1,0:T(8,128)S(1)} async-done(((f32[8,64,128]{2,1,0:T(8,128)}), f32[8,64,128]{2,1,0:T(8,128)S(1)}, u32[]{:S(2)}, u32[]{:S(2)}) %all-to-all-start.5) | async-done | bytes 262176 | tf_op jit(solution)/shard_map/all_to_all | solution.py:310
  103.5 0.0 copy-start.1
  103.5 1.9 shard_map.57
  105.4 9.7 %all_to_all.64.got_ref = f32[8,64,128]{2,1,0:T(8,128)S(1)} all-to-all(f32[8,64,128]{2,1,0:T(8,128)S(1)} %shard_map.57), channel_id=1, replica_groups=mesh['x'=4,'yq'=4,'yp'=2,'z'=8,'core'=2] {'yp','x'}, dimensions={0} | all-to-all | bytes 524288 | tf_op jit(solution)/shard_map/all_to_all | solution.py:305
  115.1 0.7 shard_map.58
  115.9 4.7 %all-to-all-start.7 = ((f32[8,64,128]{2,1,0:T(8,128)}), f32[8,64,128]{2,1,0:T(8,128)S(1)}, u32[]{:S(2)}, u32[]{:S(2)}) async-start(f32[8,64,128]{2,1,0:T(8,128)} %get-tuple-element.26), calls=%async_computation.7 | async-start | bytes 524288 | tf_op jit(solution)/shard_map/all_to_all | solution.py:310
  120.6 1.3 shard_map.59.refs_1_
  121.9 0.0 copy-done.1
  121.9 4.5 %all-to-all-done.7.refs_0_.refs_2_ = f32[8,64,128]{2,1,0:T(8,128)S(1)} async-done(((f32[8,64,128]{2,1,0:T(8,128)}), f32[8,64,128]{2,1,0:T(8,128)S(1)}, u32[]{:S(2)}, u32[]{:S(2)}) %all-to-all-start.7) | async-done | bytes 262176 | tf_op jit(solution)/shard_map/all_to_all | solution.py:310
  126.4 0.0 copy-start.3
  126.4 1.8 shard_map.60
  128.3 9.8 %all_to_all.65.got_ref = f32[8,64,128]{2,1,0:T(8,128)S(1)} all-to-all(f32[8,64,128]{2,1,0:T(8,128)S(1)} %shard_map.60), channel_id=1, replica_groups=mesh['x'=4,'yq'=4,'yp'=2,'z'=8,'core'=2] {'yp','x'}, dimensions={0} | all-to-all | bytes 524288 | tf_op jit(solution)/shard_map/all_to_all | solution.py:305
  138.1 19.8 %all_to_all.66.got_ref.refs_0_.refs_4_ = f32[4,4,64,128]{3,2,1,0:T(8,128)S(1)} all-to-all(f32[4,4,64,128]{3,2,1,0:T(8,128)S(1)} %shard_map.61), channel_id=1, replica_groups=mesh['x'=4,'yq'=4,'yp'=2,'z'=8,'core'=2] {'yq'}, dimensions={0} | all-to-all | bytes 1048576 | tf_op jit(solution)/shard_map/all_to_all | solution.py:332
  157.9 0.2 shard_map.62
  158.1 0.0 copy-done.3
  158.1 23.5 %all_to_all.67.refs_3_ = f32[8,3,3,64,128]{4,3,2,1,0:T(8,128)S(1)} all-to-all(f32[8,3,3,64,128]{4,3,2,1,0:T(8,128)S(1)} %shard_map.62), channel_id=1, replica_groups=mesh['x'=4,'yq'=4,'yp'=2,'z'=8,'core'=2] {'yp','x'}, dimensions={0} | all-to-all | bytes 4718592 | tf_op jit(solution)/shard_map/all_to_all | solution.py:334
  181.6 0.1 shard_map.63
  181.7 0.0 copy-start.2
  181.7 1.0 copy-done.2
  182.7 5.6 %all-to-all-start.11 = ((f32[8,4,64,128]{3,2,1,0:T(8,128)}), f32[8,4,64,128]{3,2,1,0:T(8,128)}, u32[]{:S(2)}, u32[]{:S(2)}) async-start(f32[8,4,64,128]{3,2,1,0:T(8,128)} %copy-done.2), calls=%async_computation.11 | async-start | bytes 2097152 | tf_op jit(solution)/shard_map/all_to_all | solution.py:337
  188.3 0.0 all-gather.5.cloned.1.call-done.refs_4_
  188.3 9.2 %shard_map.64.refs_2_ = f32[256,576]{1,0:T(8,128)} custom-call(f32[8,64,128]{2,1,0:T(8,128)} %copy-done, f32[8,64,128]{2,1,0:T(8,128)} %copy-done.1, f32[8,64,128]{2,1,0:T(8,128)} %copy-done.3, f32[8,3,3,64,128]{4,3,2,1,0:T(8,128)S(1)} %all_to_all.67.refs_3_, f32[4,2,512,576]{3,2,1,0:T(8,128)} %all-gather.5.cloned.1.call-done.refs_4_, ...), custom_call_target="tpu_custom_call" | custom-call | tf_op jit(solution)/shard_map/pallas_call | solution.py:340
  197.5 0.9 all-to-all-done.11.refs_0_
  198.4 4.4 %shard_map.65 = (f32[576,256]{1,0:T(8,128)}, f32[128,256]{1,0:T(8,128)}) custom-call(f32[8,4,64,128]{3,2,1,0:T(8,128)} %all-to-all-done.11.refs_0_, f32[4,4,256,576]{3,2,1,0:T(8,128)} %bitcast.19, f32[256,576]{1,0:T(8,128)} %shard_map.64.refs_2_, s32[1]{0:T(128)} %bitcast.7.quad_ref.refs_5_.refs_3_, f32[4,4,64,128]{3,2,1,0:T(8,128)S(1)} %all_to_all.66.got_ref.refs_0_.refs_4_), custom_call_target="tpu_custom_call" | custom-call | tf_op jit(solution)/shard_map/pallas_call | solution.py:360
  (2 shorter events, 0.1 us)
Async XLA Ops:
  9.2 20.0 %all-to-all-start = ((f32[4,224,128]{2,1,0:T(8,128)}), f32[4,224,128]{2,1,0:T(8,128)S(1)}, u32[]{:S(2)}, u32[]{:S(2)}) async-start(f32[4,224,128]{2,1,0:T(8,128)} %shard_map.50), calls=%async_computation | async-start | bytes 917504 | tf_op jit(solution)/shard_map/all_to_all | solution.py:286
  15.4 63.4 %all-gather.3.cloned.1.call-start = ((), (), s32[]{:S(2)}) async-start(), calls=%async_computation.12 | async-start | bytes 5013504 | tf_op jit(solution)/shard_map/all_gather | solution.py:297
  30.4 157.9 %all-gather.5.cloned.1.call-start = ((), (), s32[]{:S(2)}) async-start(), calls=%async_computation.13 | async-start | bytes 11141120 | tf_op jit(solution)/shard_map/all_gather | solution.py:298
  51.8 3.5 %collective-permute-start = (f32[8,2,32,128]{3,2,1,0:T(8,128)S(1)}, f32[8,2,32,128]{3,2,1,0:T(8,128)S(1)}, u32[]{:S(2)}, u32[]{:S(2)}) collective-permute-start(f32[8,2,32,128]{3,2,1,0:T(8,128)S(1)} %all_to_all.60.mine_ref), channel_id=1, source_target_pairs={{0,1},{1,0},{2,3},{3,2},{4,5},{5,4},{6,7},{7,6},{8,9},{9,8},{10,11... | collective-permute-start | bytes 786440 | tf_op jit(solution)/shard_map/ppermute | solution.py:296
  77.3 22.0 %copy-start = (f32[8,64,128]{2,1,0:T(8,128)}, f32[8,64,128]{2,1,0:T(8,128)S(1)}, u32[]{:S(2)}) copy-start(f32[8,64,128]{2,1,0:T(8,128)S(1)} %all_to_all.62.refs_0_) | copy-start | bytes 786436
  92.9 10.6 %all-to-all-start.5 = ((f32[8,64,128]{2,1,0:T(8,128)}), f32[8,64,128]{2,1,0:T(8,128)S(1)}, u32[]{:S(2)}, u32[]{:S(2)}) async-start(f32[8,64,128]{2,1,0:T(8,128)} %get-tuple-element.25), calls=%async_computation.5 | async-start | bytes 524288 | tf_op jit(solution)/shard_map/all_to_all | solution.py:310
  103.5 18.4 %copy-start.1 = (f32[8,64,128]{2,1,0:T(8,128)}, f32[8,64,128]{2,1,0:T(8,128)S(1)}, u32[]{:S(2)}) copy-start(f32[8,64,128]{2,1,0:T(8,128)S(1)} %all-to-all-done.5.refs_0_.refs_1_) | copy-start | bytes 786436
  115.9 10.6 %all-to-all-start.7 = ((f32[8,64,128]{2,1,0:T(8,128)}), f32[8,64,128]{2,1,0:T(8,128)S(1)}, u32[]{:S(2)}, u32[]{:S(2)}) async-start(f32[8,64,128]{2,1,0:T(8,128)} %get-tuple-element.26), calls=%async_computation.7 | async-start | bytes 524288 | tf_op jit(solution)/shard_map/all_to_all | solution.py:310
  126.4 31.6 %copy-start.3 = (f32[8,64,128]{2,1,0:T(8,128)}, f32[8,64,128]{2,1,0:T(8,128)S(1)}, u32[]{:S(2)}) copy-start(f32[8,64,128]{2,1,0:T(8,128)S(1)} %all-to-all-done.7.refs_0_.refs_2_) | copy-start | bytes 786436
  181.7 1.0 copy-start.2
  182.7 15.7 %all-to-all-start.11 = ((f32[8,4,64,128]{3,2,1,0:T(8,128)}), f32[8,4,64,128]{3,2,1,0:T(8,128)}, u32[]{:S(2)}, u32[]{:S(2)}) async-start(f32[8,4,64,128]{3,2,1,0:T(8,128)} %copy-done.2), calls=%async_computation.11 | async-start | bytes 2097152 | tf_op jit(solution)/shard_map/all_to_all | solution.py:337
Sparse Core Ops, SparseCore 0:
  30.5 48.2 all-gather.2
  80.9 67.4 all-gather.4
